TPU v7x, 32 devices: a whole 2x2x4 slice. The times are simulated.
32 devices in a mesh: space: 16 (over z, y, core), chan: 2 (over x).
Axes of the slice: x: 2, y: 2, z: 4, core: 2. Of those that a mesh axis runs over, the one named last changes fastest.
Arguments:
- volume: float32 [32, 32, 128, 128], P('chan', 'space'), may hold values from -6 to 6
- filters: float32 [64, 32, 3, 3, 3], P(None, 'chan'), may hold values from -0.21875 to 0.21875
- cotangent: float32 [64, 16, 64, 64], P('chan', 'space'), may hold values from -6 to 6
Outputs:
- activated: float32 [64, 16, 64, 64], P('chan', 'space')
- volume_grad: float32 [32, 32, 128, 128], P('chan', 'space')
- filter_grad: float32 [64, 32, 3, 3, 3], P(None, 'chan')
All inputs are finite; a program needn't handle non-finite values.
Results may differ from a plain program's by a relative error of at most 0.00014.
Values sent between devices are 32-bit elements; how exact they have to be, the bound alone decides.
No kernel may reach another device: no remote copies, remote signals or barrier semaphores. Data moves between devices by JAX's collectives and lax.ppermute only.
A program may use at most 192 MiB of HBM per device.

v0:
```python
import jax
import jax.numpy as jnp
from jax import lax
from jax.sharding import PartitionSpec as P


def from_behind(value, axis, steps):
    count = lax.axis_size(axis)
    initial, last = (max(0, -steps), min(count, count - steps))
    return lax.ppermute(value, axis, [(source, source + steps) for source in range(initial, last)])


def conv_local(extended, filters):
    result = lax.conv_general_dilated(
        extended[None],
        filters,
        (2, 2, 2),
        ((0, 0), (1, 1), (1, 1)),
        dimension_numbers=("NCDHW", "OIDHW", "NCDHW"),
        precision=lax.Precision.HIGHEST,
    )
    return result[0]


def on_device(volume, filters, cotangent):
    out_rows = cotangent.shape[0]
    top_plane = volume[:, -1]
    below = from_behind(top_plane, "space", 1)
    extended = jnp.concatenate([below[:, None], volume], axis=1)
    every_filter = lax.all_gather(filters, "chan", axis=1, tiled=True)
    own_filters = lax.dynamic_slice_in_dim(
        every_filter, lax.axis_index("chan") * out_rows, out_rows, 0
    )
    initial = jnp.zeros(cotangent.shape, jnp.float32)
    chosen = own_filters
    preact = initial + conv_local(lax.all_gather(extended, "chan", axis=0, tiled=True), chosen)
    activated = jax.nn.softplus(preact)
    preact_grad = cotangent * jax.nn.sigmoid(preact)
    piece = lax.all_gather(preact_grad, "chan", axis=0, tiled=True)
    start = jnp.int32(0)
    grad_filters = jnp.zeros(filters.shape, jnp.float32)
    chosen = lax.dynamic_slice_in_dim(filters, start, piece.shape[0], 0)
    unused, pullback = jax.vjp(conv_local, extended, chosen)
    grad_piece, grad_rows = pullback(piece)
    grad_extended, grad_filters = (
        grad_piece,
        lax.dynamic_update_slice_in_dim(grad_filters, grad_rows, start, 0),
    )
    spilled = from_behind(grad_extended[:, 0], "space", -1)
    volume_grad = grad_extended[:, 1:]
    volume_grad = volume_grad.at[:, -1].add(spilled)
    summed = lax.psum(grad_filters, "space")
    depth_all = volume.shape[1] * lax.axis_size("space")
    factor = float(depth_all // 2 * (volume.shape[2] // 2) * (volume.shape[3] // 2)) ** (-0.5)
    return (activated, volume_grad, summed * factor)


def solution(mesh):
    in_specs = (
        P("chan", "space", None, None),
        P(None, "chan", None, None, None),
        P("chan", "space", None, None),
    )
    out_specs = (
        P("chan", "space", None, None),
        P("chan", "space", None, None),
        P(None, "chan", None, None, None),
    )
    return jax.shard_map(
        on_device, mesh=mesh, in_specs=in_specs, out_specs=out_specs, check_vma=False
    )
```

profile of v0, /device:TPU:0, one launch (start us, length us, event | category | flops | bytes accessed | tf_op | source)
XLA Modules:
  0.0 647.1 jit_solution(8381787127257969497)
XLA Ops:
  7.2 2.4 slice_bitcast_fusion.3
  9.7 2.4 collective-permute-start
  12.1 8.6 %copy.48 = f32[16,2,128,128]{0,3,2,1:T(8,128)} copy(f32[16,2,128,128]{3,2,1,0:T(8,128)S(1)} %copy-done) | data formatting | bytes 4194304 | tf_op args[0]
  20.6 4.6 copy.47
  25.3 18.6 %pad_maximum_fusion = f32[16,3,128,128]{0,3,2,1:T(8,128)} fusion(f32[16,2,128,128]{0,3,2,1:T(8,128)} %copy.48, f32[16,1,128,128]{0,3,2,1:T(8,128)} %bitcast.46), kind=kLoop, calls=%fused_computation.6 | loop fusion | flops 786432 | bytes 6291456 | tf_op jit(solution)/shard_map/concatenate | solution.py:29
  43.9 16.0 %copy.49 = f32[16,3,128,128]{3,2,1,0:T(8,128)} copy(f32[16,3,128,128]{0,3,2,1:T(8,128)} %pad_maximum_fusion) | data formatting | bytes 6291456 | tf_op jit(solution)/shard_map/concatenate | solution.py:29
  62.0 7.1 %all_gather.10 = f32[64,32,3,3,3]{0,1,4,3,2:T(8,128)S(1)} all-gather(f32[64,16,3,3,3]{0,1,4,3,2:T(8,128)S(1)} %copy-done.2), channel_id=1, replica_groups=mesh['space'=16,'chan'=2] {'chan'}, dimensions={1}, use_global_device_ids=true | all-gather | bytes 331776 | tf_op jit(solution)/shard_map/all_gather | solution.py:30
  69.1 79.3 %all-gather.3.cloned.1.call-done = f32[32,3,128,128]{3,2,1,0:T(8,128)} async-done(((f32[16,3,128,128]{3,2,1,0:T(8,128)}), f32[32,3,128,128]{3,2,1,0:T(8,128)}) %all-gather.3.cloned.1.call-update) | async-done | bytes 6291472 | tf_op jit(solution)/shard_map/all_gather | solution.py:36
  148.4 6.7 %copy.50 = f32[32,3,128,128]{2,0,3,1:T(8,128)} copy(f32[32,3,128,128]{3,2,1,0:T(8,128)} %all-gather.3.cloned.1.call-done) | data formatting | bytes 12582912 | tf_op jit(solution)/shard_map/all_gather | solution.py:36
  155.1 6.7 %pad.2 = f32[32,3,128,1,144]{2,0,4,1,3:T(8,128)} pad(f32[32,3,128,1,128]{2,0,4,1,3:T(8,128)} %bitcast.48, f32[]{:T(128)} %constant.42.clone.1), padding=0_0x0_0x0_0x0_0x1_15 | pad | bytes 13369348 | tf_op jit(solution)/shard_map/broadcast_in_dim | solution.py:15
  161.8 24.8 %copy.52 = f32[32,3,128,1,8,18]{0,4,5,2,1,3:T(8,128)} copy(f32[32,3,128,1,8,18]{2,0,5,4,1,3:T(8,128)} %bitcast.47) | data formatting | bytes 14155776 | tf_op jit(solution)/shard_map/conv_general_dilated | solution.py:14
  186.6 2.2 slice.45
  188.8 37.1 %fusion.11 = f32[1,64,8,9,32]{4,2,3,1,0:T(8,128)} fusion(f32[32,3,128,1,7,2]{0,4,5,2,1,3:T(8,128)S(1)} %slice.45, f32[32,3,128,1,8,18]{0,4,5,2,1,3:T(8,128)} %copy.52, pred[8,9]{0,1:T(8,128)(4,1)S(1)} %copy-done.4, f32[64,32,3,3,3]{0,1,4,3,2:T(8,128)S(1)} %all_gather.10, s32[]{:T(128)S(6)} %select_n.15), kind=kOutput, calls=%fused_computation.17 | convolution fusion | flops 1526906880 | bytes 8577100 | tf_op jit(solution)/shard_map/conv_general_dilated | solution.py:14
  225.9 2.2 copy.54
  228.2 1.7 divide_multiply_fusion
  229.9 1.6 copy.56
  231.6 33.2 %all-gather.5.cloned.1.call-done = f32[64,1,64,64]{3,2,1,0:T(8,128)} async-done(((f32[32,1,64,64]{3,2,1,0:T(8,128)}), f32[64,1,64,64]{3,2,1,0:T(8,128)}) %all-gather.5.cloned.1.call-update) | async-done | bytes 1048592 | tf_op jit(solution)/shard_map/all_gather | solution.py:39
  264.8 3.1 copy.57
  267.9 1.7 pad.4
  269.6 2.3 copy.59
  272.6 86.6 %broadcast_select_fusion = f32[3,128,8,18,16]{4,2,3,1,0:T(8,128)} fusion(pred[8,18]{0,1:T(8,128)(4,1)S(1)} %copy-done.3, f32[64,16,3,3,3]{0,1,4,3,2:T(8,128)S(1)} %copy-done.2, f32[64,1,64,8,10]{0,3,4,2,1:T(8,128)S(1)} %fusion.32), kind=kOutput, calls=%fused_computation.9 | convolution fusion | flops 1521745920 | bytes 4960400 | tf_op jit(solution)/shard_map/transpose(jvp())/conv_general_dilated | solution.py:14
  359.2 17.2 %copy.60 = f32[3,128,8,18,16]{1,4,3,2,0:T(8,128)} copy(f32[3,128,8,18,16]{4,2,3,1,0:T(8,128)} %broadcast_select_fusion) | data formatting | bytes 7077888 | tf_op jit(solution)/shard_map/transpose(jvp())/conv_general_dilated | solution.py:14
  376.4 2.1 slice_bitcast_fusion
  379.6 1.3 collective-permute-start.1
  380.9 3.3 copy.61
  384.2 159.1 %fusion.25 = f32[64,16,3,3,3]{0,1,4,3,2:T(8,128)} fusion(f32[1,16,3,128,128]{1,0,4,3,2:T(1,128)} %bitcast.45, f32[1,64,1,64,64]{1,0,4,3,2:T(1,128)} %bitcast.53), kind=kOutput, calls=%fused_computation.35 | convolution fusion | flops 1344835584 | bytes 4304896 | tf_op jit(solution)/shard_map/transpose(jvp())/conv_general_dilated | solution.py:14
  543.3 2.7 copy.62
  546.0 1.5 slice.49
  547.5 85.9 %all-reduce.2.cloned.1.call-done = f32[64,16,3,3,3]{0,1,4,3,2:T(8,128)} async-done(((f32[64,16,3,3,3]{0,1,4,3,2:T(8,128)}), f32[64,16,3,3,3]{0,1,4,3,2:T(8,128)}) %all-reduce.2.cloned.1.call-update) | async-done | bytes 110608 | tf_op jit(solution)/shard_map/psum | solution.py:52
  633.5 1.6 broadcast_multiply_fusion
  635.1 2.4 fusion.16
  637.5 2.9 copy.63
  (22 shorter events, 4.0 us)
Async XLA Ops:
  7.2 4.9 copy-start
  7.2 141.2 %all-gather.3.cloned.1.call-start = ((), (), s32[]{:S(2)}) async-start(), calls=%async_computation | async-start | bytes 9437184 | tf_op jit(solution)/shard_map/all_gather | solution.py:36
  9.7 11.0 %collective-permute-start = (f32[16,128,128]{2,1,0:T(8,128)}, f32[16,128,128]{2,1,0:T(8,128)S(1)}, u32[]{:S(2)}, u32[]{:S(2)}) collective-permute-start(f32[16,128,128]{2,1,0:T(8,128)} %slice_bitcast_fusion.3), channel_id=1, source_target_pairs={{0,2},{2,4},{4,6},{6,8},{8,10},{10,12},{12,14},{14,16},{16,18},{18... | collective-permute-start | bytes 3145736 | tf_op jit(solution)/shard_map/ppermute | solution.py:10
  59.8 1.2 copy-start.1
  59.8 2.2 copy-start.2
  59.9 204.9 %all-gather.5.cloned.1.call-start = ((), (), s32[]{:S(2)}) async-start(), calls=%async_computation.1 | async-start | bytes 3145728 | tf_op jit(solution)/shard_map/all_gather | solution.py:39
  186.6 2.2 copy-start.4
  231.5 401.9 %all-reduce.2.cloned.1.call-start = ((), (), s32[]{:S(2)}) async-start(), calls=%async_computation.2 | async-start | bytes 442368 | tf_op jit(solution)/shard_map/psum | solution.py:52
  271.9 0.7 copy-start.3
  379.6 255.5 %collective-permute-start.1 = (f32[16,128,128]{1,0,2:T(8,128)}, f32[16,128,128]{1,0,2:T(8,128)}, u32[]{:S(2)}, u32[]{:S(2)}) collective-permute-start(f32[16,128,128]{1,0,2:T(8,128)} %slice_bitcast_fusion.1), channel_id=1, source_target_pairs={{2,0},{4,2},{6,4},{8,6},{10,8},{12,10},{14,12},{16,14},{18,16},{20... | collective-permute-start | bytes 3145736 | tf_op jit(solution)/shard_map/ppermute | solution.py:10
Sparse Core Ops, SparseCore 0:
  60.0 88.3 all-gather.2
  231.6 33.1 all-gather.4
  543.4 89.9 all-reduce.1
where the time goes:
time: 651 us; the launch traced here: 647 us
  matrix products  283 us (43%)
  waiting for transfers between devices  199 us (31%)
  local copies, waits for them, and re-layouts  116 us (18%)
  other arithmetic  24.5 us (4%)
  between operations  14.1 us (2%)
  blocking collectives  7.07 us (1%)
    conv_general_dilated x3, matrix products, conv_local(): lax.conv_general_dilated(extended[None], filters, (2, 2, 2), ((0, 0), (1,...  283 us
    psum x1, waiting for transfers between devices, on_device(): summed = lax.psum(grad_filters, 'space')  85.9 us
    all_gather x1, waiting for transfers between devices, on_device(): lax.all_gather(extended, 'chan', axis=0, tiled=True)  79.3 us
    conv_general_dilated x6, local copies, waits for them, and re-layouts, conv_local(): lax.conv_general_dilated(extended[None], filters, (2, 2, 2), ((0, 0), (1,...  48.8 us
    all_gather x1, waiting for transfers between devices, on_device(): piece = lax.all_gather(preact_grad, 'chan', axis=0, tiled=True)  33.2 us
    concatenate x1, other arithmetic, on_device(): extended = jnp.concatenate([below[:, None], volume], axis=1)  18.6 us
    unnamed x14, local copies, waits for them, and re-layouts  16.7 us
    concatenate x1, local copies, waits for them, and re-layouts, on_device(): extended = jnp.concatenate([below[:, None], volume], axis=1)  16 us
  transfers between devices with their start and end apart: 5, of which 3 were waited for; matrix products, arithmetic and copies ran while one was open for 27% of the time, Pallas kernels for 0%

commit v1 on v0

v1 whole, which is shorter than its diff:
```python
import functools

import jax
import jax.numpy as jnp
from jax import lax
from jax.experimental import pallas as pl
from jax.experimental.pallas import tpu as pltpu
from jax.sharding import PartitionSpec as P

F32 = jnp.float32
BF16 = jnp.bfloat16
LANES = 128
STEP = 4
VMEM = pl.BlockSpec(memory_space=pltpu.VMEM)

PLACE = {0: (1, 1), 1: (0, 0), 2: (1, 0)}


def split(x):
    hi = x.astype(BF16)
    return hi, (x - hi.astype(F32)).astype(BF16)


def pairing(half, transposed):
    size = 4 * half
    cell = lax.broadcasted_iota(jnp.int32, (size, size), 0 if transposed else 1)
    source = lax.broadcasted_iota(jnp.int32, (size, size), 1 if transposed else 0)
    parity, rest = cell // (2 * half), cell % (2 * half)
    wanted = (rest // half) * (2 * half) + 2 * (rest % half) + parity
    return (source == wanted).astype(F32).astype(BF16)


def lane_of(shape):
    return lax.broadcasted_iota(jnp.int32, shape, 1)


def parity_split(load, planes, step, matrix, half):
    tiles = []
    for plane in range(planes):
        for parity in range(2):
            for j in range(STEP):
                row = 4 * (step * STEP + j) + parity
                tiles.append(jnp.concatenate([load(plane, row), load(plane, row + 2)], axis=1))
    chans = tiles[0].shape[0]
    hi, lo = split(jnp.concatenate(tiles, axis=0))
    moved = jnp.dot(jnp.concatenate([hi, lo], axis=0), matrix, preferred_element_type=F32).astype(BF16)
    parts = []
    for part in range(2):
        rows = []
        for group in range(planes * 2):
            for column in range(2):
                pieces = []
                for j in range(STEP):
                    start = ((part * planes * 2 + group) * STEP + j) * chans
                    pieces.append(moved[start : start + chans, column * LANES : (column + 1) * LANES])
                rows.append(jnp.concatenate(pieces, axis=1))
        parts.append(jnp.concatenate(rows, axis=0))
    return parts


def shift_add(y, outs, half, carry):
    lane = lane_of((outs, LANES))
    first_column = lane % half == 0
    first_row = lane < half

    def one_column(v):
        return jnp.where(first_column, 0.0, pltpu.roll(v, 1, 1))

    pieces = []
    for j in range(STEP):
        v = [y[s * outs : (s + 1) * outs, j * LANES : (j + 1) * LANES] for s in range(4)]
        here = v[0] + one_column(v[1])
        late = pltpu.roll(v[2] + one_column(v[3]), half, 1)
        pieces.append(here + jnp.where(first_row, carry, late))
        carry = late
    return jnp.concatenate(pieces, axis=1), carry


def own_kernel(dims, vol, filt, x_hi, x_lo, part, w_halo, w_back, w_spill, w_t):
    chans, outs, planes, height, half = dims
    w_t[...] = jnp.zeros_like(w_t)
    for p in range(3):
        for q in range(3):
            for r in range(3):
                (rho, sb), (gamma, sc) = PLACE[q], PLACE[r]
                top = ((p * 2 + rho) * 2 + gamma) * chans
                left = (sb * 2 + sc) * outs
                tap = (p * 3 + q) * 3 + r
                w_t[top : top + chans, left : left + outs] = filt[tap * chans : (tap + 1) * chans, :]
    edge = 4 * chans
    hi, lo = split(w_t[...])
    w_spill[...] = jnp.concatenate([hi[:edge], hi[:edge], lo[:edge]], axis=1)
    w_back[...] = jnp.concatenate([hi[edge:], hi[edge:], lo[edge:]], axis=1)
    hi, lo = hi.astype(F32), lo.astype(F32)
    w_halo[...] = jnp.concatenate([hi[:edge], hi[:edge], lo[:edge]], axis=0).T.astype(BF16)
    w_own = jnp.concatenate([hi[edge:], hi[edge:], lo[edge:]], axis=0).T.astype(BF16)
    matrix = pairing(half, False)

    def load(plane, row):
        return vol[pl.ds(plane * height + row, chans, stride=planes * height), :]

    def body(step, carry):
        hi, lo = parity_split(load, planes, step, matrix, half)
        cells = pl.ds(pl.multiple_of(step * STEP * LANES, STEP * LANES), STEP * LANES)
        x_hi[:, cells] = hi
        x_lo[:, cells] = lo
        y = jnp.dot(w_own, jnp.concatenate([hi, lo, hi], axis=0), preferred_element_type=F32)
        total, carry = shift_add(y, outs, half, carry)
        part[:, cells] = total
        return carry

    lax.fori_loop(0, height // (4 * STEP), body, jnp.zeros((outs, LANES), F32))


def halo_kernel(dims, own, count, plane, part, w_halo, x_hi, x_lo, *rest):
    chans, outs, planes, height, half = dims
    results, total_ref = rest[:-1], rest[-1]
    matrix = pairing(half, False)
    weights = w_halo[...]

    def load(_, row):
        return plane[pl.ds(row, chans, stride=height), :]

    def body(step, carry):
        hi, lo = parity_split(load, 1, step, matrix, half)
        cells = pl.ds(pl.multiple_of(step * STEP * LANES, STEP * LANES), STEP * LANES)
        x_hi[:, cells] = hi
        x_lo[:, cells] = lo
        y = jnp.dot(weights, jnp.concatenate([hi, lo, hi], axis=0), preferred_element_type=F32)
        total, carry = shift_add(y, outs, half, carry)
        total_ref[:, cells] = part[:, cells] + total
        return carry

    lax.fori_loop(0, height // (4 * STEP), body, jnp.zeros((outs, LANES), F32))
    me = lax.axis_index("chan")
    for k in range(count):
        start = pl.multiple_of(lax.rem(me + k, count) * own, own)
        results[k][...] = total_ref[pl.ds(start, own), :]


def filter_kernel(dims, own, count, *refs):
    chans, outs, planes, height, half = dims
    grads, (x_hi, x_lo, xh_hi, xh_lo) = refs[:count], refs[count : count + 4]
    g_hi, g_lo, packed, g_all, total = refs[count + 4 :]
    cells_all = grads[0].shape[1]
    me = lax.axis_index("chan")
    for k in range(count):
        start = pl.multiple_of(lax.rem(me + count - k, count) * own, own)
        g_all[pl.ds(start, own), :cells_all] = grads[k][...]
    g_all[:, cells_all:] = jnp.zeros((outs, LANES), F32)
    total[...] = jnp.zeros_like(total)
    lane = lane_of((outs, LANES))
    last_column = lane % half == half - 1
    first_row = lane < half

    def one_column(v):
        return jnp.where(last_column, 0.0, pltpu.roll(v, LANES - 1, 1))

    def body(step, _):
        base = step * STEP * LANES
        v = [g_all[:, pl.ds(pl.multiple_of(base + j * LANES, LANES), LANES)] for j in range(STEP + 1)]
        swapped = [pltpu.roll(a, half, 1) for a in v]
        pieces = []
        for j in range(STEP):
            later = jnp.where(first_row, swapped[j], swapped[j + 1])
            pieces.append(jnp.concatenate([v[j], one_column(v[j]), later, one_column(later)], axis=0))
        hi, lo = split(jnp.concatenate(pieces, axis=1))
        cells = pl.ds(pl.multiple_of(base, STEP * LANES), STEP * LANES)
        g_hi[:, cells] = hi
        g_lo[:, cells] = lo
        a_hi = jnp.concatenate([xh_hi[:, cells], x_hi[:, cells]], axis=0)
        a_lo = jnp.concatenate([xh_lo[:, cells], x_lo[:, cells]], axis=0)
        total[...] += lax.dot_general(
            jnp.concatenate([a_hi, a_hi, a_lo], axis=1),
            jnp.concatenate([hi, lo, hi], axis=1),
            (((1,), (1,)), ((), ())),
            preferred_element_type=F32,
        )
        return 0

    lax.fori_loop(0, cells_all // (STEP * LANES), body, 0)

    def tap_block(tap, side):
        p, q, r = tap // 9, tap // 3 % 3, tap % 3
        (rho, sb), (gamma, sc) = PLACE[q], PLACE[r]
        top = ((p * 2 + rho) * 2 + gamma) * chans
        block = total[top : top + chans, sb * LANES : (sb + 1) * LANES]
        return block if sc == side else pltpu.roll(block, outs, 1)

    left_side = lane_of((chans, LANES)) < outs
    for tap in range(14):
        right = tap_block(tap + 14, 1) if tap + 14 < 27 else jnp.zeros((chans, LANES), F32)
        packed[tap * chans : (tap + 1) * chans, :] = jnp.where(left_side, tap_block(tap, 0), right)


def back_kernel(dims, planes, weights, g_hi, g_lo, out):
    chans, outs, _, height, half = dims
    matrix = pairing(half, True)
    matrix = jnp.concatenate([matrix, matrix], axis=0)
    w = weights[...]

    def body(step, _):
        cells = pl.ds(pl.multiple_of(step * STEP * LANES, STEP * LANES), STEP * LANES)
        hi, lo = g_hi[:, cells], g_lo[:, cells]
        grad = jnp.dot(w, jnp.concatenate([hi, lo, hi], axis=0), preferred_element_type=F32)
        tiles = []
        for group in range(planes * 2):
            for j in range(STEP):
                sides = [
                    grad[(group * 2 + column) * chans : (group * 2 + column + 1) * chans, j * LANES : (j + 1) * LANES]
                    for column in range(2)
                ]
                tiles.append(jnp.concatenate(sides, axis=1))
        hi, lo = split(jnp.concatenate(tiles, axis=0))
        rows = jnp.dot(jnp.concatenate([hi, lo], axis=1), matrix, preferred_element_type=F32)
        for group in range(planes * 2):
            for j in range(STEP):
                start = (group * STEP + j) * chans
                row = (group // 2) * height + 4 * (step * STEP + j) + group % 2
                for side in range(2):
                    out[pl.ds(row + 2 * side, chans, stride=planes * height), :] = rows[
                        start : start + chans, side * LANES : (side + 1) * LANES
                    ]
        return 0

    lax.fori_loop(0, height // (4 * STEP), body, 0)


def call(kernel, name, shapes, scratch, *args):
    return pl.pallas_call(
        kernel,
        name=name,
        out_shape=[jax.ShapeDtypeStruct(s, t) for s, t in shapes],
        in_specs=[VMEM] * len(args),
        out_specs=[VMEM] * len(shapes),
        scratch_shapes=scratch,
        compiler_params=pltpu.CompilerParams(vmem_limit_bytes=48 * 1024 * 1024),
    )(*args)


def turned(value, axis, steps):
    count = lax.axis_size(axis)
    return lax.ppermute(value, axis, [(s, (s + steps) % count) for s in range(count)])


def from_behind(value, axis, steps):
    count = lax.axis_size(axis)
    initial, last = (max(0, -steps), min(count, count - steps))
    return lax.ppermute(value, axis, [(source, source + steps) for source in range(initial, last)])


def sum_over(value, axis):
    count = lax.axis_size(axis)
    if count & (count - 1):
        return lax.psum(value, axis)
    bit = 1
    while bit < count:
        value = value + lax.ppermute(value, axis, [(s, s ^ bit) for s in range(count)])
        bit *= 2
    return value


def on_device(volume, filters, cotangent):
    real, planes, height, width = volume.shape
    outs = filters.shape[0]
    own = cotangent.shape[0]
    count = lax.axis_size("chan")
    half = width // 2
    cells = (height // 2) * half
    assert planes == 2 and width == LANES and height % (4 * STEP) == 0 and 2 * outs == LANES
    chans = -(-real // 16) * 16
    taps = filters.transpose(2, 3, 4, 1, 0)
    if chans > real:
        volume = jnp.pad(volume, ((0, chans - real), (0, 0), (0, 0), (0, 0)))
        taps = jnp.pad(taps, ((0, 0), (0, 0), (0, 0), (0, chans - real), (0, 0)))
    dims = (chans, outs, planes, height, half)
    halo = from_behind(volume[:, -1], "space", 1)
    x_hi, x_lo, part, w_halo, w_back, w_spill = call(
        functools.partial(own_kernel, dims),
        "own",
        [
            ((8 * chans, cells), BF16),
            ((8 * chans, cells), BF16),
            ((outs, cells), F32),
            ((4 * outs, 12 * chans), BF16),
            ((8 * chans, 12 * outs), BF16),
            ((4 * chans, 12 * outs), BF16),
        ],
        [pltpu.VMEM((12 * chans, 4 * outs), F32)],
        volume.reshape(chans * planes * height, width),
        taps.reshape(27 * chans, outs),
    )
    xh_hi, xh_lo, *pieces = call(
        functools.partial(halo_kernel, dims, own, count),
        "halo",
        [((4 * chans, cells), BF16)] * 2 + [((own, cells), F32)] * count,
        [pltpu.VMEM((outs, cells), F32)],
        halo.reshape(chans * height, width),
        part,
        w_halo,
    )
    preact = pieces[0]
    for k in range(1, count):
        preact = preact + turned(pieces[k], "chan", k)
    activated = jax.nn.softplus(preact).reshape(cotangent.shape)
    grad = cotangent.reshape(own, cells) * jax.nn.sigmoid(preact)
    grads = [grad] + [turned(grad, "chan", k) for k in range(1, count)]
    g_hi, g_lo, packed = call(
        functools.partial(filter_kernel, dims, own, count),
        "filter",
        [((4 * outs, cells), BF16)] * 2 + [((14 * chans, LANES), F32)],
        [pltpu.VMEM((outs, cells + LANES), F32), pltpu.VMEM((12 * chans, 4 * outs), F32)],
        *grads,
        x_hi,
        x_lo,
        xh_hi,
        xh_lo,
    )
    packed = sum_over(packed, "space")
    (spill,) = call(
        functools.partial(back_kernel, dims, 1), "spill", [((chans * height, width), F32)], [], w_spill, g_hi, g_lo
    )
    spilled = from_behind(spill, "space", -1)
    (volume_grad,) = call(
        functools.partial(back_kernel, dims, 2), "back", [((chans * 2 * height, width), F32)], [], w_back, g_hi, g_lo
    )
    volume_grad = volume_grad.reshape(chans, planes, height, width)
    volume_grad = volume_grad.at[:, -1].add(spilled.reshape(chans, height, width))[:real]
    depth_all = planes * lax.axis_size("space")
    factor = float(depth_all // 2 * (height // 2) * half) ** (-0.5)
    unpacked = jnp.concatenate([packed[:, :outs], packed[: 13 * chans, outs:]], axis=0) * factor
    filter_grad = unpacked.reshape(3, 3, 3, chans, outs)[:, :, :, :real].transpose(4, 3, 0, 1, 2)
    return (activated, volume_grad, filter_grad)


def solution(mesh):
    in_specs = (
        P("chan", "space", None, None),
        P(None, "chan", None, None, None),
        P("chan", "space", None, None),
    )
    out_specs = (
        P("chan", "space", None, None),
        P("chan", "space", None, None),
        P(None, "chan", None, None, None),
    )
    return jax.shard_map(
        on_device, mesh=mesh, in_specs=in_specs, out_specs=out_specs, check_vma=False
    )
```

time: 651 us -> 109 us (0.17)
  matrix products: 283 us -> 0 us
  waiting for transfers between devices: 199 us -> 30.6 us
  local copies, waits for them, and re-layouts: 116 us -> 12.9 us
  Pallas kernels: 0 us -> 28.2 us
  starting transfers between devices: 3.81 us -> 29.8 us
  other arithmetic: 24.5 us -> 6.68 us
  between operations: 14.1 us -> 0.75 us
  blocking collectives: 7.07 us -> 0 us
    conv_general_dilated x3 -> x0, matrix products: 283 us -> none  [conv_local(): lax.conv_general_dilated(extended[None], filters, (2, 2, 2), ((0, 0), (1,...]
    all_gather x2 -> x0, waiting for transfers between devices: 113 us -> none  [the longest x1 79.3 us: on_device(): lax.all_gather(extended, 'chan', axis=0, tiled=True)]
    psum x1 -> x0, waiting for transfers between devices: 85.9 us -> none  [on_device(): summed = lax.psum(grad_filters, 'space')]
    conv_general_dilated x6 -> x0, local copies, waits for them, and re-layouts: 48.8 us -> none  [conv_local(): lax.conv_general_dilated(extended[None], filters, (2, 2, 2), ((0, 0), (1,...]
    ppermute x0 -> x6, waiting for transfers between devices: none -> 30.6 us  [the longest x4 17.7 us: sum_over(): lax.ppermute(value, axis, [(s, s ^ bit) for s in range(count)])]
    pallas_call x0 -> x5, Pallas kernels: none -> 28.2 us  [call(): pl.pallas_call(kernel, name=name, out_shape=[jax.ShapeDtypeStruct(s, t) f...]
    ppermute x0 -> x6, starting transfers between devices: none -> 26 us  [the longest x4 21.6 us: sum_over(): lax.ppermute(value, axis, [(s, s ^ bit) for s in range(count)])]
    concatenate x1 -> x0, other arithmetic: 18.6 us -> none  [on_device(): extended = jnp.concatenate([below[:, None], volume], axis=1)]
  transfers between devices with their start and end apart: 5 -> 8, of which waited for: 3 -> 5; matrix products, arithmetic and copies ran while one was open for 27% -> 6% of each run, Pallas kernels for 0% -> 11%
where the time goes in v1:
time: 109 us
  waiting for transfers between devices  30.6 us (28%)
  starting transfers between devices  29.8 us (27%)
  Pallas kernels  28.2 us (26%)
  local copies, waits for them, and re-layouts  12.9 us (12%)
  other arithmetic  6.68 us (6%)
    pallas_call x5, Pallas kernels, call(): pl.pallas_call(kernel, name=name, out_shape=[jax.ShapeDtypeStruct(s, t) f...  28.2 us
    ppermute x4, starting transfers between devices, sum_over(): lax.ppermute(value, axis, [(s, s ^ bit) for s in range(count)])  21.6 us
    ppermute x4, waiting for transfers between devices, sum_over(): lax.ppermute(value, axis, [(s, s ^ bit) for s in range(count)])  17.7 us
    ppermute x2, waiting for transfers between devices, turned(): lax.ppermute(value, axis, [(s, (s + steps) % count) for s in range(count)])  12.9 us
    unnamed x16, local copies, waits for them, and re-layouts  6.52 us
    ppermute x2, starting transfers between devices, turned(): lax.ppermute(value, axis, [(s, (s + steps) % count) for s in range(count)])  4.35 us
    ppermute x2, starting transfers between devices, from_behind(): lax.ppermute(value, axis, [(source, source + steps) for source in range(i...  3.85 us
    scatter-add x1, other arithmetic, on_device(): volume_grad.at[:, -1].add(spilled.reshape(chans, height, width))[:real]  2.64 us
  transfers between devices with their start and end apart: 8, of which 5 were waited for; matrix products, arithmetic and copies ran while one was open for 6% of the time, Pallas kernels for 11%

profile of v1, /device:TPU:0, one launch (start us, length us, event | category | flops | bytes accessed | tf_op | source)
XLA Modules:
  0.0 108.9 jit_solution(1835300723818147271)
XLA Ops:
  0.6 1.4 %slice_bitcast_fusion = f32[16,128,128]{2,1,0:T(8,128)S(1)} fusion(f32[16,2,128,128]{3,2,1,0:T(8,128)} %param.5), kind=kLoop, calls=%fused_computation.3 | loop fusion | bytes 2097152 | tf_op jit(solution)/shard_map/squeeze | solution.py:277
  2.1 2.4 %collective-permute-start = (f32[16,128,128]{2,1,0:T(8,128)S(1)}, f32[16,128,128]{2,1,0:T(8,128)S(1)}, u32[]{:S(2)}, u32[]{:S(2)}) collective-permute-start(f32[16,128,128]{2,1,0:T(8,128)S(1)} %slice_bitcast_fusion), channel_id=1, source_target_pairs={{0,2},{2,4},{4,6},{6,8},{8,10},{10,12},{12,14},{14,16},{16,18},{18... | collective-permute-start | bytes 3145736 | tf_op jit(solution)/shard_map/ppermute | solution.py:249
  4.5 0.9 copy-done.7
  5.5 5.9 %own.1 = (bf16[128,4096]{1,0:T(8,128)(2,1)S(1)}, bf16[128,4096]{1,0:T(8,128)(2,1)S(1)}, f32[64,4096]{1,0:T(8,128)S(1)}, bf16[256,192]{1,0:T(8,128)(2,1)S(1)}, bf...) custom-call(f32[4096,128]{1,0:T(8,128)S(1)} %bitcast.18, f32[432,64]{1,0:T(8,128)S(1)} %bitcast.20), custom_call_target="tpu_custom_call" | custom-call | tf_op jit(solution)/shard_map/own/pallas_call | solution.py:230
  11.4 5.9 %halo.1 = (bf16[64,4096]{1,0:T(8,128)(2,1)S(1)}, bf16[64,4096]{1,0:T(8,128)(2,1)S(1)}, f32[32,4096]{1,0:T(8,128)S(1)}, f32[32,4096]{1,0:T(8,128)}) custom-call(f32[2048,128]{1,0:T(8,128)S(1)} %bitcast.19, f32[64,4096]{1,0:T(8,128)S(1)} %get-tuple-element.28.part, bf16[256,192]{1,0:T(8,128)(2,1)S(1)} %get-tuple-element.29.w_halo), custom_call_target="tpu_custom_call" | custom-call | tf_op jit(solution)/shard_map/halo/pallas_call | solution.py:230
  17.3 0.8 copy-done.5
  18.1 2.3 %collective-permute-start.1 = (f32[32,4096]{1,0:T(8,128)}, f32[32,4096]{1,0:T(8,128)}, u32[]{:S(2)}, u32[]{:S(2)}) collective-permute-start(f32[32,4096]{1,0:T(8,128)} %get-tuple-element.31), channel_id=1, source_target_pairs={{0,1},{1,0},{2,3},{3,2},{4,5},{5,4},{6,7},{7,6},{8,9},{9,8},{10,11... | collective-permute-start | bytes 1572872 | tf_op jit(solution)/shard_map/ppermute | solution.py:243
  20.4 2.4 %reshape.70 = f32[32,4096]{1,0:T(8,128)} reshape(f32[32,1,64,64]{3,2,1,0:T(8,128)} %param.7) | data formatting | bytes 1048576 | tf_op jit(solution)/shard_map/reshape | solution.py:306
  22.8 5.1 %collective-permute-done.1 = f32[32,4096]{1,0:T(8,128)} collective-permute-done((f32[32,4096]{1,0:T(8,128)}, f32[32,4096]{1,0:T(8,128)}, u32[]{:S(2)}, u32[]{:S(2)}) %collective-permute-start.1) | collective-permute-done | bytes 524320 | tf_op jit(solution)/shard_map/ppermute | solution.py:243
  27.9 2.4 %divide_multiply_fusion = (f32[32,4096]{1,0:T(8,128)S(1)}, f32[32,4096]{1,0:T(8,128)}) fusion(f32[32,4096]{1,0:T(8,128)} %reshape.70, f32[32,4096]{1,0:T(8,128)S(1)} %get-tuple-element.30, f32[32,4096]{1,0:T(8,128)} %collective-permute-done.1), kind=kLoop, calls=%fused_computation.4 | loop fusion | flops 1441792 | bytes 2621440 | tf_op jit(solution)/shard_map/mul | solution.py:306
  30.3 2.0 %collective-permute-start.2 = (f32[32,4096]{1,0:T(8,128)S(1)}, f32[32,4096]{1,0:T(8,128)S(1)}, u32[]{:S(2)}, u32[]{:S(2)}) collective-permute-start(f32[32,4096]{1,0:T(8,128)S(1)} %get-tuple-element.44.refs_0_), channel_id=1, source_target_pairs={{0,1},{1,0},{2,3},{3,2},{4,5},{5,4},{6,7},{7,6},{8,9},{9,8},{10,11... | collective-permute-start | bytes 1572872 | tf_op jit(solution)/shard_map/ppermute | solution.py:243
  32.3 7.8 %collective-permute-done.2.refs_1_ = f32[32,4096]{1,0:T(8,128)S(1)} collective-permute-done((f32[32,4096]{1,0:T(8,128)S(1)}, f32[32,4096]{1,0:T(8,128)S(1)}, u32[]{:S(2)}, u32[]{:S(2)}) %collective-permute-start.2) | collective-permute-done | bytes 524320 | tf_op jit(solution)/shard_map/ppermute | solution.py:243
  40.1 6.2 %filter.1 = (bf16[256,4096]{1,0:T(8,128)(2,1)}, bf16[256,4096]{1,0:T(8,128)(2,1)}, f32[224,128]{1,0:T(8,128)S(1)}) custom-call(f32[32,4096]{1,0:T(8,128)S(1)} %get-tuple-element.44.refs_0_, f32[32,4096]{1,0:T(8,128)S(1)} %collective-permute-done.2.refs_1_, bf16[128,4096]{1,0:T(8,128)(2,1)S(1)} %get-tuple-element.33.refs_2_, ...), custom_call_target="tpu_custom_call" | custom-call | tf_op jit(solution)/shard_map/filter/pallas_call | solution.py:230
  46.3 1.6 %copy-done = bf16[256,4096]{1,0:T(8,128)(2,1)S(1)} copy-done((bf16[256,4096]{1,0:T(8,128)(2,1)S(1)}, bf16[256,4096]{1,0:T(8,128)(2,1)}, u32[]{:S(2)}) %copy-start) | copy-done | bytes 2097176
  47.9 1.6 %copy-done.2 = bf16[256,4096]{1,0:T(8,128)(2,1)S(1)} copy-done((bf16[256,4096]{1,0:T(8,128)(2,1)S(1)}, bf16[256,4096]{1,0:T(8,128)(2,1)}, u32[]{:S(2)}) %copy-start.2) | copy-done | bytes 2097176
  49.4 4.2 %spill.1 = f32[2048,128]{1,0:T(8,128)S(1)} custom-call(bf16[64,768]{1,0:T(8,128)(2,1)S(1)} %get-tuple-element.39.weights, bf16[256,4096]{1,0:T(8,128)(2,1)S(1)} %copy-done, bf16[256,4096]{1,0:T(8,128)(2,1)S(1)} %copy-done.2), custom_call_target="tpu_custom_call" | custom-call | tf_op jit(solution)/shard_map/spill/pallas_call | solution.py:230
  53.7 0.0 copy-start.1
  53.7 1.4 %collective-permute-start.3 = (f32[2048,128]{1,0:T(8,128)S(1)}, f32[2048,128]{1,0:T(8,128)}, u32[]{:S(2)}, u32[]{:S(2)}) collective-permute-start(f32[2048,128]{1,0:T(8,128)S(1)} %spill.1), channel_id=1, source_target_pairs={{2,0},{4,2},{6,4},{8,6},{10,8},{12,10},{14,12},{16,14},{18,16},{20... | collective-permute-start | bytes 3145736 | tf_op jit(solution)/shard_map/ppermute | solution.py:249
  55.1 5.7 %collective-permute-start.4 = (f32[224,128]{1,0:T(8,128)S(1)}, f32[224,128]{1,0:T(8,128)S(1)}, u32[]{:S(2)}, u32[]{:S(2)}) collective-permute-start(f32[224,128]{1,0:T(8,128)S(1)} %get-tuple-element.40), channel_id=1, source_target_pairs={{0,2},{2,0},{4,6},{6,4},{8,10},{10,8},{12,14},{14,12},{16,18},{18,... | collective-permute-start | bytes 344072 | tf_op jit(solution)/shard_map/ppermute | solution.py:258
  60.8 1.8 %collective-permute-done.4 = f32[224,128]{1,0:T(8,128)S(1)} collective-permute-done((f32[224,128]{1,0:T(8,128)S(1)}, f32[224,128]{1,0:T(8,128)S(1)}, u32[]{:S(2)}, u32[]{:S(2)}) %collective-permute-start.4) | collective-permute-done | bytes 114720 | tf_op jit(solution)/shard_map/ppermute | solution.py:258
  62.6 11.2 %collective-permute-start.5 = (f32[224,128]{1,0:T(8,128)S(1)}, f32[224,128]{1,0:T(8,128)S(1)}, u32[]{:S(2)}, u32[]{:S(2)}) collective-permute-start(f32[224,128]{1,0:T(8,128)S(1)} %add.33), channel_id=1, source_target_pairs={{0,4},{2,6},{4,0},{6,2},{8,12},{10,14},{12,8},{14,10},{16,20},{18,... | collective-permute-start | bytes 344072 | tf_op jit(solution)/shard_map/ppermute | solution.py:258
  73.9 12.7 %collective-permute-done.5 = f32[224,128]{1,0:T(8,128)S(1)} collective-permute-done((f32[224,128]{1,0:T(8,128)S(1)}, f32[224,128]{1,0:T(8,128)S(1)}, u32[]{:S(2)}, u32[]{:S(2)}) %collective-permute-start.5) | collective-permute-done | bytes 114720 | tf_op jit(solution)/shard_map/ppermute | solution.py:258
  86.6 1.6 %collective-permute-start.6 = (f32[224,128]{1,0:T(8,128)S(1)}, f32[224,128]{1,0:T(8,128)S(1)}, u32[]{:S(2)}, u32[]{:S(2)}) collective-permute-start(f32[224,128]{1,0:T(8,128)S(1)} %add.34), channel_id=1, source_target_pairs={{0,8},{2,10},{4,12},{6,14},{8,0},{10,2},{12,4},{14,6},{16,24},{18,... | collective-permute-start | bytes 344072 | tf_op jit(solution)/shard_map/ppermute | solution.py:258
  88.2 3.2 %collective-permute-done.6 = f32[224,128]{1,0:T(8,128)S(1)} collective-permute-done((f32[224,128]{1,0:T(8,128)S(1)}, f32[224,128]{1,0:T(8,128)S(1)}, u32[]{:S(2)}, u32[]{:S(2)}) %collective-permute-start.6) | collective-permute-done | bytes 114720 | tf_op jit(solution)/shard_map/ppermute | solution.py:258
  91.4 3.1 %collective-permute-start.7 = (f32[224,128]{1,0:T(8,128)S(1)}, f32[224,128]{1,0:T(8,128)}, u32[]{:S(2)}, u32[]{:S(2)}) collective-permute-start(f32[224,128]{1,0:T(8,128)S(1)} %add.35), channel_id=1, source_target_pairs={{0,16},{2,18},{4,20},{6,22},{8,24},{10,26},{12,28},{14,30},{16,0},... | collective-permute-start | bytes 344072 | tf_op jit(solution)/shard_map/ppermute | solution.py:258
  94.5 2.4 %reshape.69 = f32[32,1,64,64]{3,2,0,1:T(8,128)} reshape(f32[32,4096]{1,0:T(8,128)} %get-tuple-element.45) | data formatting | bytes 1048576 | tf_op jit(solution)/shard_map/reshape | solution.py:305
  97.0 1.6 %copy-done.3 = bf16[256,4096]{1,0:T(8,128)(2,1)S(1)} copy-done((bf16[256,4096]{1,0:T(8,128)(2,1)S(1)}, bf16[256,4096]{1,0:T(8,128)(2,1)}, u32[]{:S(2)}) %copy-start.3) | copy-done | bytes 2097176
  98.6 6.0 %back.1 = f32[4096,128]{1,0:T(8,128)} custom-call(bf16[128,768]{1,0:T(8,128)(2,1)S(1)} %get-tuple-element.32.weights, bf16[256,4096]{1,0:T(8,128)(2,1)S(1)} %copy-done.1, bf16[256,4096]{1,0:T(8,128)(2,1)S(1)} %copy-done.3), custom_call_target="tpu_custom_call" | custom-call | tf_op jit(solution)/shard_map/back/pallas_call | solution.py:230
  104.5 0.9 add.36
  105.4 0.1 slice.42
  105.5 0.7 maximum_multiply_fusion
  106.3 2.6 %fusion = f32[16,2,128,128]{3,2,1,0:T(8,128)} fusion(f32[16,2,128,128]{3,2,1,0:T(8,128)} %bitcast.21, f32[16,1,128,128]{3,2,1,0:T(8,128)} %bitcast.8), kind=kLoop, calls=%fused_computation.2 | loop fusion | flops 262144 | bytes 3145728 | tf_op jit(solution)/shard_map/scatter-add | solution.py:328
  (16 shorter events, 0.1 us)
Async XLA Ops:
  0.6 3.9 %copy-start.4 = (f32[16,2,128,128]{3,2,1,0:T(8,128)S(1)}, f32[16,2,128,128]{3,2,1,0:T(8,128)}, u32[]{:S(2)}) copy-start(f32[16,2,128,128]{3,2,1,0:T(8,128)} %param.5) | copy-start | bytes 6291460
  2.1 9.3 %collective-permute-start = (f32[16,128,128]{2,1,0:T(8,128)S(1)}, f32[16,128,128]{2,1,0:T(8,128)S(1)}, u32[]{:S(2)}, u32[]{:S(2)}) collective-permute-start(f32[16,128,128]{2,1,0:T(8,128)S(1)} %slice_bitcast_fusion), channel_id=1, source_target_pairs={{0,2},{2,4},{4,6},{6,8},{8,10},{10,12},{12,14},{14,16},{16,18},{18... | collective-permute-start | bytes 3145736 | tf_op jit(solution)/shard_map/ppermute | solution.py:249
  4.5 0.9 copy-start.7
  17.3 0.8 copy-start.5
  18.1 9.8 %collective-permute-start.1 = (f32[32,4096]{1,0:T(8,128)}, f32[32,4096]{1,0:T(8,128)}, u32[]{:S(2)}, u32[]{:S(2)}) collective-permute-start(f32[32,4096]{1,0:T(8,128)} %get-tuple-element.31), channel_id=1, source_target_pairs={{0,1},{1,0},{2,3},{3,2},{4,5},{5,4},{6,7},{7,6},{8,9},{9,8},{10,11... | collective-permute-start | bytes 1572872 | tf_op jit(solution)/shard_map/ppermute | solution.py:243
  22.8 17.3 %copy-start.6 = (bf16[64,4096]{1,0:T(8,128)(2,1)S(1)}, bf16[64,4096]{1,0:T(8,128)(2,1)}, u32[]{:S(2)}) copy-start(bf16[64,4096]{1,0:T(8,128)(2,1)} %copy-done.5) | copy-start | bytes 1572868
  30.3 9.8 %collective-permute-start.2 = (f32[32,4096]{1,0:T(8,128)S(1)}, f32[32,4096]{1,0:T(8,128)S(1)}, u32[]{:S(2)}, u32[]{:S(2)}) collective-permute-start(f32[32,4096]{1,0:T(8,128)S(1)} %get-tuple-element.44.refs_0_), channel_id=1, source_target_pairs={{0,1},{1,0},{2,3},{3,2},{4,5},{5,4},{6,7},{7,6},{8,9},{9,8},{10,11... | collective-permute-start | bytes 1572872 | tf_op jit(solution)/shard_map/ppermute | solution.py:243
  46.3 1.6 %copy-start = (bf16[256,4096]{1,0:T(8,128)(2,1)S(1)}, bf16[256,4096]{1,0:T(8,128)(2,1)}, u32[]{:S(2)}) copy-start(bf16[256,4096]{1,0:T(8,128)(2,1)} %get-tuple-element.37.g_hi) | copy-start | bytes 6291460
  47.9 1.6 %copy-start.2 = (bf16[256,4096]{1,0:T(8,128)(2,1)S(1)}, bf16[256,4096]{1,0:T(8,128)(2,1)}, u32[]{:S(2)}) copy-start(bf16[256,4096]{1,0:T(8,128)(2,1)} %get-tuple-element.38.g_lo) | copy-start | bytes 6291460
  53.7 43.3 %copy-start.1 = (bf16[256,4096]{1,0:T(8,128)(2,1)S(1)}, bf16[256,4096]{1,0:T(8,128)(2,1)}, u32[]{:S(2)}) copy-start(bf16[256,4096]{1,0:T(8,128)(2,1)} %get-tuple-element.37.g_hi) | copy-start | bytes 6291460
  53.7 52.6 %collective-permute-start.3 = (f32[2048,128]{1,0:T(8,128)S(1)}, f32[2048,128]{1,0:T(8,128)}, u32[]{:S(2)}, u32[]{:S(2)}) collective-permute-start(f32[2048,128]{1,0:T(8,128)S(1)} %spill.1), channel_id=1, source_target_pairs={{2,0},{4,2},{6,4},{8,6},{10,8},{12,10},{14,12},{16,14},{18,16},{20... | collective-permute-start | bytes 3145736 | tf_op jit(solution)/shard_map/ppermute | solution.py:249
  55.1 7.5 %collective-permute-start.4 = (f32[224,128]{1,0:T(8,128)S(1)}, f32[224,128]{1,0:T(8,128)S(1)}, u32[]{:S(2)}, u32[]{:S(2)}) collective-permute-start(f32[224,128]{1,0:T(8,128)S(1)} %get-tuple-element.40), channel_id=1, source_target_pairs={{0,2},{2,0},{4,6},{6,4},{8,10},{10,8},{12,14},{14,12},{16,18},{18,... | collective-permute-start | bytes 344072 | tf_op jit(solution)/shard_map/ppermute | solution.py:258
  62.6 23.9 %collective-permute-start.5 = (f32[224,128]{1,0:T(8,128)S(1)}, f32[224,128]{1,0:T(8,128)S(1)}, u32[]{:S(2)}, u32[]{:S(2)}) collective-permute-start(f32[224,128]{1,0:T(8,128)S(1)} %add.33), channel_id=1, source_target_pairs={{0,4},{2,6},{4,0},{6,2},{8,12},{10,14},{12,8},{14,10},{16,20},{18,... | collective-permute-start | bytes 344072 | tf_op jit(solution)/shard_map/ppermute | solution.py:258
  86.6 4.9 %collective-permute-start.6 = (f32[224,128]{1,0:T(8,128)S(1)}, f32[224,128]{1,0:T(8,128)S(1)}, u32[]{:S(2)}, u32[]{:S(2)}) collective-permute-start(f32[224,128]{1,0:T(8,128)S(1)} %add.34), channel_id=1, source_target_pairs={{0,8},{2,10},{4,12},{6,14},{8,0},{10,2},{12,4},{14,6},{16,24},{18,... | collective-permute-start | bytes 344072 | tf_op jit(solution)/shard_map/ppermute | solution.py:258
  91.4 13.1 %collective-permute-start.7 = (f32[224,128]{1,0:T(8,128)S(1)}, f32[224,128]{1,0:T(8,128)}, u32[]{:S(2)}, u32[]{:S(2)}) collective-permute-start(f32[224,128]{1,0:T(8,128)S(1)} %add.35), channel_id=1, source_target_pairs={{0,16},{2,18},{4,20},{6,22},{8,24},{10,26},{12,28},{14,30},{16,0},... | collective-permute-start | bytes 344072 | tf_op jit(solution)/shard_map/ppermute | solution.py:258
  97.0 1.6 %copy-start.3 = (bf16[256,4096]{1,0:T(8,128)(2,1)S(1)}, bf16[256,4096]{1,0:T(8,128)(2,1)}, u32[]{:S(2)}) copy-start(bf16[256,4096]{1,0:T(8,128)(2,1)} %get-tuple-element.38.g_lo) | copy-start | bytes 6291460

commit v2 on v1

v2 whole, which is shorter than its diff:
```python
import functools

import jax
import jax.numpy as jnp
from jax import lax
from jax.experimental import pallas as pl
from jax.experimental.pallas import tpu as pltpu
from jax.sharding import PartitionSpec as P

F32 = jnp.float32
BF16 = jnp.bfloat16
LANES = 128
STEP = 8
CHUNKS = 2
VMEM = pl.BlockSpec(memory_space=pltpu.VMEM)
ANY = pl.BlockSpec(memory_space=pl.ANY)

PLACE = {0: (1, 1), 1: (0, 0), 2: (1, 0)}


def split(x):
    hi = x.astype(BF16)
    return hi, (x - hi.astype(F32)).astype(BF16)


def pairing(half, transposed):
    size = 4 * half
    cell = lax.broadcasted_iota(jnp.int32, (size, size), 0 if transposed else 1)
    source = lax.broadcasted_iota(jnp.int32, (size, size), 1 if transposed else 0)
    parity, rest = cell // (2 * half), cell % (2 * half)
    wanted = (rest // half) * (2 * half) + 2 * (rest % half) + parity
    return (source == wanted).astype(F32).astype(BF16)


def lane_of(shape):
    return lax.broadcasted_iota(jnp.int32, shape, 1)


def group(index, count=1):
    return slice(index * LANES, (index + count) * LANES)


def parity_split(load, planes, first, matrix):
    tiles = []
    for plane in range(planes):
        for parity in range(2):
            for j in range(STEP):
                row = 4 * (first + j) + parity
                tiles.append(jnp.concatenate([load(plane, row), load(plane, row + 2)], axis=1))
    chans = tiles[0].shape[0]
    hi, lo = split(jnp.concatenate(tiles, axis=0))
    moved = jnp.dot(jnp.concatenate([hi, lo], axis=0), matrix, preferred_element_type=F32).astype(BF16)
    parts = []
    for part in range(2):
        rows = []
        for parity in range(planes * 2):
            for column in range(2):
                pieces = []
                for j in range(STEP):
                    start = ((part * planes * 2 + parity) * STEP + j) * chans
                    pieces.append(moved[start : start + chans, group(column)])
                rows.append(jnp.concatenate(pieces, axis=1))
        parts.append(jnp.concatenate(rows, axis=0))
    return parts


def shift_add(y, outs, half, carry):
    lane = lane_of((outs, LANES))
    first_column = lane % half == 0
    first_row = lane < half

    def one_column(v):
        return jnp.where(first_column, 0.0, pltpu.roll(v, 1, 1))

    pieces = []
    for j in range(STEP):
        v = [y[s * outs : (s + 1) * outs, group(j)] for s in range(4)]
        here = v[0] + one_column(v[1])
        late = pltpu.roll(v[2] + one_column(v[3]), half, 1)
        pieces.append(here + jnp.where(first_row, carry, late))
        carry = late
    return jnp.concatenate(pieces, axis=1), carry


def grad_shifts(load, first, count, outs, half):
    lane = lane_of((outs, LANES))
    last_column = lane % half == half - 1
    first_row = lane < half

    def one_column(v):
        return jnp.where(last_column, 0.0, pltpu.roll(v, LANES - 1, 1))

    v = [load(first + j) for j in range(count + 1)]
    swapped = [pltpu.roll(a, half, 1) for a in v]
    pieces = []
    for j in range(count):
        later = jnp.where(first_row, swapped[j], swapped[j + 1])
        pieces.append(jnp.concatenate([v[j], one_column(v[j]), later, one_column(later)], axis=0))
    return split(jnp.concatenate(pieces, axis=1))


def gather_grads(pieces, scratch, own, count):
    me = lax.axis_index("chan")
    left = 0
    for chunk in range(len(pieces) // count):
        for k in range(count):
            piece = pieces[chunk * count + k]
            start = pl.multiple_of(lax.rem(me + count - k, count) * own, own)
            scratch[pl.ds(start, own), left : left + piece.shape[1]] = piece[...]
        left += piece.shape[1]
    if left < scratch.shape[1]:
        scratch[:, left:] = jnp.zeros((scratch.shape[0], scratch.shape[1] - left), F32)


def own_kernel(dims, vol, filt, x_hi, x_lo, part, w_halo, w_back, w_next, w_t):
    chans, outs, planes, height, half = dims
    w_t[...] = jnp.zeros_like(w_t)
    for p in range(3):
        for q in range(3):
            for r in range(3):
                (rho, sb), (gamma, sc) = PLACE[q], PLACE[r]
                top = ((p * 2 + rho) * 2 + gamma) * chans
                left = (sb * 2 + sc) * outs
                tap = (p * 3 + q) * 3 + r
                w_t[top : top + chans, left : left + outs] = filt[tap * chans : (tap + 1) * chans, :]
    edge = 4 * chans
    hi, lo = split(w_t[...])
    w_next[...] = jnp.concatenate([hi[:edge], hi[:edge], lo[:edge]], axis=1)
    w_back[...] = jnp.concatenate([hi[edge:], hi[edge:], lo[edge:]], axis=1)
    hi, lo = hi.astype(F32), lo.astype(F32)
    w_halo[...] = jnp.concatenate([hi[:edge], hi[:edge], lo[:edge]], axis=0).T.astype(BF16)
    w_own = jnp.concatenate([hi[edge:], hi[edge:], lo[edge:]], axis=0).T.astype(BF16)
    matrix = pairing(half, False)

    def load(plane, row):
        return vol[pl.ds(plane * height + row, chans, stride=planes * height), :]

    carry = jnp.zeros((outs, LANES), F32)
    for first in range(0, height // 4, STEP):
        hi, lo = parity_split(load, planes, first, matrix)
        cells = group(first, STEP)
        x_hi[:, cells] = hi
        x_lo[:, cells] = lo
        y = jnp.dot(w_own, jnp.concatenate([hi, lo, hi], axis=0), preferred_element_type=F32)
        part[:, cells], carry = shift_add(y, outs, half, carry)


def halo_kernel(dims, own, count, chunk, *refs):
    chans, outs, planes, height, half = dims
    plane, part, w_halo = refs[:3]
    before = refs[3] if chunk else None
    x_hi, x_lo, *results, total = refs[4 if chunk else 3 :]
    after = results[count] if len(results) > count else None
    matrix = pairing(half, False)
    weights = w_halo[...]
    rows = height // CHUNKS

    def load(_, row):
        return plane[pl.ds(row, chans, stride=rows), :]

    carry = before[...] if chunk else jnp.zeros((outs, LANES), F32)
    for first in range(0, rows // 4, STEP):
        hi, lo = parity_split(load, 1, first, matrix)
        cells = group(first, STEP)
        x_hi[:, cells] = hi
        x_lo[:, cells] = lo
        y = jnp.dot(weights, jnp.concatenate([hi, lo, hi], axis=0), preferred_element_type=F32)
        added, carry = shift_add(y, outs, half, carry)
        total[:, cells] = part[:, group(chunk * (rows // 4) + first, STEP)] + added
    if after is not None:
        after[...] = carry
    me = lax.axis_index("chan")
    for k in range(count):
        start = pl.multiple_of(lax.rem(me + k, count) * own, own)
        results[k][...] = total[pl.ds(start, own), :]


def filter_kernel(dims, own, count, chunk, *refs):
    chans, outs, planes, height, half = dims
    per = height // 4 // CHUNKS
    loaded = min(chunk, 1) + 1
    last = chunk == CHUNKS - 1
    pieces, refs = refs[: loaded * count], refs[loaded * count :]
    (x_hi, x_lo), refs = refs[:2], refs[2:]
    halos, refs = refs[: 2 * loaded], refs[2 * loaded :]
    if chunk:
        before, refs = refs[0], refs[1:]
    out, total, g_all = refs
    gather_grads(pieces, g_all, own, count)
    base = (chunk - loaded + 1) * per
    begin = chunk * per - (1 if chunk else 0)
    end = (chunk + 1) * per - (0 if last else 1)
    total[...] = before[...] if chunk else jnp.zeros_like(total)

    def halo_part(part, first, size):
        found = []
        for h in range(loaded):
            low = max(first - base, h * per)
            high = min(first - base + size, (h + 1) * per)
            if low < high:
                found.append(halos[2 * h + part][:, group(low - h * per, high - low)])
        return found[0] if len(found) == 1 else jnp.concatenate(found, axis=1)

    first = begin
    while first < end:
        size = min(STEP, end - first)
        hi, lo = grad_shifts(lambda g: g_all[:, group(g - base)], first, size, outs, half)
        a_hi = jnp.concatenate([halo_part(0, first, size), x_hi[:, group(first, size)]], axis=0)
        a_lo = jnp.concatenate([halo_part(1, first, size), x_lo[:, group(first, size)]], axis=0)
        total[...] += lax.dot_general(
            jnp.concatenate([a_hi, a_hi, a_lo], axis=1),
            jnp.concatenate([hi, lo, hi], axis=1),
            (((1,), (1,)), ((), ())),
            preferred_element_type=F32,
        )
        first += size
    if not last:
        out[...] = total[...]
        return

    def tap_block(tap, side):
        p, q, r = tap // 9, tap // 3 % 3, tap % 3
        (rho, sb), (gamma, sc) = PLACE[q], PLACE[r]
        top = ((p * 2 + rho) * 2 + gamma) * chans
        block = total[top : top + chans, group(sb)]
        return block if sc == side else pltpu.roll(block, outs, 1)

    left_side = lane_of((chans, LANES)) < outs
    for tap in range(14):
        right = tap_block(tap + 14, 1) if tap + 14 < 27 else jnp.zeros((chans, LANES), F32)
        out[tap * chans : (tap + 1) * chans, :] = jnp.where(left_side, tap_block(tap, 0), right)


def back_kernel(dims, own, count, depth, *refs):
    chans, outs, planes, height, half = dims
    total = count * CHUNKS
    here, refs = refs[:total], refs[total:]
    if depth:
        above, w_next, refs = refs[:total], refs[total], refs[total + 1 :]
    weights, refs = refs[0], refs[1:]
    out, g_here, plane, sem = refs[-5 if depth else -4], refs[-4 if depth else -3], refs[-2], refs[-1]
    gather_grads(here, g_here, own, count)
    if depth:
        g_above = refs[-3]
        gather_grads(above, g_above, own, count)
        w_above = w_next[...]
    matrix = pairing(half, True)
    matrix = jnp.concatenate([matrix, matrix], axis=0)
    w_here = weights[depth * 4 * chans : (depth + 1) * 4 * chans, :]
    for first in range(0, height // 4, STEP):
        hi, lo = grad_shifts(lambda g: g_here[:, group(g)], first, STEP, outs, half)
        grad = jnp.dot(w_here, jnp.concatenate([hi, lo, hi], axis=0), preferred_element_type=F32)
        if depth:
            hi, lo = grad_shifts(lambda g: g_above[:, group(g)], first, STEP, outs, half)
            grad += jnp.dot(w_above, jnp.concatenate([hi, lo, hi], axis=0), preferred_element_type=F32)
        tiles = []
        for parity in range(2):
            for j in range(STEP):
                tops = [(parity * 2 + column) * chans for column in range(2)]
                tiles.append(jnp.concatenate([grad[t : t + chans, group(j)] for t in tops], axis=1))
        hi, lo = split(jnp.concatenate(tiles, axis=0))
        rows = jnp.dot(jnp.concatenate([hi, lo], axis=1), matrix, preferred_element_type=F32)
        for parity in range(2):
            for j in range(STEP):
                start = (parity * STEP + j) * chans
                row = 4 * (first + j) + parity
                for side in range(2):
                    plane[pl.ds(row + 2 * side, chans, stride=height), :] = rows[
                        start : start + chans, group(side)
                    ]
    copies = []
    for i in range(chans):
        source = plane.at[pl.ds(i * height, height), :]
        target = out.at[pl.ds((i * planes + depth) * height, height), :]
        copies.append(pltpu.make_async_copy(source, target, sem.at[i]))
        copies[-1].start()
    for copy in copies:
        copy.wait()


def flat_kernel(half, cube, flat):
    own, cells = flat.shape
    for g in range(cells // LANES):
        sides = [cube[pl.ds(2 * g + side, own, stride=cells // half), :] for side in range(2)]
        flat[:, group(g)] = jnp.concatenate(sides, axis=1)


def activation_kernel(half, *refs):
    *chunks, cube = refs
    own, cells = chunks[0].shape
    for h, chunk in enumerate(chunks):
        for g in range(cells // LANES):
            x = chunk[:, group(g)]
            value = jnp.maximum(x, 0.0) + jnp.log1p(jnp.exp(-jnp.abs(x)))
            row = 2 * (h * (cells // LANES) + g)
            stride = len(chunks) * cells // half
            cube[pl.ds(row, own, stride=stride), :] = value[:, :half]
            cube[pl.ds(row + 1, own, stride=stride), :] = value[:, half:]


def call(kernel, name, time, shapes, scratch, *args, in_place=False):
    specs = [VMEM] * len(args)
    if in_place:
        specs[-1] = ANY
    return pl.pallas_call(
        kernel,
        name=name,
        out_shape=[jax.ShapeDtypeStruct(s, t) for s, t in shapes],
        in_specs=specs,
        out_specs=[ANY if name.startswith("back") else VMEM] * len(shapes),
        scratch_shapes=scratch,
        input_output_aliases={len(args) - 1: 0} if in_place else {},
        cost_estimate=pl.CostEstimate(flops=0, bytes_accessed=int(time * 3.6e6), transcendentals=0),
        compiler_params=pltpu.CompilerParams(vmem_limit_bytes=12 * 1024 * 1024),
    )(*args)


def turned(value, axis, steps):
    count = lax.axis_size(axis)
    return lax.ppermute(value, axis, [(s, (s + steps) % count) for s in range(count)])


def from_behind(value, axis, steps):
    count = lax.axis_size(axis)
    initial, last = (max(0, -steps), min(count, count - steps))
    return lax.ppermute(value, axis, [(source, source + steps) for source in range(initial, last)])


def sum_over(value, axis, beside):
    count = lax.axis_size(axis)
    if count & (count - 1):
        return beside(0, lax.psum(value, axis))
    bit = 1
    while bit < count:
        value = value + lax.ppermute(value, axis, [(s, s ^ bit) for s in range(count)])
        value = beside(bit.bit_length() - 1, value)
        bit *= 2
    return value


def on_device(volume, filters, cotangent):
    real, planes, height, width = volume.shape
    outs = filters.shape[0]
    own = cotangent.shape[0]
    count = lax.axis_size("chan")
    half = width // 2
    cells = (height // 2) * half
    part_cells = cells // CHUNKS
    assert planes == 2 and width == LANES and height % (4 * STEP * CHUNKS) == 0 and 2 * outs == LANES
    chans = -(-real // 16) * 16
    taps = filters.transpose(2, 3, 4, 1, 0)
    if chans > real:
        volume = jnp.pad(volume, ((0, chans - real), (0, 0), (0, 0), (0, 0)))
        taps = jnp.pad(taps, ((0, 0), (0, 0), (0, 0), (0, chans - real), (0, 0)))
    dims = (chans, outs, planes, height, half)
    rows = height // CHUNKS
    halos = [from_behind(volume[:, -1, h * rows : (h + 1) * rows], "space", 1) for h in range(CHUNKS)]
    x_hi, x_lo, part, w_halo, w_back, w_next = call(
        functools.partial(own_kernel, dims),
        "own",
        3.5,
        [
            ((8 * chans, cells), BF16),
            ((8 * chans, cells), BF16),
            ((outs, cells), F32),
            ((4 * outs, 12 * chans), BF16),
            ((8 * chans, 12 * outs), BF16),
            ((4 * chans, 12 * outs), BF16),
        ],
        [pltpu.VMEM((12 * chans, 4 * outs), F32)],
        volume.reshape(chans * planes * height, width),
        taps.reshape(27 * chans, outs),
    )
    (upstream,) = call(
        functools.partial(flat_kernel, half), "flat", 0.8, [((own, cells), F32)], [], cotangent.reshape(-1, half)
    )
    x_halos, preacts, grads, carry = [], [], [], []
    for h in range(CHUNKS):
        shapes = [((4 * chans, part_cells), BF16)] * 2 + [((own, part_cells), F32)] * count
        if h < CHUNKS - 1:
            shapes.append(((outs, LANES), F32))
        xh_hi, xh_lo, *pieces = call(
            functools.partial(halo_kernel, dims, own, count, h),
            "halo",
            1.7,
            shapes,
            [pltpu.VMEM((outs, part_cells), F32)],
            halos[h].reshape(chans * rows, width),
            part,
            w_halo,
            *carry,
        )
        x_halos += [xh_hi, xh_lo]
        carry = pieces[count:]
        preact = pieces[0]
        if h:
            preact, _ = lax.optimization_barrier((preact, grads[-1][0]))
        for k in range(1, count):
            preact = preact + turned(pieces[k], "chan", k)
        grad = upstream[:, h * part_cells : (h + 1) * part_cells] * jax.nn.sigmoid(preact)
        preacts.append(preact)
        grads.append([grad] + [turned(grad, "chan", k) for k in range(1, count)])
    above = [[from_behind(g, "space", -1) for g in chunk] for chunk in grads]
    (activated,) = call(
        functools.partial(activation_kernel, half), "activation", 1.2, [((own * (height // 2), half), F32)], [], *preacts
    )
    grads[0][0], activated = lax.optimization_barrier((grads[0][0], activated))

    summed = []
    for h in range(CHUNKS):
        low = max(h - 1, 0)
        last = h == CHUNKS - 1
        if last:
            early = [g for chunk in above[:-1] for g in chunk] + above[-1][:1]
            *early, summed_before = lax.optimization_barrier((*early, summed[0]))
            above = [early[i * count : (i + 1) * count] for i in range(CHUNKS - 1)] + [early[-1:] + above[-1][1:]]
            summed = [summed_before]
        (result,) = call(
            functools.partial(filter_kernel, dims, own, count, h),
            "filter",
            1.6,
            [((14 * chans, LANES) if last else (12 * chans, 4 * outs), F32)],
            [
                pltpu.VMEM((12 * chans, 4 * outs), F32),
                pltpu.VMEM((outs, (h - low + 1) * part_cells + (LANES if last else 0)), F32),
            ],
            *sum(grads[low : h + 1], []),
            x_hi,
            x_lo,
            *x_halos[2 * low : 2 * h + 2],
            *summed,
        )
        summed = [result]
    buffers = [
        pltpu.VMEM((outs, cells + LANES), F32),
        pltpu.VMEM((chans * height, width), F32),
        pltpu.SemaphoreType.DMA((chans,)),
    ]
    shape = [((chans * planes * height, width), F32)]
    state = {}

    def back_work(index, value):
        if index == 0:
            *late, value = lax.optimization_barrier((*above[-1][1:], value))
            above[-1][1:] = late
            sources = sum(grads, [])
            *sources, value = lax.optimization_barrier((*sources, value))
            state["sources"] = sources
            (state["grad"],) = call(
                functools.partial(back_kernel, dims, own, count, 0), "back_0", 3.0, shape, buffers, *sources, w_back
            )
        elif index == 1:
            state["grad"], value = lax.optimization_barrier((state["grad"], value))
        return value

    packed = sum_over(summed[0], "space", back_work)
    (volume_grad,) = call(
        functools.partial(back_kernel, dims, own, count, 1),
        "back_1",
        4.0,
        shape,
        [buffers[0]] + buffers,
        *state["sources"],
        *sum(above, []),
        w_next,
        w_back,
        state["grad"],
        in_place=True,
    )
    volume_grad = volume_grad.reshape(chans, planes, height, width)[:real]
    depth_all = planes * lax.axis_size("space")
    factor = float(depth_all // 2 * (height // 2) * half) ** (-0.5)
    unpacked = jnp.concatenate([packed[:, :outs], packed[: 13 * chans, outs:]], axis=0) * factor
    filter_grad = unpacked.reshape(3, 3, 3, chans, outs)[:, :, :, :real].transpose(4, 3, 0, 1, 2)
    return (activated.reshape(cotangent.shape), volume_grad, filter_grad)


def solution(mesh):
    in_specs = (
        P("chan", "space", None, None),
        P(None, "chan", None, None, None),
        P("chan", "space", None, None),
    )
    out_specs = (
        P("chan", "space", None, None),
        P("chan", "space", None, None),
        P(None, "chan", None, None, None),
    )
    return jax.shard_map(
        on_device, mesh=mesh, in_specs=in_specs, out_specs=out_specs, check_vma=False
    )
```

time: 109 us -> 68.5 us (0.63)
  waiting for transfers between devices: 30.6 us -> 18.4 us
  local copies, waits for them, and re-layouts: 12.9 us -> 2.45 us
  Pallas kernels: 28.2 us -> 20.5 us
  other arithmetic: 6.68 us -> 0.93 us
  starting transfers between devices: 29.8 us -> 25.1 us
    ppermute x4, starting transfers between devices: 21.6 us -> 7.42 us  [sum_over(): lax.ppermute(value, axis, [(s, s ^ bit) for s in range(count)])]
    ppermute x4, waiting for transfers between devices: 17.7 us -> 4.52 us  [sum_over(): lax.ppermute(value, axis, [(s, s ^ bit) for s in range(count)])]
    ppermute x2 -> x6, starting transfers between devices: 3.85 us -> 12.4 us  [from_behind(): lax.ppermute(value, axis, [(source, source + steps) for source in range(i...]
    pallas_call x5 -> x9, Pallas kernels: 28.2 us -> 20.5 us  [call(): pl.pallas_call(kernel, name=name, out_shape=[jax.ShapeDtypeStruct(s, t) f...]
    unnamed x16 -> x6, local copies, waits for them, and re-layouts: 6.52 us -> 0.94 us
    reshape x2 -> x0, local copies, waits for them, and re-layouts: 4.8 us -> none  [the longest x1 2.43 us: on_device(): activated = jax.nn.softplus(preact).reshape(cotangent.shape)]
    scatter-add x1 -> x0, other arithmetic: 2.64 us -> none  [on_device(): volume_grad.at[:, -1].add(spilled.reshape(chans, height, width))[:real]]
    mul x1 -> x2, other arithmetic: 2.37 us -> 0.16 us  [on_device(): upstream[:, h * part_cells:(h + 1) * part_cells] * jax.nn.sigmoid(preact)]
  transfers between devices with their start and end apart: 8 -> 14, of which waited for: 5 -> 6; matrix products, arithmetic and copies ran while one was open for 6% -> 0% of each run, Pallas kernels for 11% -> 30%
where the time goes in v2:
time: 68.5 us; the launch traced here: 68.2 us
  starting transfers between devices  25.1 us (37%)
  Pallas kernels  20.5 us (30%)
  waiting for transfers between devices  18.4 us (27%)
  local copies, waits for them, and re-layouts  2.45 us (4%)
  other arithmetic  0.93 us (1%)
  between operations  0.87 us (1%)
    pallas_call x9, Pallas kernels, call(): pl.pallas_call(kernel, name=name, out_shape=[jax.ShapeDtypeStruct(s, t) f...  20.5 us
    ppermute x4, waiting for transfers between devices, turned(): lax.ppermute(value, axis, [(s, (s + steps) % count) for s in range(count)])  13.9 us
    ppermute x6, starting transfers between devices, from_behind(): lax.ppermute(value, axis, [(source, source + steps) for source in range(i...  12.4 us
    ppermute x4, starting transfers between devices, sum_over(): lax.ppermute(value, axis, [(s, s ^ bit) for s in range(count)])  7.42 us
    ppermute x4, starting transfers between devices, turned(): lax.ppermute(value, axis, [(s, (s + steps) % count) for s in range(count)])  5.27 us
    ppermute x4, waiting for transfers between devices, sum_over(): lax.ppermute(value, axis, [(s, s ^ bit) for s in range(count)])  4.52 us
    squeeze x1, local copies, waits for them, and re-layouts, on_device(): volume[:, -1, h * rows:(h + 1) * rows]  1.42 us
  transfers between devices with their start and end apart: 14, of which 6 were waited for; matrix products, arithmetic and copies ran while one was open for 0% of the time, Pallas kernels for 30%

profile of v2, /device:TPU:0, one launch (start us, length us, event | category | flops | bytes accessed | tf_op | source)
XLA Modules:
  0.0 68.2 jit_solution(10936693557581300538)
XLA Ops:
  0.6 1.4 %slice_bitcast_fusion = (f32[16,64,128]{2,1,0:T(8,128)S(1)}, f32[16,64,128]{2,1,0:T(8,128)S(1)}) fusion(f32[16,2,128,128]{3,2,1,0:T(8,128)} %param.3), kind=kLoop, calls=%fused_computation | loop fusion | bytes 2097152 | tf_op jit(solution)/shard_map/squeeze | solution.py:357
  2.1 2.5 %collective-permute-start = (f32[16,64,128]{2,1,0:T(8,128)S(1)}, f32[16,64,128]{2,1,0:T(8,128)S(1)}, u32[]{:S(2)}, u32[]{:S(2)}) collective-permute-start(f32[16,64,128]{2,1,0:T(8,128)S(1)} %get-tuple-element.73), channel_id=1, source_target_pairs={{0,2},{2,4},{4,6},{6,8},{8,10},{10,12},{12,14},{14,16},{16,18},{18... | collective-permute-start | bytes 1572872 | tf_op jit(solution)/shard_map/ppermute | solution.py:326
  4.6 4.5 %collective-permute-start.2 = (f32[16,64,128]{2,1,0:T(8,128)S(1)}, f32[16,64,128]{2,1,0:T(8,128)S(1)}, u32[]{:S(2)}, u32[]{:S(2)}) collective-permute-start(f32[16,64,128]{2,1,0:T(8,128)S(1)} %get-tuple-element.72), channel_id=1, source_target_pairs={{0,2},{2,4},{4,6},{6,8},{8,10},{10,12},{12,14},{14,16},{16,18},{18... | collective-permute-start | bytes 1572872 | tf_op jit(solution)/shard_map/ppermute | solution.py:326
  9.2 0.9 %copy-done.2 = f32[64,16,3,3,3]{0,1,4,3,2:T(8,128)S(1)} copy-done((f32[64,16,3,3,3]{0,1,4,3,2:T(8,128)S(1)}, f32[64,16,3,3,3]{0,1,4,3,2:T(8,128)}, u32[]{:S(2)}) %copy-start.2) | copy-done | bytes 110616
  10.1 3.4 %own.1 = (bf16[128,4096]{1,0:T(8,128)(2,1)S(1)}, bf16[128,4096]{1,0:T(8,128)(2,1)S(1)}, f32[64,4096]{1,0:T(8,128)S(1)}, bf16[256,192]{1,0:T(8,128)(2,1)S(1)}, bf...) custom-call(f32[4096,128]{1,0:T(8,128)S(1)} %bitcast.19, f32[432,64]{1,0:T(8,128)S(1)} %bitcast.23), custom_call_target="tpu_custom_call" | custom-call | bytes 12600000 | tf_op jit(solution)/shard_map/own/pallas_call | solution.py:305
  13.6 1.3 %halo.2 = (bf16[64,2048]{1,0:T(8,128)(2,1)S(1)}, bf16[64,2048]{1,0:T(8,128)(2,1)S(1)}, f32[32,2048]{1,0:T(8,128)S(1)}, f32[32,2048]{1,0:T(8,128)S(1)}, f32[64,128]{1,0:T(8,128)S(1)}) custom-call(f32[1024,128]{1,0:T(8,128)S(1)} %bitcast.22, f32[64,4096]{1,0:T(8,128)S(1)} %get-tuple-element.34.refs_1_, bf16[256,192]{1,0:T(8,128)(2,1)S(1)} %get-tuple-element.35.refs_2_), custom_call_target="tpu_custom_call" | custom-call | bytes 6120000 | tf_op jit(solution)/shard_map/halo/pallas_call | solution.py:305
  14.9 1.6 %collective-permute-start.1 = (f32[32,2048]{1,0:T(8,128)S(1)}, f32[32,2048]{1,0:T(8,128)S(1)}, u32[]{:S(2)}, u32[]{:S(2)}) collective-permute-start(f32[32,2048]{1,0:T(8,128)S(1)} %get-tuple-element.37), channel_id=1, source_target_pairs={{0,1},{1,0},{2,3},{3,2},{4,5},{5,4},{6,7},{7,6},{8,9},{9,8},{10,11... | collective-permute-start | bytes 786440 | tf_op jit(solution)/shard_map/ppermute | solution.py:320
  16.5 0.6 flat.1
  17.1 1.3 %halo.3 = (bf16[64,2048]{1,0:T(8,128)(2,1)S(1)}, bf16[64,2048]{1,0:T(8,128)(2,1)S(1)}, f32[32,2048]{1,0:T(8,128)S(1)}, f32[32,2048]{1,0:T(8,128)S(1)}) custom-call(f32[1024,128]{1,0:T(8,128)S(1)} %bitcast.21, f32[64,4096]{1,0:T(8,128)S(1)} %get-tuple-element.34.refs_1_, bf16[256,192]{1,0:T(8,128)(2,1)S(1)} %get-tuple-element.35.refs_2_, ...), custom_call_target="tpu_custom_call" | custom-call | bytes 6120000 | tf_op jit(solution)/shard_map/halo/pallas_call | solution.py:305
  18.4 0.6 collective-permute-start.3
  19.0 4.3 %collective-permute-done.1 = f32[32,2048]{1,0:T(8,128)S(1)} collective-permute-done((f32[32,2048]{1,0:T(8,128)S(1)}, f32[32,2048]{1,0:T(8,128)S(1)}, u32[]{:S(2)}, u32[]{:S(2)}) %collective-permute-start.1) | collective-permute-done | bytes 262176 | tf_op jit(solution)/shard_map/ppermute | solution.py:320
  23.4 1.6 %collective-permute-start.4 = (f32[32,2048]{1,0:T(8,128)S(1)}, f32[32,2048]{1,0:T(8,128)S(1)}, u32[]{:S(2)}, u32[]{:S(2)}) collective-permute-start(f32[32,2048]{1,0:T(8,128)S(1)} %get-tuple-element.52.refs_0_), channel_id=1, source_target_pairs={{0,1},{1,0},{2,3},{3,2},{4,5},{5,4},{6,7},{7,6},{8,9},{9,8},{10,11... | collective-permute-start | bytes 786440 | tf_op jit(solution)/shard_map/ppermute | solution.py:320
  25.0 4.0 %collective-permute-done.3 = f32[32,2048]{1,0:T(8,128)S(1)} collective-permute-done((f32[32,2048]{1,0:T(8,128)S(1)}, f32[32,2048]{1,0:T(8,128)S(1)}, u32[]{:S(2)}, u32[]{:S(2)}) %collective-permute-start.3) | collective-permute-done | bytes 262176 | tf_op jit(solution)/shard_map/ppermute | solution.py:320
  29.0 1.6 %collective-permute-start.5 = (f32[32,2048]{1,0:T(8,128)S(1)}, f32[32,2048]{1,0:T(8,128)S(1)}, u32[]{:S(2)}, u32[]{:S(2)}) collective-permute-start(f32[32,2048]{1,0:T(8,128)S(1)} %get-tuple-element.54.refs_2_), channel_id=1, source_target_pairs={{0,1},{1,0},{2,3},{3,2},{4,5},{5,4},{6,7},{7,6},{8,9},{9,8},{10,11... | collective-permute-start | bytes 786440 | tf_op jit(solution)/shard_map/ppermute | solution.py:320
  30.6 1.3 %collective-permute-start.7 = (f32[32,2048]{1,0:T(8,128)S(1)}, f32[32,2048]{1,0:T(8,128)S(1)}, u32[]{:S(2)}, u32[]{:S(2)}) collective-permute-start(f32[32,2048]{1,0:T(8,128)S(1)} %get-tuple-element.52.refs_0_), channel_id=1, source_target_pairs={{2,0},{4,2},{6,4},{8,6},{10,8},{12,10},{14,12},{16,14},{18,16},{20... | collective-permute-start | bytes 786440 | tf_op jit(solution)/shard_map/ppermute | solution.py:326
  31.9 1.3 %collective-permute-start.9 = (f32[32,2048]{1,0:T(8,128)S(1)}, f32[32,2048]{1,0:T(8,128)S(1)}, u32[]{:S(2)}, u32[]{:S(2)}) collective-permute-start(f32[32,2048]{1,0:T(8,128)S(1)} %get-tuple-element.54.refs_2_), channel_id=1, source_target_pairs={{2,0},{4,2},{6,4},{8,6},{10,8},{12,10},{14,12},{16,14},{18,16},{20... | collective-permute-start | bytes 786440 | tf_op jit(solution)/shard_map/ppermute | solution.py:326
  33.2 1.4 %collective-permute-done.4.refs_1_ = f32[32,2048]{1,0:T(8,128)S(1)} collective-permute-done((f32[32,2048]{1,0:T(8,128)S(1)}, f32[32,2048]{1,0:T(8,128)S(1)}, u32[]{:S(2)}, u32[]{:S(2)}) %collective-permute-start.4) | collective-permute-done | bytes 262176 | tf_op jit(solution)/shard_map/ppermute | solution.py:320
  34.6 1.3 %collective-permute-start.8 = (f32[32,2048]{1,0:T(8,128)S(1)}, f32[32,2048]{1,0:T(8,128)S(1)}, u32[]{:S(2)}, u32[]{:S(2)}) collective-permute-start(f32[32,2048]{1,0:T(8,128)S(1)} %collective-permute-done.4.refs_1_), channel_id=1, source_target_pairs={{2,0},{4,2},{6,4},{8,6},{10,8},{12,10},{14,12},{16,14},{18,16},{20... | collective-permute-start | bytes 786440 | tf_op jit(solution)/shard_map/ppermute | solution.py:326
  35.9 4.2 %collective-permute-done.5.refs_3_ = f32[32,2048]{1,0:T(8,128)S(1)} collective-permute-done((f32[32,2048]{1,0:T(8,128)S(1)}, f32[32,2048]{1,0:T(8,128)S(1)}, u32[]{:S(2)}, u32[]{:S(2)}) %collective-permute-start.5) | collective-permute-done | bytes 262176 | tf_op jit(solution)/shard_map/ppermute | solution.py:320
  40.0 1.5 %collective-permute-start.6 = (f32[32,2048]{1,0:T(8,128)S(1)}, f32[32,2048]{1,0:T(8,128)S(1)}, u32[]{:S(2)}, u32[]{:S(2)}) collective-permute-start(f32[32,2048]{1,0:T(8,128)S(1)} %collective-permute-done.5.refs_3_), channel_id=1, source_target_pairs={{2,0},{4,2},{6,4},{8,6},{10,8},{12,10},{14,12},{16,14},{18,16},{20... | collective-permute-start | bytes 786440 | tf_op jit(solution)/shard_map/ppermute | solution.py:326
  41.5 2.0 %activation.1 = f32[2048,64]{1,0:T(8,128)} custom-call(f32[32,2048]{1,0:T(8,128)S(1)} %get-tuple-element.71.refs_0_, f32[32,2048]{1,0:T(8,128)S(1)} %get-tuple-element.69.refs_1_), custom_call_target="tpu_custom_call" | custom-call | bytes 4320000 | tf_op jit(solution)/shard_map/activation/pallas_call | solution.py:305
  43.5 1.4 %filter.2.refs_10_ = f32[192,256]{1,0:T(8,128)S(1)} custom-call(f32[32,2048]{1,0:T(8,128)S(1)} %get-tuple-element.52.refs_0_, f32[32,2048]{1,0:T(8,128)S(1)} %collective-permute-done.4.refs_1_, bf16[128,4096]{1,0:T(8,128)(2,1)S(1)} %get-tuple-element.44.refs_2_.refs_4_, bf16[128,4096]{1,0:T(8,128)(2,1)S(1)} %get-tuple-element.45.refs_3_.refs_5_, ...), custom_call_target="tpu_custom_call" | custom-call | bytes 5760000 | tf_op jit(solution)/shard_map/filter/pallas_call | solution.py:305
  44.9 1.6 %filter.3 = f32[224,128]{1,0:T(8,128)S(1)} custom-call(f32[32,2048]{1,0:T(8,128)S(1)} %get-tuple-element.52.refs_0_, f32[32,2048]{1,0:T(8,128)S(1)} %collective-permute-done.4.refs_1_, f32[32,2048]{1,0:T(8,128)S(1)} %get-tuple-element.54.refs_2_, f32[32,2048]{1,0:T(8,128)S(1)} %collective-permute-done.5.refs_3_, ...), custom_call_target="tpu_custom_call" | custom-call | bytes 5760000 | tf_op jit(solution)/shard_map/filter/pallas_call | solution.py:305
  46.5 1.2 %collective-permute-start.10 = (f32[224,128]{1,0:T(8,128)S(1)}, f32[224,128]{1,0:T(8,128)S(1)}, u32[]{:S(2)}, u32[]{:S(2)}) collective-permute-start(f32[224,128]{1,0:T(8,128)S(1)} %filter.3), channel_id=1, source_target_pairs={{0,2},{2,0},{4,6},{6,4},{8,10},{10,8},{12,14},{14,12},{16,18},{18,... | collective-permute-start | bytes 344072 | tf_op jit(solution)/shard_map/ppermute | solution.py:335
  47.7 1.0 %collective-permute-done.10 = f32[224,128]{1,0:T(8,128)S(1)} collective-permute-done((f32[224,128]{1,0:T(8,128)S(1)}, f32[224,128]{1,0:T(8,128)S(1)}, u32[]{:S(2)}, u32[]{:S(2)}) %collective-permute-start.10) | collective-permute-done | bytes 114720 | tf_op jit(solution)/shard_map/ppermute | solution.py:335
  48.7 1.7 %collective-permute-start.11 = (f32[224,128]{1,0:T(8,128)S(1)}, f32[224,128]{1,0:T(8,128)S(1)}, u32[]{:S(2)}, u32[]{:S(2)}) collective-permute-start(f32[224,128]{1,0:T(8,128)S(1)} %add.28), channel_id=1, source_target_pairs={{0,4},{2,6},{4,0},{6,2},{8,12},{10,14},{12,8},{14,10},{16,20},{18,... | collective-permute-start | bytes 344072 | tf_op jit(solution)/shard_map/ppermute | solution.py:335
  50.5 3.7 %back_0.1.refs_10_ = f32[4096,128]{1,0:T(8,128)} custom-call(f32[32,2048]{1,0:T(8,128)S(1)} %get-tuple-element.52.refs_0_, f32[32,2048]{1,0:T(8,128)S(1)} %collective-permute-done.4.refs_1_, f32[32,2048]{1,0:T(8,128)S(1)} %get-tuple-element.54.refs_2_, f32[32,2048]{1,0:T(8,128)S(1)} %collective-permute-done.5.refs_3_, ...), custom_call_target="tpu_custom_call" | custom-call | bytes 10800000 | tf_op jit(solution)/shard_map/back_0/pallas_call | solution.py:305
  54.2 1.6 %collective-permute-start.12 = (f32[224,128]{1,0:T(8,128)S(1)}, f32[224,128]{1,0:T(8,128)S(1)}, u32[]{:S(2)}, u32[]{:S(2)}) collective-permute-start(f32[224,128]{1,0:T(8,128)S(1)} %add.29), channel_id=1, source_target_pairs={{0,8},{2,10},{4,12},{6,14},{8,0},{10,2},{12,4},{14,6},{16,24},{18,... | collective-permute-start | bytes 344072 | tf_op jit(solution)/shard_map/ppermute | solution.py:335
  55.9 3.5 %collective-permute-done.12 = f32[224,128]{1,0:T(8,128)S(1)} collective-permute-done((f32[224,128]{1,0:T(8,128)S(1)}, f32[224,128]{1,0:T(8,128)S(1)}, u32[]{:S(2)}, u32[]{:S(2)}) %collective-permute-start.12) | collective-permute-done | bytes 114720 | tf_op jit(solution)/shard_map/ppermute | solution.py:335
  59.4 2.8 %collective-permute-start.13 = (f32[224,128]{1,0:T(8,128)S(1)}, f32[224,128]{1,0:T(8,128)S(1)}, u32[]{:S(2)}, u32[]{:S(2)}) collective-permute-start(f32[224,128]{1,0:T(8,128)S(1)} %add.30), channel_id=1, source_target_pairs={{0,16},{2,18},{4,20},{6,22},{8,24},{10,26},{12,28},{14,30},{16,0},... | collective-permute-start | bytes 344072 | tf_op jit(solution)/shard_map/ppermute | solution.py:335
  62.3 5.1 %back_1.1 = f32[4096,128]{1,0:T(8,128)} custom-call(f32[32,2048]{1,0:T(8,128)S(1)} %get-tuple-element.52.refs_0_, f32[32,2048]{1,0:T(8,128)S(1)} %collective-permute-done.4.refs_1_, f32[32,2048]{1,0:T(8,128)S(1)} %get-tuple-element.54.refs_2_, f32[32,2048]{1,0:T(8,128)S(1)} %collective-permute-done.5.refs_3_, ...), custom_call_target="tpu_custom_call", output_to_operand_aliasing={{}: (10, {})} | custom-call | bytes 14400000 | tf_op jit(solution)/shard_map/back_1/pallas_call | solution.py:305
  67.5 0.7 %maximum_multiply_fusion = f32[432,64]{1,0:T(8,128)} fusion(f32[208,64]{1,0:T(8,128)S(1)} %slice.27, f32[224,64]{1,0:T(8,128)S(1)} %bitcast.26), kind=kLoop, calls=%fused_computation.4 | loop fusion | flops 55296 | bytes 221184 | tf_op jit(solution)/shard_map/mul | solution.py:473
  (20 shorter events, 0.4 us)
Async XLA Ops:
  0.6 8.5 %copy-start = (f32[16,2,128,128]{3,2,1,0:T(8,128)S(1)}, f32[16,2,128,128]{3,2,1,0:T(8,128)}, u32[]{:S(2)}) copy-start(f32[16,2,128,128]{3,2,1,0:T(8,128)} %param.3) | copy-start | bytes 6291460
  2.1 14.4 %copy-start.1 = (f32[32,1,64,64]{3,2,1,0:T(8,128)S(1)}, f32[32,1,64,64]{3,2,1,0:T(8,128)}, u32[]{:S(2)}) copy-start(f32[32,1,64,64]{3,2,1,0:T(8,128)} %param.5) | copy-start | bytes 1572868
  2.1 11.5 %collective-permute-start = (f32[16,64,128]{2,1,0:T(8,128)S(1)}, f32[16,64,128]{2,1,0:T(8,128)S(1)}, u32[]{:S(2)}, u32[]{:S(2)}) collective-permute-start(f32[16,64,128]{2,1,0:T(8,128)S(1)} %get-tuple-element.73), channel_id=1, source_target_pairs={{0,2},{2,4},{4,6},{6,8},{8,10},{10,12},{12,14},{14,16},{16,18},{18... | collective-permute-start | bytes 1572872 | tf_op jit(solution)/shard_map/ppermute | solution.py:326
  4.6 12.5 %collective-permute-start.2 = (f32[16,64,128]{2,1,0:T(8,128)S(1)}, f32[16,64,128]{2,1,0:T(8,128)S(1)}, u32[]{:S(2)}, u32[]{:S(2)}) collective-permute-start(f32[16,64,128]{2,1,0:T(8,128)S(1)} %get-tuple-element.72), channel_id=1, source_target_pairs={{0,2},{2,4},{4,6},{6,8},{8,10},{10,12},{12,14},{14,16},{16,18},{18... | collective-permute-start | bytes 1572872 | tf_op jit(solution)/shard_map/ppermute | solution.py:326
  9.2 0.9 %copy-start.2 = (f32[64,16,3,3,3]{0,1,4,3,2:T(8,128)S(1)}, f32[64,16,3,3,3]{0,1,4,3,2:T(8,128)}, u32[]{:S(2)}) copy-start(f32[64,16,3,3,3]{0,1,4,3,2:T(8,128)} %param.4) | copy-start | bytes 331780
  14.9 8.4 %collective-permute-start.1 = (f32[32,2048]{1,0:T(8,128)S(1)}, f32[32,2048]{1,0:T(8,128)S(1)}, u32[]{:S(2)}, u32[]{:S(2)}) collective-permute-start(f32[32,2048]{1,0:T(8,128)S(1)} %get-tuple-element.37), channel_id=1, source_target_pairs={{0,1},{1,0},{2,3},{3,2},{4,5},{5,4},{6,7},{7,6},{8,9},{9,8},{10,11... | collective-permute-start | bytes 786440 | tf_op jit(solution)/shard_map/ppermute | solution.py:320
  18.4 10.5 %collective-permute-start.3 = (f32[32,2048]{1,0:T(8,128)S(1)}, f32[32,2048]{1,0:T(8,128)S(1)}, u32[]{:S(2)}, u32[]{:S(2)}) collective-permute-start(f32[32,2048]{1,0:T(8,128)S(1)} %get-tuple-element.41), channel_id=1, source_target_pairs={{0,1},{1,0},{2,3},{3,2},{4,5},{5,4},{6,7},{7,6},{8,9},{9,8},{10,11... | collective-permute-start | bytes 786440 | tf_op jit(solution)/shard_map/ppermute | solution.py:320
  23.4 11.2 %collective-permute-start.4 = (f32[32,2048]{1,0:T(8,128)S(1)}, f32[32,2048]{1,0:T(8,128)S(1)}, u32[]{:S(2)}, u32[]{:S(2)}) collective-permute-start(f32[32,2048]{1,0:T(8,128)S(1)} %get-tuple-element.52.refs_0_), channel_id=1, source_target_pairs={{0,1},{1,0},{2,3},{3,2},{4,5},{5,4},{6,7},{7,6},{8,9},{9,8},{10,11... | collective-permute-start | bytes 786440 | tf_op jit(solution)/shard_map/ppermute | solution.py:320
  29.0 11.0 %collective-permute-start.5 = (f32[32,2048]{1,0:T(8,128)S(1)}, f32[32,2048]{1,0:T(8,128)S(1)}, u32[]{:S(2)}, u32[]{:S(2)}) collective-permute-start(f32[32,2048]{1,0:T(8,128)S(1)} %get-tuple-element.54.refs_2_), channel_id=1, source_target_pairs={{0,1},{1,0},{2,3},{3,2},{4,5},{5,4},{6,7},{7,6},{8,9},{9,8},{10,11... | collective-permute-start | bytes 786440 | tf_op jit(solution)/shard_map/ppermute | solution.py:320
  30.6 14.3 %collective-permute-start.7 = (f32[32,2048]{1,0:T(8,128)S(1)}, f32[32,2048]{1,0:T(8,128)S(1)}, u32[]{:S(2)}, u32[]{:S(2)}) collective-permute-start(f32[32,2048]{1,0:T(8,128)S(1)} %get-tuple-element.52.refs_0_), channel_id=1, source_target_pairs={{2,0},{4,2},{6,4},{8,6},{10,8},{12,10},{14,12},{16,14},{18,16},{20... | collective-permute-start | bytes 786440 | tf_op jit(solution)/shard_map/ppermute | solution.py:326
  31.9 13.0 %collective-permute-start.9 = (f32[32,2048]{1,0:T(8,128)S(1)}, f32[32,2048]{1,0:T(8,128)S(1)}, u32[]{:S(2)}, u32[]{:S(2)}) collective-permute-start(f32[32,2048]{1,0:T(8,128)S(1)} %get-tuple-element.54.refs_2_), channel_id=1, source_target_pairs={{2,0},{4,2},{6,4},{8,6},{10,8},{12,10},{14,12},{16,14},{18,16},{20... | collective-permute-start | bytes 786440 | tf_op jit(solution)/shard_map/ppermute | solution.py:326
  34.6 10.3 %collective-permute-start.8 = (f32[32,2048]{1,0:T(8,128)S(1)}, f32[32,2048]{1,0:T(8,128)S(1)}, u32[]{:S(2)}, u32[]{:S(2)}) collective-permute-start(f32[32,2048]{1,0:T(8,128)S(1)} %collective-permute-done.4.refs_1_), channel_id=1, source_target_pairs={{2,0},{4,2},{6,4},{8,6},{10,8},{12,10},{14,12},{16,14},{18,16},{20... | collective-permute-start | bytes 786440 | tf_op jit(solution)/shard_map/ppermute | solution.py:326
  40.0 8.7 %collective-permute-start.6 = (f32[32,2048]{1,0:T(8,128)S(1)}, f32[32,2048]{1,0:T(8,128)S(1)}, u32[]{:S(2)}, u32[]{:S(2)}) collective-permute-start(f32[32,2048]{1,0:T(8,128)S(1)} %collective-permute-done.5.refs_3_), channel_id=1, source_target_pairs={{2,0},{4,2},{6,4},{8,6},{10,8},{12,10},{14,12},{16,14},{18,16},{20... | collective-permute-start | bytes 786440 | tf_op jit(solution)/shard_map/ppermute | solution.py:326
  46.5 2.2 %collective-permute-start.10 = (f32[224,128]{1,0:T(8,128)S(1)}, f32[224,128]{1,0:T(8,128)S(1)}, u32[]{:S(2)}, u32[]{:S(2)}) collective-permute-start(f32[224,128]{1,0:T(8,128)S(1)} %filter.3), channel_id=1, source_target_pairs={{0,2},{2,0},{4,6},{6,4},{8,10},{10,8},{12,14},{14,12},{16,18},{18,... | collective-permute-start | bytes 344072 | tf_op jit(solution)/shard_map/ppermute | solution.py:335
  48.7 5.5 %collective-permute-start.11 = (f32[224,128]{1,0:T(8,128)S(1)}, f32[224,128]{1,0:T(8,128)S(1)}, u32[]{:S(2)}, u32[]{:S(2)}) collective-permute-start(f32[224,128]{1,0:T(8,128)S(1)} %add.28), channel_id=1, source_target_pairs={{0,4},{2,6},{4,0},{6,2},{8,12},{10,14},{12,8},{14,10},{16,20},{18,... | collective-permute-start | bytes 344072 | tf_op jit(solution)/shard_map/ppermute | solution.py:335
  54.2 5.2 %collective-permute-start.12 = (f32[224,128]{1,0:T(8,128)S(1)}, f32[224,128]{1,0:T(8,128)S(1)}, u32[]{:S(2)}, u32[]{:S(2)}) collective-permute-start(f32[224,128]{1,0:T(8,128)S(1)} %add.29), channel_id=1, source_target_pairs={{0,8},{2,10},{4,12},{6,14},{8,0},{10,2},{12,4},{14,6},{16,24},{18,... | collective-permute-start | bytes 344072 | tf_op jit(solution)/shard_map/ppermute | solution.py:335
  59.4 7.9 %collective-permute-start.13 = (f32[224,128]{1,0:T(8,128)S(1)}, f32[224,128]{1,0:T(8,128)S(1)}, u32[]{:S(2)}, u32[]{:S(2)}) collective-permute-start(f32[224,128]{1,0:T(8,128)S(1)} %add.30), channel_id=1, source_target_pairs={{0,16},{2,18},{4,20},{6,22},{8,24},{10,26},{12,28},{14,30},{16,0},... | collective-permute-start | bytes 344072 | tf_op jit(solution)/shard_map/ppermute | solution.py:335

commit v3 on v2

--- a/solution.py
+++ b/solution.py
@@ -12,6 +12,7 @@
 LANES = 128
 STEP = 8
 CHUNKS = 2
+BACK = (10, 22)
 VMEM = pl.BlockSpec(memory_space=pltpu.VMEM)
 ANY = pl.BlockSpec(memory_space=pl.ANY)
 
@@ -112,7 +113,34 @@
         scratch[:, left:] = jnp.zeros((scratch.shape[0], scratch.shape[1] - left), F32)
 
 
-def own_kernel(dims, vol, filt, x_hi, x_lo, part, w_halo, w_back, w_next, w_t):
+def own_kernel(dims, chunk, vol, *refs):
+    chans, outs, planes, height, half = dims
+    rows = height // CHUNKS
+    if chunk:
+        w_own, before = refs[:2]
+        x_hi, x_lo, part, *rest = refs[2:]
+        carry, weights = before[...], w_own[...]
+        after = rest[0] if rest else None
+    else:
+        filt, x_hi, x_lo, part, w_own, w_halo, w_back, after, w_t = refs
+        carry, weights = jnp.zeros((outs, LANES), F32), lay_weights(dims, filt, w_t, w_own, w_halo, w_back)
+    matrix = pairing(half, False)
+
+    def load(plane, row):
+        return vol[pl.ds(plane * height + chunk * rows + row, chans, stride=planes * height), :]
+
+    for first in range(0, rows // 4, STEP):
+        hi, lo = parity_split(load, planes, first, matrix)
+        cells = group(first, STEP)
+        x_hi[:, cells] = hi
+        x_lo[:, cells] = lo
+        y = jnp.dot(weights, jnp.concatenate([hi, lo, hi], axis=0), preferred_element_type=F32)
+        part[:, cells], carry = shift_add(y, outs, half, carry)
+    if after is not None:
+        after[...] = carry
+
+
+def lay_weights(dims, filt, w_t, w_own, w_halo, w_back):
     chans, outs, planes, height, half = dims
     w_t[...] = jnp.zeros_like(w_t)
     for p in range(3):
@@ -125,24 +153,15 @@
                 w_t[top : top + chans, left : left + outs] = filt[tap * chans : (tap + 1) * chans, :]
     edge = 4 * chans
     hi, lo = split(w_t[...])
-    w_next[...] = jnp.concatenate([hi[:edge], hi[:edge], lo[:edge]], axis=1)
-    w_back[...] = jnp.concatenate([hi[edge:], hi[edge:], lo[edge:]], axis=1)
+    here = jnp.concatenate([hi[edge:], hi[edge:], lo[edge:]], axis=1)
+    above = jnp.concatenate([hi[:edge], hi[:edge], lo[:edge]], axis=1)
+    w_back[...] = jnp.concatenate([here, jnp.concatenate([jnp.zeros_like(above), above], axis=0)], axis=1)
     hi, lo = hi.astype(F32), lo.astype(F32)
     w_halo[...] = jnp.concatenate([hi[:edge], hi[:edge], lo[:edge]], axis=0).T.astype(BF16)
-    w_own = jnp.concatenate([hi[edge:], hi[edge:], lo[edge:]], axis=0).T.astype(BF16)
-    matrix = pairing(half, False)
-
-    def load(plane, row):
-        return vol[pl.ds(plane * height + row, chans, stride=planes * height), :]
-
-    carry = jnp.zeros((outs, LANES), F32)
-    for first in range(0, height // 4, STEP):
-        hi, lo = parity_split(load, planes, first, matrix)
-        cells = group(first, STEP)
-        x_hi[:, cells] = hi
-        x_lo[:, cells] = lo
-        y = jnp.dot(w_own, jnp.concatenate([hi, lo, hi], axis=0), preferred_element_type=F32)
-        part[:, cells], carry = shift_add(y, outs, half, carry)
+    hi, lo = split(w_t[edge:, :].T)
+    weights = jnp.concatenate([hi, hi, lo], axis=1)
+    w_own[...] = weights
+    return weights
 
 
 def halo_kernel(dims, own, count, chunk, *refs):
@@ -166,7 +185,7 @@
         x_lo[:, cells] = lo
         y = jnp.dot(weights, jnp.concatenate([hi, lo, hi], axis=0), preferred_element_type=F32)
         added, carry = shift_add(y, outs, half, carry)
-        total[:, cells] = part[:, group(chunk * (rows // 4) + first, STEP)] + added
+        total[:, cells] = part[:, cells] + added
     if after is not None:
         after[...] = carry
     me = lax.axis_index("chan")
@@ -181,7 +200,7 @@
     loaded = min(chunk, 1) + 1
     last = chunk == CHUNKS - 1
     pieces, refs = refs[: loaded * count], refs[loaded * count :]
-    (x_hi, x_lo), refs = refs[:2], refs[2:]
+    planes_x, refs = refs[: 2 * loaded], refs[2 * loaded :]
     halos, refs = refs[: 2 * loaded], refs[2 * loaded :]
     if chunk:
         before, refs = refs[0], refs[1:]
@@ -192,21 +211,22 @@
     end = (chunk + 1) * per - (0 if last else 1)
     total[...] = before[...] if chunk else jnp.zeros_like(total)
 
-    def halo_part(part, first, size):
+    def cells_of(sources, part, first, size):
         found = []
         for h in range(loaded):
             low = max(first - base, h * per)
             high = min(first - base + size, (h + 1) * per)
             if low < high:
-                found.append(halos[2 * h + part][:, group(low - h * per, high - low)])
+                found.append(sources[2 * h + part][:, group(low - h * per, high - low)])
         return found[0] if len(found) == 1 else jnp.concatenate(found, axis=1)
 
     first = begin
     while first < end:
         size = min(STEP, end - first)
         hi, lo = grad_shifts(lambda g: g_all[:, group(g - base)], first, size, outs, half)
-        a_hi = jnp.concatenate([halo_part(0, first, size), x_hi[:, group(first, size)]], axis=0)
-        a_lo = jnp.concatenate([halo_part(1, first, size), x_lo[:, group(first, size)]], axis=0)
+        a_hi, a_lo = [
+            jnp.concatenate([cells_of(v, part, first, size) for v in (halos, planes_x)], axis=0) for part in range(2)
+        ]
         total[...] += lax.dot_general(
             jnp.concatenate([a_hi, a_hi, a_lo], axis=1),
             jnp.concatenate([hi, lo, hi], axis=1),
@@ -231,48 +251,47 @@
         out[tap * chans : (tap + 1) * chans, :] = jnp.where(left_side, tap_block(tap, 0), right)
 
 
-def back_kernel(dims, own, count, depth, *refs):
+def back_kernel(dims, own, count, begin, end, low, high, *refs):
     chans, outs, planes, height, half = dims
-    total = count * CHUNKS
-    here, refs = refs[:total], refs[total:]
-    if depth:
-        above, w_next, refs = refs[:total], refs[total], refs[total + 1 :]
-    weights, refs = refs[0], refs[1:]
-    out, g_here, plane, sem = refs[-5 if depth else -4], refs[-4 if depth else -3], refs[-2], refs[-1]
+    loaded = high - low
+    here, above = refs[: loaded * count], refs[loaded * count : 2 * loaded * count]
+    weights = refs[2 * loaded * count][...]
+    out, g_here, g_above, grown, sem = refs[-5:]
     gather_grads(here, g_here, own, count)
-    if depth:
-        g_above = refs[-3]
-        gather_grads(above, g_above, own, count)
-        w_above = w_next[...]
+    gather_grads(above, g_above, own, count)
+    base = low * (height // 4 // CHUNKS)
     matrix = pairing(half, True)
     matrix = jnp.concatenate([matrix, matrix], axis=0)
-    w_here = weights[depth * 4 * chans : (depth + 1) * 4 * chans, :]
-    for first in range(0, height // 4, STEP):
-        hi, lo = grad_shifts(lambda g: g_here[:, group(g)], first, STEP, outs, half)
-        grad = jnp.dot(w_here, jnp.concatenate([hi, lo, hi], axis=0), preferred_element_type=F32)
-        if depth:
-            hi, lo = grad_shifts(lambda g: g_above[:, group(g)], first, STEP, outs, half)
-            grad += jnp.dot(w_above, jnp.concatenate([hi, lo, hi], axis=0), preferred_element_type=F32)
+    first = begin
+    while first < end:
+        size = min(STEP, end - first)
+        hi, lo = grad_shifts(lambda g: g_here[:, group(g - base)], first, size, outs, half)
+        hi_above, lo_above = grad_shifts(lambda g: g_above[:, group(g - base)], first, size, outs, half)
+        grad = jnp.dot(
+            weights,
+            jnp.concatenate([hi, lo, hi, hi_above, lo_above, hi_above], axis=0),
+            preferred_element_type=F32,
+        )
         tiles = []
-        for parity in range(2):
-            for j in range(STEP):
+        for parity in range(planes * 2):
+            for j in range(size):
                 tops = [(parity * 2 + column) * chans for column in range(2)]
                 tiles.append(jnp.concatenate([grad[t : t + chans, group(j)] for t in tops], axis=1))
         hi, lo = split(jnp.concatenate(tiles, axis=0))
         rows = jnp.dot(jnp.concatenate([hi, lo], axis=1), matrix, preferred_element_type=F32)
-        for parity in range(2):
-            for j in range(STEP):
-                start = (parity * STEP + j) * chans
-                row = 4 * (first + j) + parity
+        for parity in range(planes * 2):
+            for j in range(size):
+                start = (parity * size + j) * chans
+                row = (parity // 2) * height + 4 * (first + j) + parity % 2
                 for side in range(2):
-                    plane[pl.ds(row + 2 * side, chans, stride=height), :] = rows[
+                    grown[pl.ds(row + 2 * side, chans, stride=planes * height), :] = rows[
                         start : start + chans, group(side)
                     ]
+        first += size
     copies = []
-    for i in range(chans):
-        source = plane.at[pl.ds(i * height, height), :]
-        target = out.at[pl.ds((i * planes + depth) * height, height), :]
-        copies.append(pltpu.make_async_copy(source, target, sem.at[i]))
+    for i in range(chans * planes):
+        part = pl.ds(i * height + 4 * begin, 4 * (end - begin))
+        copies.append(pltpu.make_async_copy(grown.at[part, :], out.at[part, :], sem.at[i]))
         copies[-1].start()
     for copy in copies:
         copy.wait()
@@ -285,17 +304,22 @@
         flat[:, group(g)] = jnp.concatenate(sides, axis=1)
 
 
-def activation_kernel(half, *refs):
-    *chunks, cube = refs
-    own, cells = chunks[0].shape
-    for h, chunk in enumerate(chunks):
-        for g in range(cells // LANES):
-            x = chunk[:, group(g)]
-            value = jnp.maximum(x, 0.0) + jnp.log1p(jnp.exp(-jnp.abs(x)))
-            row = 2 * (h * (cells // LANES) + g)
-            stride = len(chunks) * cells // half
-            cube[pl.ds(row, own, stride=stride), :] = value[:, :half]
-            cube[pl.ds(row + 1, own, stride=stride), :] = value[:, half:]
+def activation_kernel(half, h, chunk, *refs):
+    out, cube, sem = refs[-3:]
+    own, cells = chunk.shape
+    rows = cells // half
+    for g in range(cells // LANES):
+        x = chunk[:, group(g)]
+        value = jnp.maximum(x, 0.0) + jnp.log1p(jnp.exp(-jnp.abs(x)))
+        cube[pl.ds(2 * g, own, stride=rows), :] = value[:, :half]
+        cube[pl.ds(2 * g + 1, own, stride=rows), :] = value[:, half:]
+    copies = []
+    for i in range(own):
+        target = out.at[pl.ds((i * CHUNKS + h) * rows, rows), :]
+        copies.append(pltpu.make_async_copy(cube.at[pl.ds(i * rows, rows), :], target, sem.at[i]))
+        copies[-1].start()
+    for copy in copies:
+        copy.wait()
 
 
 def call(kernel, name, time, shapes, scratch, *args, in_place=False):
@@ -307,10 +331,10 @@
         name=name,
         out_shape=[jax.ShapeDtypeStruct(s, t) for s, t in shapes],
         in_specs=specs,
-        out_specs=[ANY if name.startswith("back") else VMEM] * len(shapes),
+        out_specs=[ANY if name in ("back", "activation") else VMEM] * len(shapes),
         scratch_shapes=scratch,
         input_output_aliases={len(args) - 1: 0} if in_place else {},
-        cost_estimate=pl.CostEstimate(flops=0, bytes_accessed=int(time * 3.6e6), transcendentals=0),
+        cost_estimate=pl.CostEstimate(flops=0, bytes_accessed=int(time * 3.6e2), transcendentals=0),
         compiler_params=pltpu.CompilerParams(vmem_limit_bytes=12 * 1024 * 1024),
     )(*args)
 
@@ -355,26 +379,53 @@
     dims = (chans, outs, planes, height, half)
     rows = height // CHUNKS
     halos = [from_behind(volume[:, -1, h * rows : (h + 1) * rows], "space", 1) for h in range(CHUNKS)]
-    x_hi, x_lo, part, w_halo, w_back, w_next = call(
-        functools.partial(own_kernel, dims),
-        "own",
-        3.5,
-        [
-            ((8 * chans, cells), BF16),
-            ((8 * chans, cells), BF16),
-            ((outs, cells), F32),
-            ((4 * outs, 12 * chans), BF16),
-            ((8 * chans, 12 * outs), BF16),
-            ((4 * chans, 12 * outs), BF16),
-        ],
-        [pltpu.VMEM((12 * chans, 4 * outs), F32)],
-        volume.reshape(chans * planes * height, width),
-        taps.reshape(27 * chans, outs),
-    )
+    halos = [halo.reshape(chans * rows, width) for halo in halos]
+    x_own, parts, before = [], [], []
+    for h in range(CHUNKS):
+        shapes = [((8 * chans, part_cells), BF16)] * 2 + [((outs, part_cells), F32)]
+        carry = [((outs, LANES), F32)] if h < CHUNKS - 1 else []
+        if h:
+            results = call(
+                functools.partial(own_kernel, dims, h), "own", 1.6, shapes + carry, [], volume.reshape(-1, width), w_own, *before
+            )
+            before = results[3:]
+        else:
+            results = call(
+                functools.partial(own_kernel, dims, h),
+                "own",
+                2.2,
+                shapes
+                + [
+                    ((4 * outs, 24 * chans), BF16),
+                    ((4 * outs, 12 * chans), BF16),
+                    ((8 * chans, 24 * outs), BF16),
+                    ((outs, LANES), F32),
+                ],
+                [pltpu.VMEM((12 * chans, 4 * outs), F32)],
+                volume.reshape(-1, width),
+                taps.reshape(27 * chans, outs),
+            )
+            w_own, w_halo, w_back, carried = results[3:]
+            before = [carried]
+        x_own += results[:2]
+        parts.append(results[2])
     (upstream,) = call(
         functools.partial(flat_kernel, half), "flat", 0.8, [((own, cells), F32)], [], cotangent.reshape(-1, half)
     )
-    x_halos, preacts, grads, carry = [], [], [], []
+    x_halos, grads, carry, activated = [], [], [], []
+
+    def activate(h, preact, *before):
+        return call(
+            functools.partial(activation_kernel, half, h),
+            "activation",
+            1.0,
+            [((own * (height // 2), half), F32)],
+            [pltpu.VMEM((own * (height // 2 // CHUNKS), half), F32), pltpu.SemaphoreType.DMA((own,))],
+            preact,
+            *before,
+            in_place=bool(h),
+        )
+
     for h in range(CHUNKS):
         shapes = [((4 * chans, part_cells), BF16)] * 2 + [((own, part_cells), F32)] * count
         if h < CHUNKS - 1:
@@ -385,8 +436,8 @@
             1.7,
             shapes,
             [pltpu.VMEM((outs, part_cells), F32)],
-            halos[h].reshape(chans * rows, width),
-            part,
+            halos[h],
+            parts[h],
             w_halo,
             *carry,
         )
@@ -394,27 +445,26 @@
         carry = pieces[count:]
         preact = pieces[0]
         if h:
-            preact, _ = lax.optimization_barrier((preact, grads[-1][0]))
+            preact, activated = lax.optimization_barrier((preact, activated))
         for k in range(1, count):
             preact = preact + turned(pieces[k], "chan", k)
         grad = upstream[:, h * part_cells : (h + 1) * part_cells] * jax.nn.sigmoid(preact)
-        preacts.append(preact)
+        if h < CHUNKS - 1:
+            activated = list(activate(h, preact, *activated))
         grads.append([grad] + [turned(grad, "chan", k) for k in range(1, count)])
-    above = [[from_behind(g, "space", -1) for g in chunk] for chunk in grads]
-    (activated,) = call(
-        functools.partial(activation_kernel, half), "activation", 1.2, [((own * (height // 2), half), F32)], [], *preacts
-    )
-    grads[0][0], activated = lax.optimization_barrier((grads[0][0], activated))
+    above = [[from_behind(g, "space", -1) for g in (chunk if h < CHUNKS - 1 else chunk[:1])] for h, chunk in enumerate(grads)]
 
     summed = []
     for h in range(CHUNKS):
         low = max(h - 1, 0)
         last = h == CHUNKS - 1
+        sources = sum(grads[low : h + 1], [])
         if last:
-            early = [g for chunk in above[:-1] for g in chunk] + above[-1][:1]
-            *early, summed_before = lax.optimization_barrier((*early, summed[0]))
-            above = [early[i * count : (i + 1) * count] for i in range(CHUNKS - 1)] + [early[-1:] + above[-1][1:]]
-            summed = [summed_before]
+            *early, summed[0] = lax.optimization_barrier((*[chunk[0] for chunk in above], summed[0]))
+            for chunk, grad in zip(above, early):
+                chunk[0] = grad
+            *sent, summed[0] = lax.optimization_barrier((*grads[-1][1:], summed[0]))
+            above[-1] += [from_behind(g, "space", -1) for g in sent]
         (result,) = call(
             functools.partial(filter_kernel, dims, own, count, h),
             "filter",
@@ -424,49 +474,49 @@
                 pltpu.VMEM((12 * chans, 4 * outs), F32),
                 pltpu.VMEM((outs, (h - low + 1) * part_cells + (LANES if last else 0)), F32),
             ],
-            *sum(grads[low : h + 1], []),
-            x_hi,
-            x_lo,
+            *sources,
+            *x_own[2 * low : 2 * h + 2],
             *x_halos[2 * low : 2 * h + 2],
             *summed,
         )
         summed = [result]
-    buffers = [
-        pltpu.VMEM((outs, cells + LANES), F32),
-        pltpu.VMEM((chans * height, width), F32),
-        pltpu.SemaphoreType.DMA((chans,)),
-    ]
-    shape = [((chans * planes * height, width), F32)]
-    state = {}
-
-    def back_work(index, value):
-        if index == 0:
-            *late, value = lax.optimization_barrier((*above[-1][1:], value))
-            above[-1][1:] = late
-            sources = sum(grads, [])
-            *sources, value = lax.optimization_barrier((*sources, value))
-            state["sources"] = sources
-            (state["grad"],) = call(
-                functools.partial(back_kernel, dims, own, count, 0), "back_0", 3.0, shape, buffers, *sources, w_back
-            )
-        elif index == 1:
-            state["grad"], value = lax.optimization_barrier((state["grad"], value))
+    per = height // 4 // CHUNKS
+    cuts = [0] + [height // 4 * share // 32 // 2 * 2 for share in BACK] + [height // 4]
+    state = {"grad": [], "done": 0}
+
+    def rows_of_grad(value):
+        i = state["done"]
+        begin, end = cuts[i], cuts[i + 1]
+        low, high = begin // per, min(end // per + 1, CHUNKS)
+        sources = sum(grads[low:high], []) + sum(above[low:high], [])
+        *sources, value = lax.optimization_barrier((*sources, value))
+        state["grad"] = call(
+            functools.partial(back_kernel, dims, own, count, begin, end, low, high),
+            "back",
+            2.5,
+            [((chans * planes * height, width), F32)],
+            [pltpu.VMEM((outs, (high - low) * part_cells + (LANES if high == CHUNKS else 0)), F32)] * 2
+            + [pltpu.VMEM((chans * planes * height, width), F32), pltpu.SemaphoreType.DMA((chans * planes,))],
+            *sources,
+            w_back,
+            *state["grad"],
+            in_place=bool(i),
+        )
+        state["done"] += 1
         return value
 
-    packed = sum_over(summed[0], "space", back_work)
-    (volume_grad,) = call(
-        functools.partial(back_kernel, dims, own, count, 1),
-        "back_1",
-        4.0,
-        shape,
-        [buffers[0]] + buffers,
-        *state["sources"],
-        *sum(above, []),
-        w_next,
-        w_back,
-        state["grad"],
-        in_place=True,
-    )
+    def beside(index, value):
+        if state["grad"]:
+            *state["grad"], value = lax.optimization_barrier((*state["grad"], value))
+        if state["done"] == len(cuts) - 2:
+            state["preact"], value = lax.optimization_barrier((preact, value))
+        return rows_of_grad(value) if state["done"] < len(cuts) - 1 else value
+
+    packed = sum_over(summed[0], "space", beside)
+    while state["done"] < len(cuts) - 1:
+        packed = rows_of_grad(packed)
+    (volume_grad,) = state["grad"]
+    (activated,) = activate(CHUNKS - 1, state.get("preact", preact), *activated)
     volume_grad = volume_grad.reshape(chans, planes, height, width)[:real]
     depth_all = planes * lax.axis_size("space")
     factor = float(depth_all // 2 * (height // 2) * half) ** (-0.5)

time: 68.5 us -> 64.5 us (0.942)
  waiting for transfers between devices: 18.4 us -> 12.3 us
  Pallas kernels: 20.5 us -> 21.9 us
  starting transfers between devices: 25.1 us -> 25.8 us
    ppermute x4, waiting for transfers between devices: 13.9 us -> 9.66 us  [turned(): lax.ppermute(value, axis, [(s, (s + steps) % count) for s in range(count)])]
    ppermute x4, waiting for transfers between devices: 4.52 us -> 2.6 us  [sum_over(): lax.ppermute(value, axis, [(s, s ^ bit) for s in range(count)])]
    pallas_call x9 -> x12, Pallas kernels: 20.5 us -> 21.9 us  [call(): pl.pallas_call(kernel, name=name, out_shape=[jax.ShapeDtypeStruct(s, t) f...]
    ppermute x4, starting transfers between devices: 7.42 us -> 8.23 us  [sum_over(): lax.ppermute(value, axis, [(s, s ^ bit) for s in range(count)])]
  transfers between devices with their start and end apart: 14 -> 14, of which waited for: 6 -> 7; matrix products, arithmetic and copies ran while one was open for 0% -> 0% of each run, Pallas kernels for 30% -> 34%
where the time goes in v3:
time: 64.5 us; the launch traced here: 64.3 us
  starting transfers between devices  25.8 us (40%)
  Pallas kernels  21.9 us (34%)
  waiting for transfers between devices  12.3 us (19%)
  local copies, waits for them, and re-layouts  2.45 us (4%)
  other arithmetic  0.96 us (1%)
  between operations  0.89 us (1%)
    pallas_call x12, Pallas kernels, call(): pl.pallas_call(kernel, name=name, out_shape=[jax.ShapeDtypeStruct(s, t) f...  21.9 us
    ppermute x6, starting transfers between devices, from_behind(): lax.ppermute(value, axis, [(source, source + steps) for source in range(i...  12.4 us
    ppermute x4, waiting for transfers between devices, turned(): lax.ppermute(value, axis, [(s, (s + steps) % count) for s in range(count)])  9.66 us
    ppermute x4, starting transfers between devices, sum_over(): lax.ppermute(value, axis, [(s, s ^ bit) for s in range(count)])  8.23 us
    ppermute x4, starting transfers between devices, turned(): lax.ppermute(value, axis, [(s, (s + steps) % count) for s in range(count)])  5.19 us
    ppermute x4, waiting for transfers between devices, sum_over(): lax.ppermute(value, axis, [(s, s ^ bit) for s in range(count)])  2.6 us
    squeeze x1, local copies, waits for them, and re-layouts, on_device(): volume[:, -1, h * rows:(h + 1) * rows]  1.42 us
  transfers between devices with their start and end apart: 14, of which 7 were waited for; matrix products, arithmetic and copies ran while one was open for 0% of the time, Pallas kernels for 34%

profile of v3, /device:TPU:0, one launch (start us, length us, event | category | flops | bytes accessed | tf_op | source)
XLA Modules:
  0.0 64.3 jit_solution(470833211201986015)
XLA Ops:
  0.6 1.4 %slice_bitcast_fusion = (f32[16,64,128]{2,1,0:T(8,128)S(1)}, f32[16,64,128]{2,1,0:T(8,128)S(1)}) fusion(f32[16,2,128,128]{3,2,1,0:T(8,128)} %param.3), kind=kLoop, calls=%fused_computation | loop fusion | bytes 2097152 | tf_op jit(solution)/shard_map/squeeze | solution.py:381
  2.1 2.5 %collective-permute-start.1 = (f32[16,64,128]{2,1,0:T(8,128)S(1)}, f32[16,64,128]{2,1,0:T(8,128)S(1)}, u32[]{:S(2)}, u32[]{:S(2)}) collective-permute-start(f32[16,64,128]{2,1,0:T(8,128)S(1)} %get-tuple-element.116), channel_id=1, source_target_pairs={{0,2},{2,4},{4,6},{6,8},{8,10},{10,12},{12,14},{14,16},{16,18},{18... | collective-permute-start | bytes 1572872 | tf_op jit(solution)/shard_map/ppermute | solution.py:350
  4.6 4.5 %collective-permute-start = (f32[16,64,128]{2,1,0:T(8,128)S(1)}, f32[16,64,128]{2,1,0:T(8,128)S(1)}, u32[]{:S(2)}, u32[]{:S(2)}) collective-permute-start(f32[16,64,128]{2,1,0:T(8,128)S(1)} %get-tuple-element.117), channel_id=1, source_target_pairs={{0,2},{2,4},{4,6},{6,8},{8,10},{10,12},{12,14},{14,16},{16,18},{18... | collective-permute-start | bytes 1572872 | tf_op jit(solution)/shard_map/ppermute | solution.py:350
  9.2 0.9 %copy-done.2 = f32[64,16,3,3,3]{0,1,4,3,2:T(8,128)S(1)} copy-done((f32[64,16,3,3,3]{0,1,4,3,2:T(8,128)S(1)}, f32[64,16,3,3,3]{0,1,4,3,2:T(8,128)}, u32[]{:S(2)}) %copy-start.2) | copy-done | bytes 110616
  10.1 2.0 %own.2 = (bf16[128,2048]{1,0:T(8,128)(2,1)S(1)}, bf16[128,2048]{1,0:T(8,128)(2,1)S(1)}, f32[64,2048]{1,0:T(8,128)S(1)}, bf16[256,384]{1,0:T(8,128)(2,1)S(1)}, bf...) custom-call(f32[4096,128]{1,0:T(8,128)S(1)} %bitcast.19, f32[432,64]{1,0:T(8,128)S(1)} %bitcast.24), custom_call_target="tpu_custom_call" | custom-call | bytes 792 | tf_op jit(solution)/shard_map/own/pallas_call | solution.py:329
  12.1 1.4 %halo.2 = (bf16[64,2048]{1,0:T(8,128)(2,1)S(1)}, bf16[64,2048]{1,0:T(8,128)(2,1)S(1)}, f32[32,2048]{1,0:T(8,128)S(1)}, f32[32,2048]{1,0:T(8,128)S(1)}, f32[64,128]{1,0:T(8,128)S(1)}) custom-call(f32[1024,128]{1,0:T(8,128)S(1)} %bitcast.23, f32[64,2048]{1,0:T(8,128)S(1)} %get-tuple-element.60.refs_1_, bf16[256,192]{1,0:T(8,128)(2,1)S(1)} %get-tuple-element.59.refs_2_), custom_call_target="tpu_custom_call" | custom-call | bytes 612 | tf_op jit(solution)/shard_map/halo/pallas_call | solution.py:329
  13.5 1.6 %collective-permute-start.2 = (f32[32,2048]{1,0:T(8,128)S(1)}, f32[32,2048]{1,0:T(8,128)S(1)}, u32[]{:S(2)}, u32[]{:S(2)}) collective-permute-start(f32[32,2048]{1,0:T(8,128)S(1)} %get-tuple-element.64), channel_id=1, source_target_pairs={{0,1},{1,0},{2,3},{3,2},{4,5},{5,4},{6,7},{7,6},{8,9},{9,8},{10,11... | collective-permute-start | bytes 786440 | tf_op jit(solution)/shard_map/ppermute | solution.py:344
  15.6 2.0 %own.3 = (bf16[128,2048]{1,0:T(8,128)(2,1)S(1)}, bf16[128,2048]{1,0:T(8,128)(2,1)S(1)}, f32[64,2048]{1,0:T(8,128)S(1)}) custom-call(f32[4096,128]{1,0:T(8,128)S(1)} %bitcast.20, bf16[256,384]{1,0:T(8,128)(2,1)S(1)} %get-tuple-element.56.refs_0_, f32[64,128]{1,0:T(8,128)S(1)} %get-tuple-element.57.refs_1_), custom_call_target="tpu_custom_call" | custom-call | bytes 576 | tf_op jit(solution)/shard_map/own/pallas_call | solution.py:329
  17.6 1.3 %halo.3 = (bf16[64,2048]{1,0:T(8,128)(2,1)S(1)}, bf16[64,2048]{1,0:T(8,128)(2,1)S(1)}, f32[32,2048]{1,0:T(8,128)S(1)}, f32[32,2048]{1,0:T(8,128)S(1)}) custom-call(f32[1024,128]{1,0:T(8,128)S(1)} %bitcast.22, f32[64,2048]{1,0:T(8,128)S(1)} %get-tuple-element.58.refs_1_, bf16[256,192]{1,0:T(8,128)(2,1)S(1)} %get-tuple-element.59.refs_2_, ...), custom_call_target="tpu_custom_call" | custom-call | bytes 612 | tf_op jit(solution)/shard_map/halo/pallas_call | solution.py:329
  19.5 2.9 %collective-permute-done.2 = f32[32,2048]{1,0:T(8,128)S(1)} collective-permute-done((f32[32,2048]{1,0:T(8,128)S(1)}, f32[32,2048]{1,0:T(8,128)S(1)}, u32[]{:S(2)}, u32[]{:S(2)}) %collective-permute-start.2) | collective-permute-done | bytes 262176 | tf_op jit(solution)/shard_map/ppermute | solution.py:344
  22.6 1.3 %collective-permute-start.6 = (f32[32,2048]{1,0:T(8,128)S(1)}, f32[32,2048]{1,0:T(8,128)S(1)}, u32[]{:S(2)}, u32[]{:S(2)}) collective-permute-start(f32[32,2048]{1,0:T(8,128)S(1)} %get-tuple-element.87.refs_0_), channel_id=1, source_target_pairs={{2,0},{4,2},{6,4},{8,6},{10,8},{12,10},{14,12},{16,14},{18,16},{20... | collective-permute-start | bytes 786440 | tf_op jit(solution)/shard_map/ppermute | solution.py:350
  23.9 1.5 %collective-permute-start.4 = (f32[32,2048]{1,0:T(8,128)S(1)}, f32[32,2048]{1,0:T(8,128)S(1)}, u32[]{:S(2)}, u32[]{:S(2)}) collective-permute-start(f32[32,2048]{1,0:T(8,128)S(1)} %get-tuple-element.87.refs_0_), channel_id=1, source_target_pairs={{0,1},{1,0},{2,3},{3,2},{4,5},{5,4},{6,7},{7,6},{8,9},{9,8},{10,11... | collective-permute-start | bytes 786440 | tf_op jit(solution)/shard_map/ppermute | solution.py:344
  25.4 1.6 %activation.2.refs_0_ = f32[2048,64]{1,0:T(8,128)} custom-call(f32[32,2048]{1,0:T(8,128)S(1)} %get-tuple-element.115.chunk), custom_call_target="tpu_custom_call" | custom-call | bytes 360 | tf_op jit(solution)/shard_map/activation/pallas_call | solution.py:329
  27.0 1.1 %collective-permute-done.3 = f32[32,2048]{1,0:T(8,128)S(1)} collective-permute-done((f32[32,2048]{1,0:T(8,128)S(1)}, f32[32,2048]{1,0:T(8,128)S(1)}, u32[]{:S(2)}, u32[]{:S(2)}) %collective-permute-start.3) | collective-permute-done | bytes 262176 | tf_op jit(solution)/shard_map/ppermute | solution.py:344
  28.2 1.3 %collective-permute-start.7 = (f32[32,2048]{1,0:T(8,128)S(1)}, f32[32,2048]{1,0:T(8,128)S(1)}, u32[]{:S(2)}, u32[]{:S(2)}) collective-permute-start(f32[32,2048]{1,0:T(8,128)S(1)} %get-tuple-element.101.refs_2_.refs_0_), channel_id=1, source_target_pairs={{2,0},{4,2},{6,4},{8,6},{10,8},{12,10},{14,12},{16,14},{18,16},{20... | collective-permute-start | bytes 786440 | tf_op jit(solution)/shard_map/ppermute | solution.py:350
  29.5 1.5 %collective-permute-start.5 = (f32[32,2048]{1,0:T(8,128)S(1)}, f32[32,2048]{1,0:T(8,128)S(1)}, u32[]{:S(2)}, u32[]{:S(2)}) collective-permute-start(f32[32,2048]{1,0:T(8,128)S(1)} %get-tuple-element.101.refs_2_.refs_0_), channel_id=1, source_target_pairs={{0,1},{1,0},{2,3},{3,2},{4,5},{5,4},{6,7},{7,6},{8,9},{9,8},{10,11... | collective-permute-start | bytes 786440 | tf_op jit(solution)/shard_map/ppermute | solution.py:344
  31.0 2.7 %collective-permute-done.4.refs_1_ = f32[32,2048]{1,0:T(8,128)S(1)} collective-permute-done((f32[32,2048]{1,0:T(8,128)S(1)}, f32[32,2048]{1,0:T(8,128)S(1)}, u32[]{:S(2)}, u32[]{:S(2)}) %collective-permute-start.4) | collective-permute-done | bytes 262176 | tf_op jit(solution)/shard_map/ppermute | solution.py:344
  33.7 1.3 %collective-permute-start.8 = (f32[32,2048]{1,0:T(8,128)S(1)}, f32[32,2048]{1,0:T(8,128)S(1)}, u32[]{:S(2)}, u32[]{:S(2)}) collective-permute-start(f32[32,2048]{1,0:T(8,128)S(1)} %collective-permute-done.4.refs_1_), channel_id=1, source_target_pairs={{2,0},{4,2},{6,4},{8,6},{10,8},{12,10},{14,12},{16,14},{18,16},{20... | collective-permute-start | bytes 786440 | tf_op jit(solution)/shard_map/ppermute | solution.py:350
  35.0 1.4 %filter.2.refs_12_ = f32[192,256]{1,0:T(8,128)S(1)} custom-call(f32[32,2048]{1,0:T(8,128)S(1)} %get-tuple-element.87.refs_0_, f32[32,2048]{1,0:T(8,128)S(1)} %collective-permute-done.4.refs_1_, bf16[128,2048]{1,0:T(8,128)(2,1)S(1)} %get-tuple-element.67.refs_2_.refs_4_, bf16[128,2048]{1,0:T(8,128)(2,1)S(1)} %get-tuple-element.68.refs_3_.refs_5_, ...), custom_call_target="tpu_custom_call" | custom-call | bytes 576 | tf_op jit(solution)/shard_map/filter/pallas_call | solution.py:329
  36.4 2.9 %collective-permute-done.5.refs_3_.refs_1_ = f32[32,2048]{1,0:T(8,128)S(1)} collective-permute-done((f32[32,2048]{1,0:T(8,128)S(1)}, f32[32,2048]{1,0:T(8,128)S(1)}, u32[]{:S(2)}, u32[]{:S(2)}) %collective-permute-start.5) | collective-permute-done | bytes 262176 | tf_op jit(solution)/shard_map/ppermute | solution.py:344
  39.3 1.5 %collective-permute-start.9 = (f32[32,2048]{1,0:T(8,128)S(1)}, f32[32,2048]{1,0:T(8,128)S(1)}, u32[]{:S(2)}, u32[]{:S(2)}) collective-permute-start(f32[32,2048]{1,0:T(8,128)S(1)} %collective-permute-done.5.refs_3_.refs_1_), channel_id=1, source_target_pairs={{2,0},{4,2},{6,4},{8,6},{10,8},{12,10},{14,12},{16,14},{18,16},{20... | collective-permute-start | bytes 786440 | tf_op jit(solution)/shard_map/ppermute | solution.py:350
  40.8 1.6 %filter.3 = f32[224,128]{1,0:T(8,128)S(1)} custom-call(f32[32,2048]{1,0:T(8,128)S(1)} %get-tuple-element.87.refs_0_, f32[32,2048]{1,0:T(8,128)S(1)} %collective-permute-done.4.refs_1_, f32[32,2048]{1,0:T(8,128)S(1)} %get-tuple-element.101.refs_2_.refs_0_, f32[32,2048]{1,0:T(8,128)S(1)} %collective-permute-done.5.refs_3_.refs_1_, ...), custom_call_target="tpu_custom_call" | custom-call | bytes 576 | tf_op jit(solution)/shard_map/filter/pallas_call | solution.py:329
  42.4 1.2 %collective-permute-start.10 = (f32[224,128]{1,0:T(8,128)S(1)}, f32[224,128]{1,0:T(8,128)S(1)}, u32[]{:S(2)}, u32[]{:S(2)}) collective-permute-start(f32[224,128]{1,0:T(8,128)S(1)} %filter.3), channel_id=1, source_target_pairs={{0,2},{2,0},{4,6},{6,4},{8,10},{10,8},{12,14},{14,12},{16,18},{18,... | collective-permute-start | bytes 344072 | tf_op jit(solution)/shard_map/ppermute | solution.py:359
  43.6 1.0 %collective-permute-done.10 = f32[224,128]{1,0:T(8,128)S(1)} collective-permute-done((f32[224,128]{1,0:T(8,128)S(1)}, f32[224,128]{1,0:T(8,128)S(1)}, u32[]{:S(2)}, u32[]{:S(2)}) %collective-permute-start.10) | collective-permute-done | bytes 114720 | tf_op jit(solution)/shard_map/ppermute | solution.py:359
  44.6 2.1 %collective-permute-start.11 = (f32[224,128]{1,0:T(8,128)S(1)}, f32[224,128]{1,0:T(8,128)S(1)}, u32[]{:S(2)}, u32[]{:S(2)}) collective-permute-start(f32[224,128]{1,0:T(8,128)S(1)} %add.28), channel_id=1, source_target_pairs={{0,4},{2,6},{4,0},{6,2},{8,12},{10,14},{12,8},{14,10},{16,20},{18,... | collective-permute-start | bytes 344072 | tf_op jit(solution)/shard_map/ppermute | solution.py:359
  46.7 2.6 %back.3.refs_9_ = f32[4096,128]{1,0:T(8,128)} custom-call(f32[32,2048]{1,0:T(8,128)S(1)} %get-tuple-element.87.refs_0_, f32[32,2048]{1,0:T(8,128)S(1)} %collective-permute-done.4.refs_1_, f32[32,2048]{1,0:T(8,128)S(1)} %collective-permute-done.6.refs_2_.refs_4_, f32[32,2048]{1,0:T(8,128)S(1)} %collective-permute-done.8.refs_3_.refs_5_, ...), custom_call_target="tpu_custom_call" | custom-call | bytes 900 | tf_op jit(solution)/shard_map/back/pallas_call | solution.py:329
  49.3 1.0 %collective-permute-done.11 = f32[224,128]{1,0:T(8,128)S(1)} collective-permute-done((f32[224,128]{1,0:T(8,128)S(1)}, f32[224,128]{1,0:T(8,128)S(1)}, u32[]{:S(2)}, u32[]{:S(2)}) %collective-permute-start.11) | collective-permute-done | bytes 114720 | tf_op jit(solution)/shard_map/ppermute | solution.py:359
  50.4 2.3 %collective-permute-start.12 = (f32[224,128]{1,0:T(8,128)S(1)}, f32[224,128]{1,0:T(8,128)S(1)}, u32[]{:S(2)}, u32[]{:S(2)}) collective-permute-start(f32[224,128]{1,0:T(8,128)S(1)} %add.29), channel_id=1, source_target_pairs={{0,8},{2,10},{4,12},{6,14},{8,0},{10,2},{12,4},{14,6},{16,24},{18,... | collective-permute-start | bytes 344072 | tf_op jit(solution)/shard_map/ppermute | solution.py:359
  52.7 3.2 %back.4.refs_5_ = f32[4096,128]{1,0:T(8,128)} custom-call(f32[32,2048]{1,0:T(8,128)S(1)} %get-tuple-element.87.refs_0_, f32[32,2048]{1,0:T(8,128)S(1)} %collective-permute-done.4.refs_1_, f32[32,2048]{1,0:T(8,128)S(1)} %get-tuple-element.101.refs_2_.refs_0_, f32[32,2048]{1,0:T(8,128)S(1)} %collective-permute-done.5.refs_3_.refs_1_, ...), custom_call_target="tpu_custom_call", output_to_operand_aliasing={{}: (9, {})} | custom-call | bytes 900 | tf_op jit(solution)/shard_map/back/pallas_call | solution.py:329
  55.9 2.7 %collective-permute-start.13 = (f32[224,128]{1,0:T(8,128)S(1)}, f32[224,128]{1,0:T(8,128)S(1)}, u32[]{:S(2)}, u32[]{:S(2)}) collective-permute-start(f32[224,128]{1,0:T(8,128)S(1)} %add.30), channel_id=1, source_target_pairs={{0,16},{2,18},{4,20},{6,22},{8,24},{10,26},{12,28},{14,30},{16,0},... | collective-permute-start | bytes 344072 | tf_op jit(solution)/shard_map/ppermute | solution.py:359
  58.6 1.6 %activation.3 = f32[2048,64]{1,0:T(8,128)} custom-call(f32[32,2048]{1,0:T(8,128)S(1)} %get-tuple-element.98.chunk, f32[2048,64]{1,0:T(8,128)} %activation.2.refs_0_), custom_call_target="tpu_custom_call", output_to_operand_aliasing={{}: (1, {})} | custom-call | bytes 360 | tf_op jit(solution)/shard_map/activation/pallas_call | solution.py:329
  60.2 2.6 %back.5 = f32[4096,128]{1,0:T(8,128)} custom-call(f32[32,2048]{1,0:T(8,128)S(1)} %get-tuple-element.101.refs_2_.refs_0_, f32[32,2048]{1,0:T(8,128)S(1)} %collective-permute-done.5.refs_3_.refs_1_, f32[32,2048]{1,0:T(8,128)S(1)} %collective-permute-done.7.refs_6_.refs_2_, ...), custom_call_target="tpu_custom_call", output_to_operand_aliasing={{}: (5, {})} | custom-call | bytes 900 | tf_op jit(solution)/shard_map/back/pallas_call | solution.py:329
  (23 shorter events, 2.9 us)
Async XLA Ops:
  0.6 8.5 %copy-start = (f32[16,2,128,128]{3,2,1,0:T(8,128)S(1)}, f32[16,2,128,128]{3,2,1,0:T(8,128)}, u32[]{:S(2)}) copy-start(f32[16,2,128,128]{3,2,1,0:T(8,128)} %param.3) | copy-start | bytes 6291460
  2.1 12.9 %copy-start.1 = (f32[32,1,64,64]{3,2,1,0:T(8,128)S(1)}, f32[32,1,64,64]{3,2,1,0:T(8,128)}, u32[]{:S(2)}) copy-start(f32[32,1,64,64]{3,2,1,0:T(8,128)} %param.5) | copy-start | bytes 1572868
  2.1 10.0 %collective-permute-start.1 = (f32[16,64,128]{2,1,0:T(8,128)S(1)}, f32[16,64,128]{2,1,0:T(8,128)S(1)}, u32[]{:S(2)}, u32[]{:S(2)}) collective-permute-start(f32[16,64,128]{2,1,0:T(8,128)S(1)} %get-tuple-element.116), channel_id=1, source_target_pairs={{0,2},{2,4},{4,6},{6,8},{8,10},{10,12},{12,14},{14,16},{16,18},{18... | collective-permute-start | bytes 1572872 | tf_op jit(solution)/shard_map/ppermute | solution.py:350
  4.6 13.0 %collective-permute-start = (f32[16,64,128]{2,1,0:T(8,128)S(1)}, f32[16,64,128]{2,1,0:T(8,128)S(1)}, u32[]{:S(2)}, u32[]{:S(2)}) collective-permute-start(f32[16,64,128]{2,1,0:T(8,128)S(1)} %get-tuple-element.117), channel_id=1, source_target_pairs={{0,2},{2,4},{4,6},{6,8},{8,10},{10,12},{12,14},{14,16},{16,18},{18... | collective-permute-start | bytes 1572872 | tf_op jit(solution)/shard_map/ppermute | solution.py:350
  9.2 0.9 %copy-start.2 = (f32[64,16,3,3,3]{0,1,4,3,2:T(8,128)S(1)}, f32[64,16,3,3,3]{0,1,4,3,2:T(8,128)}, u32[]{:S(2)}) copy-start(f32[64,16,3,3,3]{0,1,4,3,2:T(8,128)} %param.4) | copy-start | bytes 331780
  13.5 9.0 %collective-permute-start.2 = (f32[32,2048]{1,0:T(8,128)S(1)}, f32[32,2048]{1,0:T(8,128)S(1)}, u32[]{:S(2)}, u32[]{:S(2)}) collective-permute-start(f32[32,2048]{1,0:T(8,128)S(1)} %get-tuple-element.64), channel_id=1, source_target_pairs={{0,1},{1,0},{2,3},{3,2},{4,5},{5,4},{6,7},{7,6},{8,9},{9,8},{10,11... | collective-permute-start | bytes 786440 | tf_op jit(solution)/shard_map/ppermute | solution.py:344
  18.9 9.2 %collective-permute-start.3 = (f32[32,2048]{1,0:T(8,128)S(1)}, f32[32,2048]{1,0:T(8,128)S(1)}, u32[]{:S(2)}, u32[]{:S(2)}) collective-permute-start(f32[32,2048]{1,0:T(8,128)S(1)} %get-tuple-element.66), channel_id=1, source_target_pairs={{0,1},{1,0},{2,3},{3,2},{4,5},{5,4},{6,7},{7,6},{8,9},{9,8},{10,11... | collective-permute-start | bytes 786440 | tf_op jit(solution)/shard_map/ppermute | solution.py:344
  22.6 13.8 %collective-permute-start.6 = (f32[32,2048]{1,0:T(8,128)S(1)}, f32[32,2048]{1,0:T(8,128)S(1)}, u32[]{:S(2)}, u32[]{:S(2)}) collective-permute-start(f32[32,2048]{1,0:T(8,128)S(1)} %get-tuple-element.87.refs_0_), channel_id=1, source_target_pairs={{2,0},{4,2},{6,4},{8,6},{10,8},{12,10},{14,12},{16,14},{18,16},{20... | collective-permute-start | bytes 786440 | tf_op jit(solution)/shard_map/ppermute | solution.py:350
  23.9 9.8 %collective-permute-start.4 = (f32[32,2048]{1,0:T(8,128)S(1)}, f32[32,2048]{1,0:T(8,128)S(1)}, u32[]{:S(2)}, u32[]{:S(2)}) collective-permute-start(f32[32,2048]{1,0:T(8,128)S(1)} %get-tuple-element.87.refs_0_), channel_id=1, source_target_pairs={{0,1},{1,0},{2,3},{3,2},{4,5},{5,4},{6,7},{7,6},{8,9},{9,8},{10,11... | collective-permute-start | bytes 786440 | tf_op jit(solution)/shard_map/ppermute | solution.py:344
  28.2 8.2 %collective-permute-start.7 = (f32[32,2048]{1,0:T(8,128)S(1)}, f32[32,2048]{1,0:T(8,128)S(1)}, u32[]{:S(2)}, u32[]{:S(2)}) collective-permute-start(f32[32,2048]{1,0:T(8,128)S(1)} %get-tuple-element.101.refs_2_.refs_0_), channel_id=1, source_target_pairs={{2,0},{4,2},{6,4},{8,6},{10,8},{12,10},{14,12},{16,14},{18,16},{20... | collective-permute-start | bytes 786440 | tf_op jit(solution)/shard_map/ppermute | solution.py:350
  29.5 9.8 %collective-permute-start.5 = (f32[32,2048]{1,0:T(8,128)S(1)}, f32[32,2048]{1,0:T(8,128)S(1)}, u32[]{:S(2)}, u32[]{:S(2)}) collective-permute-start(f32[32,2048]{1,0:T(8,128)S(1)} %get-tuple-element.101.refs_2_.refs_0_), channel_id=1, source_target_pairs={{0,1},{1,0},{2,3},{3,2},{4,5},{5,4},{6,7},{7,6},{8,9},{9,8},{10,11... | collective-permute-start | bytes 786440 | tf_op jit(solution)/shard_map/ppermute | solution.py:344
  33.7 10.9 %collective-permute-start.8 = (f32[32,2048]{1,0:T(8,128)S(1)}, f32[32,2048]{1,0:T(8,128)S(1)}, u32[]{:S(2)}, u32[]{:S(2)}) collective-permute-start(f32[32,2048]{1,0:T(8,128)S(1)} %collective-permute-done.4.refs_1_), channel_id=1, source_target_pairs={{2,0},{4,2},{6,4},{8,6},{10,8},{12,10},{14,12},{16,14},{18,16},{20... | collective-permute-start | bytes 786440 | tf_op jit(solution)/shard_map/ppermute | solution.py:350
  39.3 11.1 %collective-permute-start.9 = (f32[32,2048]{1,0:T(8,128)S(1)}, f32[32,2048]{1,0:T(8,128)S(1)}, u32[]{:S(2)}, u32[]{:S(2)}) collective-permute-start(f32[32,2048]{1,0:T(8,128)S(1)} %collective-permute-done.5.refs_3_.refs_1_), channel_id=1, source_target_pairs={{2,0},{4,2},{6,4},{8,6},{10,8},{12,10},{14,12},{16,14},{18,16},{20... | collective-permute-start | bytes 786440 | tf_op jit(solution)/shard_map/ppermute | solution.py:350
  42.4 2.2 %collective-permute-start.10 = (f32[224,128]{1,0:T(8,128)S(1)}, f32[224,128]{1,0:T(8,128)S(1)}, u32[]{:S(2)}, u32[]{:S(2)}) collective-permute-start(f32[224,128]{1,0:T(8,128)S(1)} %filter.3), channel_id=1, source_target_pairs={{0,2},{2,0},{4,6},{6,4},{8,10},{10,8},{12,14},{14,12},{16,18},{18,... | collective-permute-start | bytes 344072 | tf_op jit(solution)/shard_map/ppermute | solution.py:359
  44.6 5.7 %collective-permute-start.11 = (f32[224,128]{1,0:T(8,128)S(1)}, f32[224,128]{1,0:T(8,128)S(1)}, u32[]{:S(2)}, u32[]{:S(2)}) collective-permute-start(f32[224,128]{1,0:T(8,128)S(1)} %add.28), channel_id=1, source_target_pairs={{0,4},{2,6},{4,0},{6,2},{8,12},{10,14},{12,8},{14,10},{16,20},{18,... | collective-permute-start | bytes 344072 | tf_op jit(solution)/shard_map/ppermute | solution.py:359
  50.4 5.5 %collective-permute-start.12 = (f32[224,128]{1,0:T(8,128)S(1)}, f32[224,128]{1,0:T(8,128)S(1)}, u32[]{:S(2)}, u32[]{:S(2)}) collective-permute-start(f32[224,128]{1,0:T(8,128)S(1)} %add.29), channel_id=1, source_target_pairs={{0,8},{2,10},{4,12},{6,14},{8,0},{10,2},{12,4},{14,6},{16,24},{18,... | collective-permute-start | bytes 344072 | tf_op jit(solution)/shard_map/ppermute | solution.py:359
  55.9 7.5 %collective-permute-start.13 = (f32[224,128]{1,0:T(8,128)S(1)}, f32[224,128]{1,0:T(8,128)S(1)}, u32[]{:S(2)}, u32[]{:S(2)}) collective-permute-start(f32[224,128]{1,0:T(8,128)S(1)} %add.30), channel_id=1, source_target_pairs={{0,16},{2,18},{4,20},{6,22},{8,24},{10,26},{12,28},{14,30},{16,0},... | collective-permute-start | bytes 344072 | tf_op jit(solution)/shard_map/ppermute | solution.py:359

commit v4 on v3

--- a/solution.py
+++ b/solution.py
@@ -12,7 +12,7 @@
 LANES = 128
 STEP = 8
 CHUNKS = 2
-BACK = (10, 22)
+BACK = (14,)
 VMEM = pl.BlockSpec(memory_space=pltpu.VMEM)
 ANY = pl.BlockSpec(memory_space=pl.ANY)
 
@@ -204,7 +204,7 @@
     halos, refs = refs[: 2 * loaded], refs[2 * loaded :]
     if chunk:
         before, refs = refs[0], refs[1:]
-    out, total, g_all = refs
+    *out, total, g_all = refs
     gather_grads(pieces, g_all, own, count)
     base = (chunk - loaded + 1) * per
     begin = chunk * per - (1 if chunk else 0)
@@ -235,8 +235,9 @@
         )
         first += size
     if not last:
-        out[...] = total[...]
+        out[0][...] = total[...]
         return
+    kept, sent, packed = out
 
     def tap_block(tap, side):
         p, q, r = tap // 9, tap // 3 % 3, tap % 3
@@ -248,7 +249,11 @@
     left_side = lane_of((chans, LANES)) < outs
     for tap in range(14):
         right = tap_block(tap + 14, 1) if tap + 14 < 27 else jnp.zeros((chans, LANES), F32)
-        out[tap * chans : (tap + 1) * chans, :] = jnp.where(left_side, tap_block(tap, 0), right)
+        packed[tap * chans : (tap + 1) * chans, :] = jnp.where(left_side, tap_block(tap, 0), right)
+    size = 7 * chans
+    side = lax.rem(lax.axis_index("space"), 2)
+    kept[...] = packed[pl.ds(pl.multiple_of(side * size, size), size), :]
+    sent[...] = packed[pl.ds(pl.multiple_of((1 - side) * size, size), size), :]
 
 
 def back_kernel(dims, own, count, begin, end, low, high, *refs):
@@ -350,16 +355,21 @@
     return lax.ppermute(value, axis, [(source, source + steps) for source in range(initial, last)])
 
 
-def sum_over(value, axis, beside):
+def sum_over(kept, sent, axis, beside):
     count = lax.axis_size(axis)
-    if count & (count - 1):
-        return beside(0, lax.psum(value, axis))
-    bit = 1
+    assert count > 1 and not count & (count - 1)
+
+    def swapped(value, bit):
+        return lax.ppermute(value, axis, [(s, s ^ bit) for s in range(count)])
+
+    value = beside(0, kept + swapped(sent, 1))
+    bit = 2
     while bit < count:
-        value = value + lax.ppermute(value, axis, [(s, s ^ bit) for s in range(count)])
-        value = beside(bit.bit_length() - 1, value)
+        value = beside(bit.bit_length() - 1, value + swapped(value, bit))
         bit *= 2
-    return value
+    other = swapped(value, 1)
+    first = lax.rem(lax.axis_index(axis), 2) == 0
+    return jnp.where(first, value, other), jnp.where(first, other, value)
 
 
 def on_device(volume, filters, cotangent):
@@ -412,7 +422,7 @@
     (upstream,) = call(
         functools.partial(flat_kernel, half), "flat", 0.8, [((own, cells), F32)], [], cotangent.reshape(-1, half)
     )
-    x_halos, grads, carry, activated = [], [], [], []
+    x_halos, grads, above, carry, activated = [], [], [], [], []
 
     def activate(h, preact, *before):
         return call(
@@ -449,28 +459,34 @@
         for k in range(1, count):
             preact = preact + turned(pieces[k], "chan", k)
         grad = upstream[:, h * part_cells : (h + 1) * part_cells] * jax.nn.sigmoid(preact)
+        above.append([from_behind(grad, "space", -1)])
+        grads.append([grad] + [turned(grad, "chan", k) for k in range(1, count)])
         if h < CHUNKS - 1:
             activated = list(activate(h, preact, *activated))
-        grads.append([grad] + [turned(grad, "chan", k) for k in range(1, count)])
-    above = [[from_behind(g, "space", -1) for g in (chunk if h < CHUNKS - 1 else chunk[:1])] for h, chunk in enumerate(grads)]
+    for h in range(CHUNKS - 1):
+        sent = grads[h][1:]
+        above[h] += [from_behind(g, "space", -1) for g in sent]
 
     summed = []
     for h in range(CHUNKS):
         low = max(h - 1, 0)
         last = h == CHUNKS - 1
         sources = sum(grads[low : h + 1], [])
+        if not last:
+            sources[0], above[h][0] = lax.optimization_barrier((sources[0], above[h][0]))
         if last:
             *early, summed[0] = lax.optimization_barrier((*[chunk[0] for chunk in above], summed[0]))
             for chunk, grad in zip(above, early):
                 chunk[0] = grad
             *sent, summed[0] = lax.optimization_barrier((*grads[-1][1:], summed[0]))
             above[-1] += [from_behind(g, "space", -1) for g in sent]
-        (result,) = call(
+        summed = call(
             functools.partial(filter_kernel, dims, own, count, h),
             "filter",
             1.6,
-            [((14 * chans, LANES) if last else (12 * chans, 4 * outs), F32)],
-            [
+            [((7 * chans, LANES), F32)] * 2 if last else [((12 * chans, 4 * outs), F32)],
+            ([pltpu.VMEM((14 * chans, LANES), F32)] if last else [])
+            + [
                 pltpu.VMEM((12 * chans, 4 * outs), F32),
                 pltpu.VMEM((outs, (h - low + 1) * part_cells + (LANES if last else 0)), F32),
             ],
@@ -479,7 +495,7 @@
             *x_halos[2 * low : 2 * h + 2],
             *summed,
         )
-        summed = [result]
+        summed = list(summed)
     per = height // 4 // CHUNKS
     cuts = [0] + [height // 4 * share // 32 // 2 * 2 for share in BACK] + [height // 4]
     state = {"grad": [], "done": 0}
@@ -506,21 +522,25 @@
         return value
 
     def beside(index, value):
-        if state["grad"]:
-            *state["grad"], value = lax.optimization_barrier((*state["grad"], value))
-        if state["done"] == len(cuts) - 2:
-            state["preact"], value = lax.optimization_barrier((preact, value))
-        return rows_of_grad(value) if state["done"] < len(cuts) - 1 else value
-
-    packed = sum_over(summed[0], "space", beside)
+        for started in ("grad", "activated"):
+            if state.get(started):
+                *state[started], value = lax.optimization_barrier((*state[started], value))
+        if state["done"] < len(cuts) - 1:
+            return rows_of_grad(value)
+        if "activated" not in state:
+            shown, value = lax.optimization_barrier((preact, value))
+            state["activated"] = list(activate(CHUNKS - 1, shown, *activated))
+        return value
+
+    low, high = sum_over(*summed, "space", beside)
     while state["done"] < len(cuts) - 1:
-        packed = rows_of_grad(packed)
+        low = rows_of_grad(low)
     (volume_grad,) = state["grad"]
-    (activated,) = activate(CHUNKS - 1, state.get("preact", preact), *activated)
+    (activated,) = state.get("activated") or activate(CHUNKS - 1, preact, *activated)
     volume_grad = volume_grad.reshape(chans, planes, height, width)[:real]
     depth_all = planes * lax.axis_size("space")
     factor = float(depth_all // 2 * (height // 2) * half) ** (-0.5)
-    unpacked = jnp.concatenate([packed[:, :outs], packed[: 13 * chans, outs:]], axis=0) * factor
+    unpacked = jnp.concatenate([low[:, :outs], high[:, :outs], low[:, outs:], high[:-chans, outs:]], axis=0) * factor
     filter_grad = unpacked.reshape(3, 3, 3, chans, outs)[:, :, :, :real].transpose(4, 3, 0, 1, 2)
     return (activated.reshape(cotangent.shape), volume_grad, filter_grad)
 

time: 64.5 us -> 64.1 us (level)
  Pallas kernels: 21.9 us -> 20.7 us
  waiting for transfers between devices: 12.3 us -> 13.1 us
    pallas_call x12 -> x11, Pallas kernels: 21.9 us -> 20.7 us  [call(): pl.pallas_call(kernel, name=name, out_shape=[jax.ShapeDtypeStruct(s, t) f...]
    ppermute x4 -> x5, waiting for transfers between devices: 2.6 us -> 3.36 us  [swapped(): return lax.ppermute(value, axis, [(s, s ^ bit) for s in range(count)])]
    ppermute x4 -> x5, starting transfers between devices: 8.23 us -> 8.14 us  [swapped(): return lax.ppermute(value, axis, [(s, s ^ bit) for s in range(count)])]
  transfers between devices with their start and end apart: 14 -> 15, of which waited for: 7 -> 7; matrix products, arithmetic and copies ran while one was open for 0% -> 0% of each run, Pallas kernels for 34% -> 32%
where the time goes in v4:
time: 64.1 us; the launch traced here: 63.8 us
  starting transfers between devices  25.7 us (40%)
  Pallas kernels  20.7 us (32%)
  waiting for transfers between devices  13.1 us (20%)
  local copies, waits for them, and re-layouts  2.52 us (4%)
  other arithmetic  0.95 us (1%)
  between operations  0.89 us (1%)
    pallas_call x11, Pallas kernels, call(): pl.pallas_call(kernel, name=name, out_shape=[jax.ShapeDtypeStruct(s, t) f...  20.7 us
    ppermute x6, starting transfers between devices, from_behind(): lax.ppermute(value, axis, [(source, source + steps) for source in range(i...  12.4 us
    ppermute x4, waiting for transfers between devices, turned(): lax.ppermute(value, axis, [(s, (s + steps) % count) for s in range(count)])  9.67 us
    ppermute x5, starting transfers between devices, swapped(): return lax.ppermute(value, axis, [(s, s ^ bit) for s in range(count)])  8.14 us
    ppermute x4, starting transfers between devices, turned(): lax.ppermute(value, axis, [(s, (s + steps) % count) for s in range(count)])  5.19 us
    ppermute x5, waiting for transfers between devices, swapped(): return lax.ppermute(value, axis, [(s, s ^ bit) for s in range(count)])  3.36 us
    squeeze x1, local copies, waits for them, and re-layouts, on_device(): volume[:, -1, h * rows:(h + 1) * rows]  1.42 us
  transfers between devices with their start and end apart: 15, of which 7 were waited for; matrix products, arithmetic and copies ran while one was open for 0% of the time, Pallas kernels for 32%

profile of v4, /device:TPU:0, one launch (start us, length us, event | category | flops | bytes accessed | tf_op | source)
XLA Modules:
  0.0 63.8 jit_solution(13910661607099789731)
XLA Ops:
  0.6 1.4 %slice_bitcast_fusion = (f32[16,64,128]{2,1,0:T(8,128)S(1)}, f32[16,64,128]{2,1,0:T(8,128)S(1)}) fusion(f32[16,2,128,128]{3,2,1,0:T(8,128)} %param.3), kind=kLoop, calls=%fused_computation | loop fusion | bytes 2097152 | tf_op jit(solution)/shard_map/squeeze | solution.py:391
  2.1 2.5 %collective-permute-start.1 = (f32[16,64,128]{2,1,0:T(8,128)S(1)}, f32[16,64,128]{2,1,0:T(8,128)S(1)}, u32[]{:S(2)}, u32[]{:S(2)}) collective-permute-start(f32[16,64,128]{2,1,0:T(8,128)S(1)} %get-tuple-element.118), channel_id=1, source_target_pairs={{0,2},{2,4},{4,6},{6,8},{8,10},{10,12},{12,14},{14,16},{16,18},{18... | collective-permute-start | bytes 1572872 | tf_op jit(solution)/shard_map/ppermute | solution.py:355
  4.6 4.5 %collective-permute-start = (f32[16,64,128]{2,1,0:T(8,128)S(1)}, f32[16,64,128]{2,1,0:T(8,128)S(1)}, u32[]{:S(2)}, u32[]{:S(2)}) collective-permute-start(f32[16,64,128]{2,1,0:T(8,128)S(1)} %get-tuple-element.119), channel_id=1, source_target_pairs={{0,2},{2,4},{4,6},{6,8},{8,10},{10,12},{12,14},{14,16},{16,18},{18... | collective-permute-start | bytes 1572872 | tf_op jit(solution)/shard_map/ppermute | solution.py:355
  9.2 0.9 %copy-done.2 = f32[64,16,3,3,3]{0,1,4,3,2:T(8,128)S(1)} copy-done((f32[64,16,3,3,3]{0,1,4,3,2:T(8,128)S(1)}, f32[64,16,3,3,3]{0,1,4,3,2:T(8,128)}, u32[]{:S(2)}) %copy-start.2) | copy-done | bytes 110616
  10.1 2.0 %own.2 = (bf16[128,2048]{1,0:T(8,128)(2,1)S(1)}, bf16[128,2048]{1,0:T(8,128)(2,1)S(1)}, f32[64,2048]{1,0:T(8,128)S(1)}, bf16[256,384]{1,0:T(8,128)(2,1)S(1)}, bf...) custom-call(f32[4096,128]{1,0:T(8,128)S(1)} %bitcast.19, f32[432,64]{1,0:T(8,128)S(1)} %bitcast.24), custom_call_target="tpu_custom_call" | custom-call | bytes 792 | tf_op jit(solution)/shard_map/own/pallas_call | solution.py:334
  12.1 1.4 %halo.2 = (bf16[64,2048]{1,0:T(8,128)(2,1)S(1)}, bf16[64,2048]{1,0:T(8,128)(2,1)S(1)}, f32[32,2048]{1,0:T(8,128)S(1)}, f32[32,2048]{1,0:T(8,128)S(1)}, f32[64,128]{1,0:T(8,128)S(1)}) custom-call(f32[1024,128]{1,0:T(8,128)S(1)} %bitcast.23, f32[64,2048]{1,0:T(8,128)S(1)} %get-tuple-element.61.refs_1_, bf16[256,192]{1,0:T(8,128)(2,1)S(1)} %get-tuple-element.60.refs_2_), custom_call_target="tpu_custom_call" | custom-call | bytes 612 | tf_op jit(solution)/shard_map/halo/pallas_call | solution.py:334
  13.5 1.6 %collective-permute-start.2 = (f32[32,2048]{1,0:T(8,128)S(1)}, f32[32,2048]{1,0:T(8,128)S(1)}, u32[]{:S(2)}, u32[]{:S(2)}) collective-permute-start(f32[32,2048]{1,0:T(8,128)S(1)} %get-tuple-element.65), channel_id=1, source_target_pairs={{0,1},{1,0},{2,3},{3,2},{4,5},{5,4},{6,7},{7,6},{8,9},{9,8},{10,11... | collective-permute-start | bytes 786440 | tf_op jit(solution)/shard_map/ppermute | solution.py:349
  15.6 2.0 %own.3 = (bf16[128,2048]{1,0:T(8,128)(2,1)S(1)}, bf16[128,2048]{1,0:T(8,128)(2,1)S(1)}, f32[64,2048]{1,0:T(8,128)S(1)}) custom-call(f32[4096,128]{1,0:T(8,128)S(1)} %bitcast.20, bf16[256,384]{1,0:T(8,128)(2,1)S(1)} %get-tuple-element.57.refs_0_, f32[64,128]{1,0:T(8,128)S(1)} %get-tuple-element.58.refs_1_), custom_call_target="tpu_custom_call" | custom-call | bytes 576 | tf_op jit(solution)/shard_map/own/pallas_call | solution.py:334
  17.6 1.3 %halo.3 = (bf16[64,2048]{1,0:T(8,128)(2,1)S(1)}, bf16[64,2048]{1,0:T(8,128)(2,1)S(1)}, f32[32,2048]{1,0:T(8,128)S(1)}, f32[32,2048]{1,0:T(8,128)S(1)}) custom-call(f32[1024,128]{1,0:T(8,128)S(1)} %bitcast.22, f32[64,2048]{1,0:T(8,128)S(1)} %get-tuple-element.59.refs_1_, bf16[256,192]{1,0:T(8,128)(2,1)S(1)} %get-tuple-element.60.refs_2_, ...), custom_call_target="tpu_custom_call" | custom-call | bytes 612 | tf_op jit(solution)/shard_map/halo/pallas_call | solution.py:334
  19.5 2.9 %collective-permute-done.2 = f32[32,2048]{1,0:T(8,128)S(1)} collective-permute-done((f32[32,2048]{1,0:T(8,128)S(1)}, f32[32,2048]{1,0:T(8,128)S(1)}, u32[]{:S(2)}, u32[]{:S(2)}) %collective-permute-start.2) | collective-permute-done | bytes 262176 | tf_op jit(solution)/shard_map/ppermute | solution.py:349
  22.6 1.3 %collective-permute-start.6 = (f32[32,2048]{1,0:T(8,128)S(1)}, f32[32,2048]{1,0:T(8,128)S(1)}, u32[]{:S(2)}, u32[]{:S(2)}) collective-permute-start(f32[32,2048]{1,0:T(8,128)S(1)} %get-tuple-element.92.refs_0_), channel_id=1, source_target_pairs={{2,0},{4,2},{6,4},{8,6},{10,8},{12,10},{14,12},{16,14},{18,16},{20... | collective-permute-start | bytes 786440 | tf_op jit(solution)/shard_map/ppermute | solution.py:355
  23.9 1.5 %collective-permute-start.4 = (f32[32,2048]{1,0:T(8,128)S(1)}, f32[32,2048]{1,0:T(8,128)S(1)}, u32[]{:S(2)}, u32[]{:S(2)}) collective-permute-start(f32[32,2048]{1,0:T(8,128)S(1)} %get-tuple-element.92.refs_0_), channel_id=1, source_target_pairs={{0,1},{1,0},{2,3},{3,2},{4,5},{5,4},{6,7},{7,6},{8,9},{9,8},{10,11... | collective-permute-start | bytes 786440 | tf_op jit(solution)/shard_map/ppermute | solution.py:349
  25.4 1.6 %activation.2.refs_0_ = f32[2048,64]{1,0:T(8,128)} custom-call(f32[32,2048]{1,0:T(8,128)S(1)} %get-tuple-element.117.chunk), custom_call_target="tpu_custom_call" | custom-call | bytes 360 | tf_op jit(solution)/shard_map/activation/pallas_call | solution.py:334
  27.0 1.1 %collective-permute-done.3 = f32[32,2048]{1,0:T(8,128)S(1)} collective-permute-done((f32[32,2048]{1,0:T(8,128)S(1)}, f32[32,2048]{1,0:T(8,128)S(1)}, u32[]{:S(2)}, u32[]{:S(2)}) %collective-permute-start.3) | collective-permute-done | bytes 262176 | tf_op jit(solution)/shard_map/ppermute | solution.py:349
  28.2 1.3 %collective-permute-start.7 = (f32[32,2048]{1,0:T(8,128)S(1)}, f32[32,2048]{1,0:T(8,128)S(1)}, u32[]{:S(2)}, u32[]{:S(2)}) collective-permute-start(f32[32,2048]{1,0:T(8,128)S(1)} %get-tuple-element.94.refs_2_), channel_id=1, source_target_pairs={{2,0},{4,2},{6,4},{8,6},{10,8},{12,10},{14,12},{16,14},{18,16},{20... | collective-permute-start | bytes 786440 | tf_op jit(solution)/shard_map/ppermute | solution.py:355
  29.5 1.5 %collective-permute-start.5 = (f32[32,2048]{1,0:T(8,128)S(1)}, f32[32,2048]{1,0:T(8,128)S(1)}, u32[]{:S(2)}, u32[]{:S(2)}) collective-permute-start(f32[32,2048]{1,0:T(8,128)S(1)} %get-tuple-element.94.refs_2_), channel_id=1, source_target_pairs={{0,1},{1,0},{2,3},{3,2},{4,5},{5,4},{6,7},{7,6},{8,9},{9,8},{10,11... | collective-permute-start | bytes 786440 | tf_op jit(solution)/shard_map/ppermute | solution.py:349
  31.0 2.7 %collective-permute-done.4.refs_1_ = f32[32,2048]{1,0:T(8,128)S(1)} collective-permute-done((f32[32,2048]{1,0:T(8,128)S(1)}, f32[32,2048]{1,0:T(8,128)S(1)}, u32[]{:S(2)}, u32[]{:S(2)}) %collective-permute-start.4) | collective-permute-done | bytes 262176 | tf_op jit(solution)/shard_map/ppermute | solution.py:349
  33.7 1.3 %collective-permute-start.8 = (f32[32,2048]{1,0:T(8,128)S(1)}, f32[32,2048]{1,0:T(8,128)S(1)}, u32[]{:S(2)}, u32[]{:S(2)}) collective-permute-start(f32[32,2048]{1,0:T(8,128)S(1)} %collective-permute-done.4.refs_1_), channel_id=1, source_target_pairs={{2,0},{4,2},{6,4},{8,6},{10,8},{12,10},{14,12},{16,14},{18,16},{20... | collective-permute-start | bytes 786440 | tf_op jit(solution)/shard_map/ppermute | solution.py:355
  35.0 1.4 %filter.2.refs_12_ = f32[192,256]{1,0:T(8,128)S(1)} custom-call(f32[32,2048]{1,0:T(8,128)S(1)} %get-tuple-element.92.refs_0_, f32[32,2048]{1,0:T(8,128)S(1)} %collective-permute-done.4.refs_1_, bf16[128,2048]{1,0:T(8,128)(2,1)S(1)} %get-tuple-element.70.refs_2_.refs_4_, bf16[128,2048]{1,0:T(8,128)(2,1)S(1)} %get-tuple-element.71.refs_3_.refs_5_, ...), custom_call_target="tpu_custom_call" | custom-call | bytes 576 | tf_op jit(solution)/shard_map/filter/pallas_call | solution.py:334
  36.4 2.9 %collective-permute-done.5.refs_3_ = f32[32,2048]{1,0:T(8,128)S(1)} collective-permute-done((f32[32,2048]{1,0:T(8,128)S(1)}, f32[32,2048]{1,0:T(8,128)S(1)}, u32[]{:S(2)}, u32[]{:S(2)}) %collective-permute-start.5) | collective-permute-done | bytes 262176 | tf_op jit(solution)/shard_map/ppermute | solution.py:349
  39.3 1.5 %collective-permute-start.9 = (f32[32,2048]{1,0:T(8,128)S(1)}, f32[32,2048]{1,0:T(8,128)S(1)}, u32[]{:S(2)}, u32[]{:S(2)}) collective-permute-start(f32[32,2048]{1,0:T(8,128)S(1)} %collective-permute-done.5.refs_3_), channel_id=1, source_target_pairs={{2,0},{4,2},{6,4},{8,6},{10,8},{12,10},{14,12},{16,14},{18,16},{20... | collective-permute-start | bytes 786440 | tf_op jit(solution)/shard_map/ppermute | solution.py:355
  40.8 1.7 %filter.3 = (f32[112,128]{1,0:T(8,128)S(1)}, f32[112,128]{1,0:T(8,128)S(1)}) custom-call(f32[32,2048]{1,0:T(8,128)S(1)} %get-tuple-element.92.refs_0_, f32[32,2048]{1,0:T(8,128)S(1)} %collective-permute-done.4.refs_1_, f32[32,2048]{1,0:T(8,128)S(1)} %get-tuple-element.94.refs_2_, f32[32,2048]{1,0:T(8,128)S(1)} %collective-permute-done.5.refs_3_, ...), custom_call_target="tpu_custom_call" | custom-call | bytes 576 | tf_op jit(solution)/shard_map/filter/pallas_call | solution.py:334
  42.5 1.2 %collective-permute-start.10 = (f32[112,128]{1,0:T(8,128)S(1)}, f32[112,128]{1,0:T(8,128)S(1)}, u32[]{:S(2)}, u32[]{:S(2)}) collective-permute-start(f32[112,128]{1,0:T(8,128)S(1)} %get-tuple-element.84), channel_id=1, source_target_pairs={{0,2},{2,0},{4,6},{6,4},{8,10},{10,8},{12,14},{14,12},{16,18},{18,... | collective-permute-start | bytes 172040 | tf_op jit(solution)/shard_map/ppermute | solution.py:363
  43.7 0.9 %collective-permute-done.10 = f32[112,128]{1,0:T(8,128)S(1)} collective-permute-done((f32[112,128]{1,0:T(8,128)S(1)}, f32[112,128]{1,0:T(8,128)S(1)}, u32[]{:S(2)}, u32[]{:S(2)}) %collective-permute-start.10) | collective-permute-done | bytes 57376 | tf_op jit(solution)/shard_map/ppermute | solution.py:363
  44.6 2.1 %collective-permute-start.11 = (f32[112,128]{1,0:T(8,128)S(1)}, f32[112,128]{1,0:T(8,128)S(1)}, u32[]{:S(2)}, u32[]{:S(2)}) collective-permute-start(f32[112,128]{1,0:T(8,128)S(1)} %add.28), channel_id=1, source_target_pairs={{0,4},{2,6},{4,0},{6,2},{8,12},{10,14},{12,8},{14,10},{16,20},{18,... | collective-permute-start | bytes 172040 | tf_op jit(solution)/shard_map/ppermute | solution.py:363
  46.6 3.3 %back.2.refs_9_ = f32[4096,128]{1,0:T(8,128)} custom-call(f32[32,2048]{1,0:T(8,128)S(1)} %get-tuple-element.92.refs_0_, f32[32,2048]{1,0:T(8,128)S(1)} %collective-permute-done.4.refs_1_, f32[32,2048]{1,0:T(8,128)S(1)} %collective-permute-done.6.refs_2_.refs_4_, f32[32,2048]{1,0:T(8,128)S(1)} %collective-permute-done.8.refs_3_.refs_5_, ...), custom_call_target="tpu_custom_call" | custom-call | bytes 900 | tf_op jit(solution)/shard_map/back/pallas_call | solution.py:334
  49.9 1.6 %collective-permute-start.12 = (f32[112,128]{1,0:T(8,128)S(1)}, f32[112,128]{1,0:T(8,128)S(1)}, u32[]{:S(2)}, u32[]{:S(2)}) collective-permute-start(f32[112,128]{1,0:T(8,128)S(1)} %add.29), channel_id=1, source_target_pairs={{0,8},{2,10},{4,12},{6,14},{8,0},{10,2},{12,4},{14,6},{16,24},{18,... | collective-permute-start | bytes 172040 | tf_op jit(solution)/shard_map/ppermute | solution.py:363
  51.6 4.0 %back.3 = f32[4096,128]{1,0:T(8,128)} custom-call(f32[32,2048]{1,0:T(8,128)S(1)} %get-tuple-element.92.refs_0_, f32[32,2048]{1,0:T(8,128)S(1)} %collective-permute-done.4.refs_1_, f32[32,2048]{1,0:T(8,128)S(1)} %get-tuple-element.94.refs_2_, f32[32,2048]{1,0:T(8,128)S(1)} %collective-permute-done.5.refs_3_, ...), custom_call_target="tpu_custom_call", output_to_operand_aliasing={{}: (9, {})} | custom-call | bytes 900 | tf_op jit(solution)/shard_map/back/pallas_call | solution.py:334
  55.6 3.2 %collective-permute-start.13 = (f32[112,128]{1,0:T(8,128)S(1)}, f32[112,128]{1,0:T(8,128)S(1)}, u32[]{:S(2)}, u32[]{:S(2)}) collective-permute-start(f32[112,128]{1,0:T(8,128)S(1)} %add.30), channel_id=1, source_target_pairs={{0,16},{2,18},{4,20},{6,22},{8,24},{10,26},{12,28},{14,30},{16,0},... | collective-permute-start | bytes 172040 | tf_op jit(solution)/shard_map/ppermute | solution.py:363
  58.8 1.6 %activation.3 = f32[2048,64]{1,0:T(8,128)} custom-call(f32[32,2048]{1,0:T(8,128)S(1)} %get-tuple-element.103.chunk, f32[2048,64]{1,0:T(8,128)} %activation.2.refs_0_), custom_call_target="tpu_custom_call", output_to_operand_aliasing={{}: (1, {})} | custom-call | bytes 360 | tf_op jit(solution)/shard_map/activation/pallas_call | solution.py:334
  60.4 1.2 %collective-permute-done.13 = f32[112,128]{1,0:T(8,128)S(1)} collective-permute-done((f32[112,128]{1,0:T(8,128)S(1)}, f32[112,128]{1,0:T(8,128)S(1)}, u32[]{:S(2)}, u32[]{:S(2)}) %collective-permute-start.13) | collective-permute-done | bytes 57376 | tf_op jit(solution)/shard_map/ppermute | solution.py:363
  61.7 1.2 %collective-permute-done.14 = f32[112,128]{1,0:T(8,128)S(1)} collective-permute-done((f32[112,128]{1,0:T(8,128)S(1)}, f32[112,128]{1,0:T(8,128)S(1)}, u32[]{:S(2)}, u32[]{:S(2)}) %collective-permute-start.14) | collective-permute-done | bytes 57376 | tf_op jit(solution)/shard_map/ppermute | solution.py:363
  (26 shorter events, 2.4 us)
Async XLA Ops:
  0.6 8.5 %copy-start = (f32[16,2,128,128]{3,2,1,0:T(8,128)S(1)}, f32[16,2,128,128]{3,2,1,0:T(8,128)}, u32[]{:S(2)}) copy-start(f32[16,2,128,128]{3,2,1,0:T(8,128)} %param.3) | copy-start | bytes 6291460
  2.1 12.9 %copy-start.1 = (f32[32,1,64,64]{3,2,1,0:T(8,128)S(1)}, f32[32,1,64,64]{3,2,1,0:T(8,128)}, u32[]{:S(2)}) copy-start(f32[32,1,64,64]{3,2,1,0:T(8,128)} %param.5) | copy-start | bytes 1572868
  2.1 10.0 %collective-permute-start.1 = (f32[16,64,128]{2,1,0:T(8,128)S(1)}, f32[16,64,128]{2,1,0:T(8,128)S(1)}, u32[]{:S(2)}, u32[]{:S(2)}) collective-permute-start(f32[16,64,128]{2,1,0:T(8,128)S(1)} %get-tuple-element.118), channel_id=1, source_target_pairs={{0,2},{2,4},{4,6},{6,8},{8,10},{10,12},{12,14},{14,16},{16,18},{18... | collective-permute-start | bytes 1572872 | tf_op jit(solution)/shard_map/ppermute | solution.py:355
  4.6 13.0 %collective-permute-start = (f32[16,64,128]{2,1,0:T(8,128)S(1)}, f32[16,64,128]{2,1,0:T(8,128)S(1)}, u32[]{:S(2)}, u32[]{:S(2)}) collective-permute-start(f32[16,64,128]{2,1,0:T(8,128)S(1)} %get-tuple-element.119), channel_id=1, source_target_pairs={{0,2},{2,4},{4,6},{6,8},{8,10},{10,12},{12,14},{14,16},{16,18},{18... | collective-permute-start | bytes 1572872 | tf_op jit(solution)/shard_map/ppermute | solution.py:355
  9.2 0.9 %copy-start.2 = (f32[64,16,3,3,3]{0,1,4,3,2:T(8,128)S(1)}, f32[64,16,3,3,3]{0,1,4,3,2:T(8,128)}, u32[]{:S(2)}) copy-start(f32[64,16,3,3,3]{0,1,4,3,2:T(8,128)} %param.4) | copy-start | bytes 331780
  13.5 9.0 %collective-permute-start.2 = (f32[32,2048]{1,0:T(8,128)S(1)}, f32[32,2048]{1,0:T(8,128)S(1)}, u32[]{:S(2)}, u32[]{:S(2)}) collective-permute-start(f32[32,2048]{1,0:T(8,128)S(1)} %get-tuple-element.65), channel_id=1, source_target_pairs={{0,1},{1,0},{2,3},{3,2},{4,5},{5,4},{6,7},{7,6},{8,9},{9,8},{10,11... | collective-permute-start | bytes 786440 | tf_op jit(solution)/shard_map/ppermute | solution.py:349
  18.9 9.2 %collective-permute-start.3 = (f32[32,2048]{1,0:T(8,128)S(1)}, f32[32,2048]{1,0:T(8,128)S(1)}, u32[]{:S(2)}, u32[]{:S(2)}) collective-permute-start(f32[32,2048]{1,0:T(8,128)S(1)} %get-tuple-element.67), channel_id=1, source_target_pairs={{0,1},{1,0},{2,3},{3,2},{4,5},{5,4},{6,7},{7,6},{8,9},{9,8},{10,11... | collective-permute-start | bytes 786440 | tf_op jit(solution)/shard_map/ppermute | solution.py:349
  22.6 12.4 %collective-permute-start.6 = (f32[32,2048]{1,0:T(8,128)S(1)}, f32[32,2048]{1,0:T(8,128)S(1)}, u32[]{:S(2)}, u32[]{:S(2)}) collective-permute-start(f32[32,2048]{1,0:T(8,128)S(1)} %get-tuple-element.92.refs_0_), channel_id=1, source_target_pairs={{2,0},{4,2},{6,4},{8,6},{10,8},{12,10},{14,12},{16,14},{18,16},{20... | collective-permute-start | bytes 786440 | tf_op jit(solution)/shard_map/ppermute | solution.py:355
  23.9 9.8 %collective-permute-start.4 = (f32[32,2048]{1,0:T(8,128)S(1)}, f32[32,2048]{1,0:T(8,128)S(1)}, u32[]{:S(2)}, u32[]{:S(2)}) collective-permute-start(f32[32,2048]{1,0:T(8,128)S(1)} %get-tuple-element.92.refs_0_), channel_id=1, source_target_pairs={{0,1},{1,0},{2,3},{3,2},{4,5},{5,4},{6,7},{7,6},{8,9},{9,8},{10,11... | collective-permute-start | bytes 786440 | tf_op jit(solution)/shard_map/ppermute | solution.py:349
  28.2 8.2 %collective-permute-start.7 = (f32[32,2048]{1,0:T(8,128)S(1)}, f32[32,2048]{1,0:T(8,128)S(1)}, u32[]{:S(2)}, u32[]{:S(2)}) collective-permute-start(f32[32,2048]{1,0:T(8,128)S(1)} %get-tuple-element.94.refs_2_), channel_id=1, source_target_pairs={{2,0},{4,2},{6,4},{8,6},{10,8},{12,10},{14,12},{16,14},{18,16},{20... | collective-permute-start | bytes 786440 | tf_op jit(solution)/shard_map/ppermute | solution.py:355
  29.5 9.8 %collective-permute-start.5 = (f32[32,2048]{1,0:T(8,128)S(1)}, f32[32,2048]{1,0:T(8,128)S(1)}, u32[]{:S(2)}, u32[]{:S(2)}) collective-permute-start(f32[32,2048]{1,0:T(8,128)S(1)} %get-tuple-element.94.refs_2_), channel_id=1, source_target_pairs={{0,1},{1,0},{2,3},{3,2},{4,5},{5,4},{6,7},{7,6},{8,9},{9,8},{10,11... | collective-permute-start | bytes 786440 | tf_op jit(solution)/shard_map/ppermute | solution.py:349
  33.7 10.8 %collective-permute-start.8 = (f32[32,2048]{1,0:T(8,128)S(1)}, f32[32,2048]{1,0:T(8,128)S(1)}, u32[]{:S(2)}, u32[]{:S(2)}) collective-permute-start(f32[32,2048]{1,0:T(8,128)S(1)} %collective-permute-done.4.refs_1_), channel_id=1, source_target_pairs={{2,0},{4,2},{6,4},{8,6},{10,8},{12,10},{14,12},{16,14},{18,16},{20... | collective-permute-start | bytes 786440 | tf_op jit(solution)/shard_map/ppermute | solution.py:355
  39.3 10.6 %collective-permute-start.9 = (f32[32,2048]{1,0:T(8,128)S(1)}, f32[32,2048]{1,0:T(8,128)S(1)}, u32[]{:S(2)}, u32[]{:S(2)}) collective-permute-start(f32[32,2048]{1,0:T(8,128)S(1)} %collective-permute-done.5.refs_3_), channel_id=1, source_target_pairs={{2,0},{4,2},{6,4},{8,6},{10,8},{12,10},{14,12},{16,14},{18,16},{20... | collective-permute-start | bytes 786440 | tf_op jit(solution)/shard_map/ppermute | solution.py:355
  42.5 2.1 %collective-permute-start.10 = (f32[112,128]{1,0:T(8,128)S(1)}, f32[112,128]{1,0:T(8,128)S(1)}, u32[]{:S(2)}, u32[]{:S(2)}) collective-permute-start(f32[112,128]{1,0:T(8,128)S(1)} %get-tuple-element.84), channel_id=1, source_target_pairs={{0,2},{2,0},{4,6},{6,4},{8,10},{10,8},{12,14},{14,12},{16,18},{18,... | collective-permute-start | bytes 172040 | tf_op jit(solution)/shard_map/ppermute | solution.py:363
  44.6 5.4 %collective-permute-start.11 = (f32[112,128]{1,0:T(8,128)S(1)}, f32[112,128]{1,0:T(8,128)S(1)}, u32[]{:S(2)}, u32[]{:S(2)}) collective-permute-start(f32[112,128]{1,0:T(8,128)S(1)} %add.28), channel_id=1, source_target_pairs={{0,4},{2,6},{4,0},{6,2},{8,12},{10,14},{12,8},{14,10},{16,20},{18,... | collective-permute-start | bytes 172040 | tf_op jit(solution)/shard_map/ppermute | solution.py:363
  49.9 5.6 %collective-permute-start.12 = (f32[112,128]{1,0:T(8,128)S(1)}, f32[112,128]{1,0:T(8,128)S(1)}, u32[]{:S(2)}, u32[]{:S(2)}) collective-permute-start(f32[112,128]{1,0:T(8,128)S(1)} %add.29), channel_id=1, source_target_pairs={{0,8},{2,10},{4,12},{6,14},{8,0},{10,2},{12,4},{14,6},{16,24},{18,... | collective-permute-start | bytes 172040 | tf_op jit(solution)/shard_map/ppermute | solution.py:363
  55.6 6.0 %collective-permute-start.13 = (f32[112,128]{1,0:T(8,128)S(1)}, f32[112,128]{1,0:T(8,128)S(1)}, u32[]{:S(2)}, u32[]{:S(2)}) collective-permute-start(f32[112,128]{1,0:T(8,128)S(1)} %add.30), channel_id=1, source_target_pairs={{0,16},{2,18},{4,20},{6,22},{8,24},{10,26},{12,28},{14,30},{16,0},... | collective-permute-start | bytes 172040 | tf_op jit(solution)/shard_map/ppermute | solution.py:363
  61.6 1.3 %collective-permute-start.14 = (f32[112,128]{1,0:T(8,128)S(1)}, f32[112,128]{1,0:T(8,128)S(1)}, u32[]{:S(2)}, u32[]{:S(2)}) collective-permute-start(f32[112,128]{1,0:T(8,128)S(1)} %add.31), channel_id=1, source_target_pairs={{0,2},{2,0},{4,6},{6,4},{8,10},{10,8},{12,14},{14,12},{16,18},{18,... | collective-permute-start | bytes 172040 | tf_op jit(solution)/shard_map/ppermute | solution.py:363

commit v5 on v4

--- a/solution.py
+++ b/solution.py
@@ -12,7 +12,7 @@
 LANES = 128
 STEP = 8
 CHUNKS = 2
-BACK = (14,)
+BACK = (8, 22)
 VMEM = pl.BlockSpec(memory_space=pltpu.VMEM)
 ANY = pl.BlockSpec(memory_space=pl.ANY)
 
@@ -100,17 +100,18 @@
     return split(jnp.concatenate(pieces, axis=1))
 
 
-def gather_grads(pieces, scratch, own, count):
+def gather_grads(pieces, scratch, own, count, begin, end):
     me = lax.axis_index("chan")
-    left = 0
-    for chunk in range(len(pieces) // count):
+    per = pieces[0].shape[1] // LANES
+    chunks = len(pieces) // count
+    for chunk in range(chunks):
+        low, high = max(begin, chunk * per), min(end, (chunk + 1) * per)
         for k in range(count):
+            start = pl.multiple_of(lax.rem(me + count - k, count) * own, own)
             piece = pieces[chunk * count + k]
-            start = pl.multiple_of(lax.rem(me + count - k, count) * own, own)
-            scratch[pl.ds(start, own), left : left + piece.shape[1]] = piece[...]
-        left += piece.shape[1]
-    if left < scratch.shape[1]:
-        scratch[:, left:] = jnp.zeros((scratch.shape[0], scratch.shape[1] - left), F32)
+            scratch[pl.ds(start, own), group(low - begin, high - low)] = piece[:, group(low - chunk * per, high - low)]
+    if end > chunks * per:
+        scratch[:, group(chunks * per - begin)] = jnp.zeros((scratch.shape[0], LANES), F32)
 
 
 def own_kernel(dims, chunk, vol, *refs):
@@ -205,10 +206,10 @@
     if chunk:
         before, refs = refs[0], refs[1:]
     *out, total, g_all = refs
-    gather_grads(pieces, g_all, own, count)
     base = (chunk - loaded + 1) * per
     begin = chunk * per - (1 if chunk else 0)
     end = (chunk + 1) * per - (0 if last else 1)
+    gather_grads(pieces, g_all, own, count, begin - base, end + 1 - base)
     total[...] = before[...] if chunk else jnp.zeros_like(total)
 
     def cells_of(sources, part, first, size):
@@ -223,7 +224,7 @@
     first = begin
     while first < end:
         size = min(STEP, end - first)
-        hi, lo = grad_shifts(lambda g: g_all[:, group(g - base)], first, size, outs, half)
+        hi, lo = grad_shifts(lambda g: g_all[:, group(g - begin)], first, size, outs, half)
         a_hi, a_lo = [
             jnp.concatenate([cells_of(v, part, first, size) for v in (halos, planes_x)], axis=0) for part in range(2)
         ]
@@ -262,16 +263,17 @@
     here, above = refs[: loaded * count], refs[loaded * count : 2 * loaded * count]
     weights = refs[2 * loaded * count][...]
     out, g_here, g_above, grown, sem = refs[-5:]
-    gather_grads(here, g_here, own, count)
-    gather_grads(above, g_above, own, count)
     base = low * (height // 4 // CHUNKS)
+    gather_grads(here, g_here, own, count, begin - base, end + 1 - base)
+    gather_grads(above, g_above, own, count, begin - base, end + 1 - base)
+    flat = grown.reshape(chans * planes * height, LANES)
     matrix = pairing(half, True)
     matrix = jnp.concatenate([matrix, matrix], axis=0)
     first = begin
     while first < end:
         size = min(STEP, end - first)
-        hi, lo = grad_shifts(lambda g: g_here[:, group(g - base)], first, size, outs, half)
-        hi_above, lo_above = grad_shifts(lambda g: g_above[:, group(g - base)], first, size, outs, half)
+        hi, lo = grad_shifts(lambda g: g_here[:, group(g - begin)], first, size, outs, half)
+        hi_above, lo_above = grad_shifts(lambda g: g_above[:, group(g - begin)], first, size, outs, half)
         grad = jnp.dot(
             weights,
             jnp.concatenate([hi, lo, hi, hi_above, lo_above, hi_above], axis=0),
@@ -289,17 +291,14 @@
                 start = (parity * size + j) * chans
                 row = (parity // 2) * height + 4 * (first + j) + parity % 2
                 for side in range(2):
-                    grown[pl.ds(row + 2 * side, chans, stride=planes * height), :] = rows[
+                    flat[pl.ds(row + 2 * side, chans, stride=planes * height), :] = rows[
                         start : start + chans, group(side)
                     ]
         first += size
-    copies = []
-    for i in range(chans * planes):
-        part = pl.ds(i * height + 4 * begin, 4 * (end - begin))
-        copies.append(pltpu.make_async_copy(grown.at[part, :], out.at[part, :], sem.at[i]))
-        copies[-1].start()
-    for copy in copies:
-        copy.wait()
+    part = pl.ds(4 * begin, 4 * (end - begin))
+    copy = pltpu.make_async_copy(grown.at[:, part, :], out.at[:, part, :], sem)
+    copy.start()
+    copy.wait()
 
 
 def flat_kernel(half, cube, flat):
@@ -478,7 +477,9 @@
             *early, summed[0] = lax.optimization_barrier((*[chunk[0] for chunk in above], summed[0]))
             for chunk, grad in zip(above, early):
                 chunk[0] = grad
-            *sent, summed[0] = lax.optimization_barrier((*grads[-1][1:], summed[0]))
+            shown, summed[0] = lax.optimization_barrier((preact, summed[0]))
+            activated = list(activate(CHUNKS - 1, shown, *activated))
+            *sent, summed[0], activated[0] = lax.optimization_barrier((*grads[-1][1:], summed[0], activated[0]))
             above[-1] += [from_behind(g, "space", -1) for g in sent]
         summed = call(
             functools.partial(filter_kernel, dims, own, count, h),
@@ -488,7 +489,7 @@
             ([pltpu.VMEM((14 * chans, LANES), F32)] if last else [])
             + [
                 pltpu.VMEM((12 * chans, 4 * outs), F32),
-                pltpu.VMEM((outs, (h - low + 1) * part_cells + (LANES if last else 0)), F32),
+                pltpu.VMEM((outs, part_cells + (LANES * (2 if last else 1) if h else 0)), F32),
             ],
             *sources,
             *x_own[2 * low : 2 * h + 2],
@@ -510,9 +511,9 @@
             functools.partial(back_kernel, dims, own, count, begin, end, low, high),
             "back",
             2.5,
-            [((chans * planes * height, width), F32)],
-            [pltpu.VMEM((outs, (high - low) * part_cells + (LANES if high == CHUNKS else 0)), F32)] * 2
-            + [pltpu.VMEM((chans * planes * height, width), F32), pltpu.SemaphoreType.DMA((chans * planes,))],
+            [((chans * planes, height, width), F32)],
+            [pltpu.VMEM((outs, (end + 1 - begin) * LANES), F32)] * 2
+            + [pltpu.VMEM((chans * planes, height, width), F32), pltpu.SemaphoreType.DMA],
             *sources,
             w_back,
             *state["grad"],
@@ -522,21 +523,15 @@
         return value
 
     def beside(index, value):
-        for started in ("grad", "activated"):
-            if state.get(started):
-                *state[started], value = lax.optimization_barrier((*state[started], value))
-        if state["done"] < len(cuts) - 1:
-            return rows_of_grad(value)
-        if "activated" not in state:
-            shown, value = lax.optimization_barrier((preact, value))
-            state["activated"] = list(activate(CHUNKS - 1, shown, *activated))
-        return value
+        if state["grad"]:
+            *state["grad"], value = lax.optimization_barrier((*state["grad"], value))
+        return rows_of_grad(value) if state["done"] < len(cuts) - 1 else value
 
     low, high = sum_over(*summed, "space", beside)
     while state["done"] < len(cuts) - 1:
         low = rows_of_grad(low)
     (volume_grad,) = state["grad"]
-    (activated,) = state.get("activated") or activate(CHUNKS - 1, preact, *activated)
+    (activated,) = activated
     volume_grad = volume_grad.reshape(chans, planes, height, width)[:real]
     depth_all = planes * lax.axis_size("space")
     factor = float(depth_all // 2 * (height // 2) * half) ** (-0.5)

time: 64.1 us -> 62.3 us (0.972)
  waiting for transfers between devices: 13.1 us -> 10.7 us
    ppermute x4, waiting for transfers between devices: 9.67 us -> 8.08 us  [turned(): lax.ppermute(value, axis, [(s, (s + steps) % count) for s in range(count)])]
    ppermute x5, waiting for transfers between devices: 3.36 us -> 2.57 us  [swapped(): return lax.ppermute(value, axis, [(s, s ^ bit) for s in range(count)])]
    pallas_call x11 -> x12, Pallas kernels: 20.7 us -> 20.9 us  [call(): pl.pallas_call(kernel, name=name, out_shape=[jax.ShapeDtypeStruct(s, t) f...]
  transfers between devices with their start and end apart: 15 -> 15, of which waited for: 7 -> 8; matrix products, arithmetic and copies ran while one was open for 0% -> 0% of each run, Pallas kernels for 32% -> 34%
where the time goes in v5:
time: 62.3 us; the launch traced here: 62 us
  starting transfers between devices  26.1 us (42%)
  Pallas kernels  20.9 us (34%)
  waiting for transfers between devices  10.7 us (17%)
  local copies, waits for them, and re-layouts  2.52 us (4%)
  other arithmetic  0.95 us (2%)
  between operations  0.89 us (1%)
    pallas_call x12, Pallas kernels, call(): pl.pallas_call(kernel, name=name, out_shape=[jax.ShapeDtypeStruct(s, t) f...  20.9 us
    ppermute x6, starting transfers between devices, from_behind(): lax.ppermute(value, axis, [(source, source + steps) for source in range(i...  12.4 us
    ppermute x5, starting transfers between devices, swapped(): return lax.ppermute(value, axis, [(s, s ^ bit) for s in range(count)])  8.54 us
    ppermute x4, waiting for transfers between devices, turned(): lax.ppermute(value, axis, [(s, (s + steps) % count) for s in range(count)])  8.08 us
    ppermute x4, starting transfers between devices, turned(): lax.ppermute(value, axis, [(s, (s + steps) % count) for s in range(count)])  5.19 us
    ppermute x5, waiting for transfers between devices, swapped(): return lax.ppermute(value, axis, [(s, s ^ bit) for s in range(count)])  2.57 us
    squeeze x1, local copies, waits for them, and re-layouts, on_device(): volume[:, -1, h * rows:(h + 1) * rows]  1.42 us
  transfers between devices with their start and end apart: 15, of which 8 were waited for; matrix products, arithmetic and copies ran while one was open for 0% of the time, Pallas kernels for 34%

profile of v5, /device:TPU:0, one launch (start us, length us, event | category | flops | bytes accessed | tf_op | source)
XLA Modules:
  0.0 62.0 jit_solution(3200388077330528834)
XLA Ops:
  0.6 1.4 %slice_bitcast_fusion = (f32[16,64,128]{2,1,0:T(8,128)S(1)}, f32[16,64,128]{2,1,0:T(8,128)S(1)}) fusion(f32[16,2,128,128]{3,2,1,0:T(8,128)} %param.3), kind=kLoop, calls=%fused_computation | loop fusion | bytes 2097152 | tf_op jit(solution)/shard_map/squeeze | solution.py:390
  2.1 2.5 %collective-permute-start.1 = (f32[16,64,128]{2,1,0:T(8,128)S(1)}, f32[16,64,128]{2,1,0:T(8,128)S(1)}, u32[]{:S(2)}, u32[]{:S(2)}) collective-permute-start(f32[16,64,128]{2,1,0:T(8,128)S(1)} %get-tuple-element.126), channel_id=1, source_target_pairs={{0,2},{2,4},{4,6},{6,8},{8,10},{10,12},{12,14},{14,16},{16,18},{18... | collective-permute-start | bytes 1572872 | tf_op jit(solution)/shard_map/ppermute | solution.py:354
  4.6 4.5 %collective-permute-start = (f32[16,64,128]{2,1,0:T(8,128)S(1)}, f32[16,64,128]{2,1,0:T(8,128)S(1)}, u32[]{:S(2)}, u32[]{:S(2)}) collective-permute-start(f32[16,64,128]{2,1,0:T(8,128)S(1)} %get-tuple-element.127), channel_id=1, source_target_pairs={{0,2},{2,4},{4,6},{6,8},{8,10},{10,12},{12,14},{14,16},{16,18},{18... | collective-permute-start | bytes 1572872 | tf_op jit(solution)/shard_map/ppermute | solution.py:354
  9.2 0.9 %copy-done.2 = f32[64,16,3,3,3]{0,1,4,3,2:T(8,128)S(1)} copy-done((f32[64,16,3,3,3]{0,1,4,3,2:T(8,128)S(1)}, f32[64,16,3,3,3]{0,1,4,3,2:T(8,128)}, u32[]{:S(2)}) %copy-start.2) | copy-done | bytes 110616
  10.1 2.0 %own.2 = (bf16[128,2048]{1,0:T(8,128)(2,1)S(1)}, bf16[128,2048]{1,0:T(8,128)(2,1)S(1)}, f32[64,2048]{1,0:T(8,128)S(1)}, bf16[256,384]{1,0:T(8,128)(2,1)S(1)}, bf...) custom-call(f32[4096,128]{1,0:T(8,128)S(1)} %bitcast.19, f32[432,64]{1,0:T(8,128)S(1)} %bitcast.24), custom_call_target="tpu_custom_call" | custom-call | bytes 792 | tf_op jit(solution)/shard_map/own/pallas_call | solution.py:333
  12.1 1.4 %halo.2 = (bf16[64,2048]{1,0:T(8,128)(2,1)S(1)}, bf16[64,2048]{1,0:T(8,128)(2,1)S(1)}, f32[32,2048]{1,0:T(8,128)S(1)}, f32[32,2048]{1,0:T(8,128)S(1)}, f32[64,128]{1,0:T(8,128)S(1)}) custom-call(f32[1024,128]{1,0:T(8,128)S(1)} %bitcast.23, f32[64,2048]{1,0:T(8,128)S(1)} %get-tuple-element.65.refs_1_, bf16[256,192]{1,0:T(8,128)(2,1)S(1)} %get-tuple-element.64.refs_2_), custom_call_target="tpu_custom_call" | custom-call | bytes 612 | tf_op jit(solution)/shard_map/halo/pallas_call | solution.py:333
  13.5 1.6 %collective-permute-start.2 = (f32[32,2048]{1,0:T(8,128)S(1)}, f32[32,2048]{1,0:T(8,128)S(1)}, u32[]{:S(2)}, u32[]{:S(2)}) collective-permute-start(f32[32,2048]{1,0:T(8,128)S(1)} %get-tuple-element.69), channel_id=1, source_target_pairs={{0,1},{1,0},{2,3},{3,2},{4,5},{5,4},{6,7},{7,6},{8,9},{9,8},{10,11... | collective-permute-start | bytes 786440 | tf_op jit(solution)/shard_map/ppermute | solution.py:348
  15.6 2.0 %own.3 = (bf16[128,2048]{1,0:T(8,128)(2,1)S(1)}, bf16[128,2048]{1,0:T(8,128)(2,1)S(1)}, f32[64,2048]{1,0:T(8,128)S(1)}) custom-call(f32[4096,128]{1,0:T(8,128)S(1)} %bitcast.20, bf16[256,384]{1,0:T(8,128)(2,1)S(1)} %get-tuple-element.61.refs_0_, f32[64,128]{1,0:T(8,128)S(1)} %get-tuple-element.62.refs_1_), custom_call_target="tpu_custom_call" | custom-call | bytes 576 | tf_op jit(solution)/shard_map/own/pallas_call | solution.py:333
  17.6 1.3 %halo.3 = (bf16[64,2048]{1,0:T(8,128)(2,1)S(1)}, bf16[64,2048]{1,0:T(8,128)(2,1)S(1)}, f32[32,2048]{1,0:T(8,128)S(1)}, f32[32,2048]{1,0:T(8,128)S(1)}) custom-call(f32[1024,128]{1,0:T(8,128)S(1)} %bitcast.22, f32[64,2048]{1,0:T(8,128)S(1)} %get-tuple-element.63.refs_1_, bf16[256,192]{1,0:T(8,128)(2,1)S(1)} %get-tuple-element.64.refs_2_, ...), custom_call_target="tpu_custom_call" | custom-call | bytes 612 | tf_op jit(solution)/shard_map/halo/pallas_call | solution.py:333
  19.5 2.9 %collective-permute-done.2 = f32[32,2048]{1,0:T(8,128)S(1)} collective-permute-done((f32[32,2048]{1,0:T(8,128)S(1)}, f32[32,2048]{1,0:T(8,128)S(1)}, u32[]{:S(2)}, u32[]{:S(2)}) %collective-permute-start.2) | collective-permute-done | bytes 262176 | tf_op jit(solution)/shard_map/ppermute | solution.py:348
  22.6 1.3 %collective-permute-start.5 = (f32[32,2048]{1,0:T(8,128)S(1)}, f32[32,2048]{1,0:T(8,128)S(1)}, u32[]{:S(2)}, u32[]{:S(2)}) collective-permute-start(f32[32,2048]{1,0:T(8,128)S(1)} %get-tuple-element.100.refs_0_), channel_id=1, source_target_pairs={{2,0},{4,2},{6,4},{8,6},{10,8},{12,10},{14,12},{16,14},{18,16},{20... | collective-permute-start | bytes 786440 | tf_op jit(solution)/shard_map/ppermute | solution.py:354
  23.9 1.5 %collective-permute-start.7 = (f32[32,2048]{1,0:T(8,128)S(1)}, f32[32,2048]{1,0:T(8,128)S(1)}, u32[]{:S(2)}, u32[]{:S(2)}) collective-permute-start(f32[32,2048]{1,0:T(8,128)S(1)} %get-tuple-element.100.refs_0_), channel_id=1, source_target_pairs={{0,1},{1,0},{2,3},{3,2},{4,5},{5,4},{6,7},{7,6},{8,9},{9,8},{10,11... | collective-permute-start | bytes 786440 | tf_op jit(solution)/shard_map/ppermute | solution.py:348
  25.4 1.6 %activation.2.refs_0_ = f32[2048,64]{1,0:T(8,128)} custom-call(f32[32,2048]{1,0:T(8,128)S(1)} %get-tuple-element.123.chunk), custom_call_target="tpu_custom_call" | custom-call | bytes 360 | tf_op jit(solution)/shard_map/activation/pallas_call | solution.py:333
  27.0 1.1 %collective-permute-done.3 = f32[32,2048]{1,0:T(8,128)S(1)} collective-permute-done((f32[32,2048]{1,0:T(8,128)S(1)}, f32[32,2048]{1,0:T(8,128)S(1)}, u32[]{:S(2)}, u32[]{:S(2)}) %collective-permute-start.3) | collective-permute-done | bytes 262176 | tf_op jit(solution)/shard_map/ppermute | solution.py:348
  28.2 1.3 %collective-permute-start.6 = (f32[32,2048]{1,0:T(8,128)S(1)}, f32[32,2048]{1,0:T(8,128)S(1)}, u32[]{:S(2)}, u32[]{:S(2)}) collective-permute-start(f32[32,2048]{1,0:T(8,128)S(1)} %get-tuple-element.111.refs_2_.refs_0_), channel_id=1, source_target_pairs={{2,0},{4,2},{6,4},{8,6},{10,8},{12,10},{14,12},{16,14},{18,16},{20... | collective-permute-start | bytes 786440 | tf_op jit(solution)/shard_map/ppermute | solution.py:354
  29.5 1.5 %collective-permute-start.4 = (f32[32,2048]{1,0:T(8,128)S(1)}, f32[32,2048]{1,0:T(8,128)S(1)}, u32[]{:S(2)}, u32[]{:S(2)}) collective-permute-start(f32[32,2048]{1,0:T(8,128)S(1)} %get-tuple-element.111.refs_2_.refs_0_), channel_id=1, source_target_pairs={{0,1},{1,0},{2,3},{3,2},{4,5},{5,4},{6,7},{7,6},{8,9},{9,8},{10,11... | collective-permute-start | bytes 786440 | tf_op jit(solution)/shard_map/ppermute | solution.py:348
  31.0 2.7 %collective-permute-done.7.refs_1_ = f32[32,2048]{1,0:T(8,128)S(1)} collective-permute-done((f32[32,2048]{1,0:T(8,128)S(1)}, f32[32,2048]{1,0:T(8,128)S(1)}, u32[]{:S(2)}, u32[]{:S(2)}) %collective-permute-start.7) | collective-permute-done | bytes 262176 | tf_op jit(solution)/shard_map/ppermute | solution.py:348
  33.7 1.3 %collective-permute-start.9 = (f32[32,2048]{1,0:T(8,128)S(1)}, f32[32,2048]{1,0:T(8,128)S(1)}, u32[]{:S(2)}, u32[]{:S(2)}) collective-permute-start(f32[32,2048]{1,0:T(8,128)S(1)} %collective-permute-done.7.refs_1_), channel_id=1, source_target_pairs={{2,0},{4,2},{6,4},{8,6},{10,8},{12,10},{14,12},{16,14},{18,16},{20... | collective-permute-start | bytes 786440 | tf_op jit(solution)/shard_map/ppermute | solution.py:354
  35.0 1.4 %filter.2.refs_12_ = f32[192,256]{1,0:T(8,128)S(1)} custom-call(f32[32,2048]{1,0:T(8,128)S(1)} %get-tuple-element.100.refs_0_, f32[32,2048]{1,0:T(8,128)S(1)} %collective-permute-done.7.refs_1_, bf16[128,2048]{1,0:T(8,128)(2,1)S(1)} %get-tuple-element.74.refs_2_.refs_4_, bf16[128,2048]{1,0:T(8,128)(2,1)S(1)} %get-tuple-element.75.refs_3_.refs_5_, ...), custom_call_target="tpu_custom_call" | custom-call | bytes 576 | tf_op jit(solution)/shard_map/filter/pallas_call | solution.py:333
  36.4 1.6 %activation.3 = f32[2048,64]{1,0:T(8,128)} custom-call(f32[32,2048]{1,0:T(8,128)S(1)} %get-tuple-element.80.chunk, f32[2048,64]{1,0:T(8,128)} %activation.2.refs_0_), custom_call_target="tpu_custom_call", output_to_operand_aliasing={{}: (1, {})} | custom-call | bytes 360 | tf_op jit(solution)/shard_map/activation/pallas_call | solution.py:333
  38.0 1.3 %collective-permute-done.4.refs_3_.refs_1_ = f32[32,2048]{1,0:T(8,128)S(1)} collective-permute-done((f32[32,2048]{1,0:T(8,128)S(1)}, f32[32,2048]{1,0:T(8,128)S(1)}, u32[]{:S(2)}, u32[]{:S(2)}) %collective-permute-start.4) | collective-permute-done | bytes 262176 | tf_op jit(solution)/shard_map/ppermute | solution.py:348
  39.3 1.5 %collective-permute-start.8 = (f32[32,2048]{1,0:T(8,128)S(1)}, f32[32,2048]{1,0:T(8,128)S(1)}, u32[]{:S(2)}, u32[]{:S(2)}) collective-permute-start(f32[32,2048]{1,0:T(8,128)S(1)} %collective-permute-done.4.refs_3_.refs_1_), channel_id=1, source_target_pairs={{2,0},{4,2},{6,4},{8,6},{10,8},{12,10},{14,12},{16,14},{18,16},{20... | collective-permute-start | bytes 786440 | tf_op jit(solution)/shard_map/ppermute | solution.py:354
  40.8 1.6 %filter.3 = (f32[112,128]{1,0:T(8,128)S(1)}, f32[112,128]{1,0:T(8,128)S(1)}) custom-call(f32[32,2048]{1,0:T(8,128)S(1)} %get-tuple-element.100.refs_0_, f32[32,2048]{1,0:T(8,128)S(1)} %collective-permute-done.7.refs_1_, f32[32,2048]{1,0:T(8,128)S(1)} %get-tuple-element.111.refs_2_.refs_0_, f32[32,2048]{1,0:T(8,128)S(1)} %collective-permute-done.4.refs_3_.refs_1_, ...), custom_call_target="tpu_custom_call" | custom-call | bytes 576 | tf_op jit(solution)/shard_map/filter/pallas_call | solution.py:333
  42.4 1.2 %collective-permute-start.10 = (f32[112,128]{1,0:T(8,128)S(1)}, f32[112,128]{1,0:T(8,128)S(1)}, u32[]{:S(2)}, u32[]{:S(2)}) collective-permute-start(f32[112,128]{1,0:T(8,128)S(1)} %get-tuple-element.92), channel_id=1, source_target_pairs={{0,2},{2,0},{4,6},{6,4},{8,10},{10,8},{12,14},{14,12},{16,18},{18,... | collective-permute-start | bytes 172040 | tf_op jit(solution)/shard_map/ppermute | solution.py:362
  43.6 0.9 %collective-permute-done.10 = f32[112,128]{1,0:T(8,128)S(1)} collective-permute-done((f32[112,128]{1,0:T(8,128)S(1)}, f32[112,128]{1,0:T(8,128)S(1)}, u32[]{:S(2)}, u32[]{:S(2)}) %collective-permute-start.10) | collective-permute-done | bytes 57376 | tf_op jit(solution)/shard_map/ppermute | solution.py:362
  44.5 2.1 %collective-permute-start.11 = (f32[112,128]{1,0:T(8,128)S(1)}, f32[112,128]{1,0:T(8,128)S(1)}, u32[]{:S(2)}, u32[]{:S(2)}) collective-permute-start(f32[112,128]{1,0:T(8,128)S(1)} %add.28), channel_id=1, source_target_pairs={{0,4},{2,6},{4,0},{6,2},{8,12},{10,14},{12,8},{14,10},{16,20},{18,... | collective-permute-start | bytes 172040 | tf_op jit(solution)/shard_map/ppermute | solution.py:362
  46.6 2.1 %back.3.refs_9_ = f32[32,128,128]{2,1,0:T(8,128)} custom-call(f32[32,2048]{1,0:T(8,128)S(1)} %get-tuple-element.100.refs_0_, f32[32,2048]{1,0:T(8,128)S(1)} %collective-permute-done.7.refs_1_, f32[32,2048]{1,0:T(8,128)S(1)} %collective-permute-done.5.refs_2_.refs_4_, f32[32,2048]{1,0:T(8,128)S(1)} %collective-permute-done.9.refs_3_.refs_5_, ...), custom_call_target="tpu_custom_call" | custom-call | bytes 900 | tf_op jit(solution)/shard_map/back/pallas_call | solution.py:333
  49.0 2.6 %collective-permute-start.12 = (f32[112,128]{1,0:T(8,128)S(1)}, f32[112,128]{1,0:T(8,128)S(1)}, u32[]{:S(2)}, u32[]{:S(2)}) collective-permute-start(f32[112,128]{1,0:T(8,128)S(1)} %add.29), channel_id=1, source_target_pairs={{0,8},{2,10},{4,12},{6,14},{8,0},{10,2},{12,4},{14,6},{16,24},{18,... | collective-permute-start | bytes 172040 | tf_op jit(solution)/shard_map/ppermute | solution.py:362
  51.6 3.0 %back.4.refs_5_ = f32[32,128,128]{2,1,0:T(8,128)} custom-call(f32[32,2048]{1,0:T(8,128)S(1)} %get-tuple-element.100.refs_0_, f32[32,2048]{1,0:T(8,128)S(1)} %collective-permute-done.7.refs_1_, f32[32,2048]{1,0:T(8,128)S(1)} %get-tuple-element.111.refs_2_.refs_0_, ...), custom_call_target="tpu_custom_call", output_to_operand_aliasing={{}: (9, {})} | custom-call | bytes 900 | tf_op jit(solution)/shard_map/back/pallas_call | solution.py:333
  54.6 2.7 %collective-permute-start.13 = (f32[112,128]{1,0:T(8,128)S(1)}, f32[112,128]{1,0:T(8,128)S(1)}, u32[]{:S(2)}, u32[]{:S(2)}) collective-permute-start(f32[112,128]{1,0:T(8,128)S(1)} %add.30), channel_id=1, source_target_pairs={{0,16},{2,18},{4,20},{6,22},{8,24},{10,26},{12,28},{14,30},{16,0},... | collective-permute-start | bytes 172040 | tf_op jit(solution)/shard_map/ppermute | solution.py:362
  57.3 2.4 %back.5 = f32[32,128,128]{2,1,0:T(8,128)} custom-call(f32[32,2048]{1,0:T(8,128)S(1)} %get-tuple-element.111.refs_2_.refs_0_, f32[32,2048]{1,0:T(8,128)S(1)} %collective-permute-done.4.refs_3_.refs_1_, f32[32,2048]{1,0:T(8,128)S(1)} %collective-permute-done.6.refs_6_.refs_2_, ...), custom_call_target="tpu_custom_call", output_to_operand_aliasing={{}: (5, {})} | custom-call | bytes 900 | tf_op jit(solution)/shard_map/back/pallas_call | solution.py:333
  59.9 1.2 %collective-permute-done.14 = f32[112,128]{1,0:T(8,128)S(1)} collective-permute-done((f32[112,128]{1,0:T(8,128)S(1)}, f32[112,128]{1,0:T(8,128)S(1)}, u32[]{:S(2)}, u32[]{:S(2)}) %collective-permute-start.14) | collective-permute-done | bytes 57376 | tf_op jit(solution)/shard_map/ppermute | solution.py:362
  (27 shorter events, 2.8 us)
Async XLA Ops:
  0.6 8.5 %copy-start = (f32[16,2,128,128]{3,2,1,0:T(8,128)S(1)}, f32[16,2,128,128]{3,2,1,0:T(8,128)}, u32[]{:S(2)}) copy-start(f32[16,2,128,128]{3,2,1,0:T(8,128)} %param.3) | copy-start | bytes 6291460
  2.1 12.9 %copy-start.1 = (f32[32,1,64,64]{3,2,1,0:T(8,128)S(1)}, f32[32,1,64,64]{3,2,1,0:T(8,128)}, u32[]{:S(2)}) copy-start(f32[32,1,64,64]{3,2,1,0:T(8,128)} %param.5) | copy-start | bytes 1572868
  2.1 10.0 %collective-permute-start.1 = (f32[16,64,128]{2,1,0:T(8,128)S(1)}, f32[16,64,128]{2,1,0:T(8,128)S(1)}, u32[]{:S(2)}, u32[]{:S(2)}) collective-permute-start(f32[16,64,128]{2,1,0:T(8,128)S(1)} %get-tuple-element.126), channel_id=1, source_target_pairs={{0,2},{2,4},{4,6},{6,8},{8,10},{10,12},{12,14},{14,16},{16,18},{18... | collective-permute-start | bytes 1572872 | tf_op jit(solution)/shard_map/ppermute | solution.py:354
  4.6 13.0 %collective-permute-start = (f32[16,64,128]{2,1,0:T(8,128)S(1)}, f32[16,64,128]{2,1,0:T(8,128)S(1)}, u32[]{:S(2)}, u32[]{:S(2)}) collective-permute-start(f32[16,64,128]{2,1,0:T(8,128)S(1)} %get-tuple-element.127), channel_id=1, source_target_pairs={{0,2},{2,4},{4,6},{6,8},{8,10},{10,12},{12,14},{14,16},{16,18},{18... | collective-permute-start | bytes 1572872 | tf_op jit(solution)/shard_map/ppermute | solution.py:354
  9.2 0.9 %copy-start.2 = (f32[64,16,3,3,3]{0,1,4,3,2:T(8,128)S(1)}, f32[64,16,3,3,3]{0,1,4,3,2:T(8,128)}, u32[]{:S(2)}) copy-start(f32[64,16,3,3,3]{0,1,4,3,2:T(8,128)} %param.4) | copy-start | bytes 331780
  13.5 9.0 %collective-permute-start.2 = (f32[32,2048]{1,0:T(8,128)S(1)}, f32[32,2048]{1,0:T(8,128)S(1)}, u32[]{:S(2)}, u32[]{:S(2)}) collective-permute-start(f32[32,2048]{1,0:T(8,128)S(1)} %get-tuple-element.69), channel_id=1, source_target_pairs={{0,1},{1,0},{2,3},{3,2},{4,5},{5,4},{6,7},{7,6},{8,9},{9,8},{10,11... | collective-permute-start | bytes 786440 | tf_op jit(solution)/shard_map/ppermute | solution.py:348
  18.9 9.2 %collective-permute-start.3 = (f32[32,2048]{1,0:T(8,128)S(1)}, f32[32,2048]{1,0:T(8,128)S(1)}, u32[]{:S(2)}, u32[]{:S(2)}) collective-permute-start(f32[32,2048]{1,0:T(8,128)S(1)} %get-tuple-element.71), channel_id=1, source_target_pairs={{0,1},{1,0},{2,3},{3,2},{4,5},{5,4},{6,7},{7,6},{8,9},{9,8},{10,11... | collective-permute-start | bytes 786440 | tf_op jit(solution)/shard_map/ppermute | solution.py:348
  22.6 12.4 %collective-permute-start.5 = (f32[32,2048]{1,0:T(8,128)S(1)}, f32[32,2048]{1,0:T(8,128)S(1)}, u32[]{:S(2)}, u32[]{:S(2)}) collective-permute-start(f32[32,2048]{1,0:T(8,128)S(1)} %get-tuple-element.100.refs_0_), channel_id=1, source_target_pairs={{2,0},{4,2},{6,4},{8,6},{10,8},{12,10},{14,12},{16,14},{18,16},{20... | collective-permute-start | bytes 786440 | tf_op jit(solution)/shard_map/ppermute | solution.py:354
  23.9 9.8 %collective-permute-start.7 = (f32[32,2048]{1,0:T(8,128)S(1)}, f32[32,2048]{1,0:T(8,128)S(1)}, u32[]{:S(2)}, u32[]{:S(2)}) collective-permute-start(f32[32,2048]{1,0:T(8,128)S(1)} %get-tuple-element.100.refs_0_), channel_id=1, source_target_pairs={{0,1},{1,0},{2,3},{3,2},{4,5},{5,4},{6,7},{7,6},{8,9},{9,8},{10,11... | collective-permute-start | bytes 786440 | tf_op jit(solution)/shard_map/ppermute | solution.py:348
  28.2 8.2 %collective-permute-start.6 = (f32[32,2048]{1,0:T(8,128)S(1)}, f32[32,2048]{1,0:T(8,128)S(1)}, u32[]{:S(2)}, u32[]{:S(2)}) collective-permute-start(f32[32,2048]{1,0:T(8,128)S(1)} %get-tuple-element.111.refs_2_.refs_0_), channel_id=1, source_target_pairs={{2,0},{4,2},{6,4},{8,6},{10,8},{12,10},{14,12},{16,14},{18,16},{20... | collective-permute-start | bytes 786440 | tf_op jit(solution)/shard_map/ppermute | solution.py:354
  29.5 9.8 %collective-permute-start.4 = (f32[32,2048]{1,0:T(8,128)S(1)}, f32[32,2048]{1,0:T(8,128)S(1)}, u32[]{:S(2)}, u32[]{:S(2)}) collective-permute-start(f32[32,2048]{1,0:T(8,128)S(1)} %get-tuple-element.111.refs_2_.refs_0_), channel_id=1, source_target_pairs={{0,1},{1,0},{2,3},{3,2},{4,5},{5,4},{6,7},{7,6},{8,9},{9,8},{10,11... | collective-permute-start | bytes 786440 | tf_op jit(solution)/shard_map/ppermute | solution.py:348
  33.7 10.8 %collective-permute-start.9 = (f32[32,2048]{1,0:T(8,128)S(1)}, f32[32,2048]{1,0:T(8,128)S(1)}, u32[]{:S(2)}, u32[]{:S(2)}) collective-permute-start(f32[32,2048]{1,0:T(8,128)S(1)} %collective-permute-done.7.refs_1_), channel_id=1, source_target_pairs={{2,0},{4,2},{6,4},{8,6},{10,8},{12,10},{14,12},{16,14},{18,16},{20... | collective-permute-start | bytes 786440 | tf_op jit(solution)/shard_map/ppermute | solution.py:354
  39.3 9.7 %collective-permute-start.8 = (f32[32,2048]{1,0:T(8,128)S(1)}, f32[32,2048]{1,0:T(8,128)S(1)}, u32[]{:S(2)}, u32[]{:S(2)}) collective-permute-start(f32[32,2048]{1,0:T(8,128)S(1)} %collective-permute-done.4.refs_3_.refs_1_), channel_id=1, source_target_pairs={{2,0},{4,2},{6,4},{8,6},{10,8},{12,10},{14,12},{16,14},{18,16},{20... | collective-permute-start | bytes 786440 | tf_op jit(solution)/shard_map/ppermute | solution.py:354
  42.4 2.1 %collective-permute-start.10 = (f32[112,128]{1,0:T(8,128)S(1)}, f32[112,128]{1,0:T(8,128)S(1)}, u32[]{:S(2)}, u32[]{:S(2)}) collective-permute-start(f32[112,128]{1,0:T(8,128)S(1)} %get-tuple-element.92), channel_id=1, source_target_pairs={{0,2},{2,0},{4,6},{6,4},{8,10},{10,8},{12,14},{14,12},{16,18},{18,... | collective-permute-start | bytes 172040 | tf_op jit(solution)/shard_map/ppermute | solution.py:362
  44.5 4.5 %collective-permute-start.11 = (f32[112,128]{1,0:T(8,128)S(1)}, f32[112,128]{1,0:T(8,128)S(1)}, u32[]{:S(2)}, u32[]{:S(2)}) collective-permute-start(f32[112,128]{1,0:T(8,128)S(1)} %add.28), channel_id=1, source_target_pairs={{0,4},{2,6},{4,0},{6,2},{8,12},{10,14},{12,8},{14,10},{16,20},{18,... | collective-permute-start | bytes 172040 | tf_op jit(solution)/shard_map/ppermute | solution.py:362
  49.0 5.6 %collective-permute-start.12 = (f32[112,128]{1,0:T(8,128)S(1)}, f32[112,128]{1,0:T(8,128)S(1)}, u32[]{:S(2)}, u32[]{:S(2)}) collective-permute-start(f32[112,128]{1,0:T(8,128)S(1)} %add.29), channel_id=1, source_target_pairs={{0,8},{2,10},{4,12},{6,14},{8,0},{10,2},{12,4},{14,6},{16,24},{18,... | collective-permute-start | bytes 172040 | tf_op jit(solution)/shard_map/ppermute | solution.py:362
  54.6 5.2 %collective-permute-start.13 = (f32[112,128]{1,0:T(8,128)S(1)}, f32[112,128]{1,0:T(8,128)S(1)}, u32[]{:S(2)}, u32[]{:S(2)}) collective-permute-start(f32[112,128]{1,0:T(8,128)S(1)} %add.30), channel_id=1, source_target_pairs={{0,16},{2,18},{4,20},{6,22},{8,24},{10,26},{12,28},{14,30},{16,0},... | collective-permute-start | bytes 172040 | tf_op jit(solution)/shard_map/ppermute | solution.py:362
  59.8 1.3 %collective-permute-start.14 = (f32[112,128]{1,0:T(8,128)S(1)}, f32[112,128]{1,0:T(8,128)S(1)}, u32[]{:S(2)}, u32[]{:S(2)}) collective-permute-start(f32[112,128]{1,0:T(8,128)S(1)} %add.31), channel_id=1, source_target_pairs={{0,2},{2,0},{4,6},{6,4},{8,10},{10,8},{12,14},{14,12},{16,18},{18,... | collective-permute-start | bytes 172040 | tf_op jit(solution)/shard_map/ppermute | solution.py:362

commit v6 on v5

--- a/solution.py
+++ b/solution.py
@@ -12,7 +12,7 @@
 LANES = 128
 STEP = 8
 CHUNKS = 2
-BACK = (8, 22)
+BACK = (10, 22)
 VMEM = pl.BlockSpec(memory_space=pltpu.VMEM)
 ANY = pl.BlockSpec(memory_space=pl.ANY)
 
@@ -31,6 +31,12 @@
     parity, rest = cell // (2 * half), cell % (2 * half)
     wanted = (rest // half) * (2 * half) + 2 * (rest % half) + parity
     return (source == wanted).astype(F32).astype(BF16)
+
+
+def steps(begin, end):
+    runs = -(-(end - begin) // (STEP + 1))
+    cuts = [begin + (end - begin) * i // runs for i in range(runs + 1)]
+    return [(low, high - low) for low, high in zip(cuts, cuts[1:])]
 
 
 def lane_of(shape):
@@ -221,9 +227,7 @@
                 found.append(sources[2 * h + part][:, group(low - h * per, high - low)])
         return found[0] if len(found) == 1 else jnp.concatenate(found, axis=1)
 
-    first = begin
-    while first < end:
-        size = min(STEP, end - first)
+    for first, size in steps(begin, end):
         hi, lo = grad_shifts(lambda g: g_all[:, group(g - begin)], first, size, outs, half)
         a_hi, a_lo = [
             jnp.concatenate([cells_of(v, part, first, size) for v in (halos, planes_x)], axis=0) for part in range(2)
@@ -234,7 +238,6 @@
             (((1,), (1,)), ((), ())),
             preferred_element_type=F32,
         )
-        first += size
     if not last:
         out[0][...] = total[...]
         return
@@ -269,9 +272,7 @@
     flat = grown.reshape(chans * planes * height, LANES)
     matrix = pairing(half, True)
     matrix = jnp.concatenate([matrix, matrix], axis=0)
-    first = begin
-    while first < end:
-        size = min(STEP, end - first)
+    for first, size in steps(begin, end):
         hi, lo = grad_shifts(lambda g: g_here[:, group(g - begin)], first, size, outs, half)
         hi_above, lo_above = grad_shifts(lambda g: g_above[:, group(g - begin)], first, size, outs, half)
         grad = jnp.dot(
@@ -294,7 +295,6 @@
                     flat[pl.ds(row + 2 * side, chans, stride=planes * height), :] = rows[
                         start : start + chans, group(side)
                     ]
-        first += size
     part = pl.ds(4 * begin, 4 * (end - begin))
     copy = pltpu.make_async_copy(grown.at[:, part, :], out.at[:, part, :], sem)
     copy.start()

time: 62.3 us -> 62.1 us (level)
  transfers between devices with their start and end apart: 15 -> 15, of which waited for: 8 -> 6; matrix products, arithmetic and copies ran while one was open for 0% -> 0% of each run, Pallas kernels for 34% -> 35%
where the time goes in v6:
time: 62.1 us; the launch traced here: 61.9 us
  starting transfers between devices  25.9 us (42%)
  Pallas kernels  21.4 us (34%)
  waiting for transfers between devices  10.2 us (16%)
  local copies, waits for them, and re-layouts  2.52 us (4%)
  other arithmetic  0.95 us (2%)
  between operations  0.91 us (1%)
    pallas_call x12, Pallas kernels, call(): pl.pallas_call(kernel, name=name, out_shape=[jax.ShapeDtypeStruct(s, t) f...  21.4 us
    ppermute x6, starting transfers between devices, from_behind(): lax.ppermute(value, axis, [(source, source + steps) for source in range(i...  12.4 us
    ppermute x5, starting transfers between devices, swapped(): return lax.ppermute(value, axis, [(s, s ^ bit) for s in range(count)])  8.31 us
    ppermute x4, waiting for transfers between devices, turned(): lax.ppermute(value, axis, [(s, (s + steps) % count) for s in range(count)])  8.11 us
    ppermute x4, starting transfers between devices, turned(): lax.ppermute(value, axis, [(s, (s + steps) % count) for s in range(count)])  5.19 us
    ppermute x5, waiting for transfers between devices, swapped(): return lax.ppermute(value, axis, [(s, s ^ bit) for s in range(count)])  2.12 us
    squeeze x1, local copies, waits for them, and re-layouts, on_device(): volume[:, -1, h * rows:(h + 1) * rows]  1.42 us
  transfers between devices with their start and end apart: 15, of which 6 were waited for; matrix products, arithmetic and copies ran while one was open for 0% of the time, Pallas kernels for 35%

profile of v6, /device:TPU:0, one launch (start us, length us, event | category | flops | bytes accessed | tf_op | source)
XLA Modules:
  0.0 61.9 jit_solution(15224851740088592880)
XLA Ops:
  0.6 1.4 %slice_bitcast_fusion = (f32[16,64,128]{2,1,0:T(8,128)S(1)}, f32[16,64,128]{2,1,0:T(8,128)S(1)}) fusion(f32[16,2,128,128]{3,2,1,0:T(8,128)} %param.3), kind=kLoop, calls=%fused_computation | loop fusion | bytes 2097152 | tf_op jit(solution)/shard_map/squeeze | solution.py:390
  2.1 2.5 %collective-permute-start.1 = (f32[16,64,128]{2,1,0:T(8,128)S(1)}, f32[16,64,128]{2,1,0:T(8,128)S(1)}, u32[]{:S(2)}, u32[]{:S(2)}) collective-permute-start(f32[16,64,128]{2,1,0:T(8,128)S(1)} %get-tuple-element.126), channel_id=1, source_target_pairs={{0,2},{2,4},{4,6},{6,8},{8,10},{10,12},{12,14},{14,16},{16,18},{18... | collective-permute-start | bytes 1572872 | tf_op jit(solution)/shard_map/ppermute | solution.py:354
  4.6 4.5 %collective-permute-start = (f32[16,64,128]{2,1,0:T(8,128)S(1)}, f32[16,64,128]{2,1,0:T(8,128)S(1)}, u32[]{:S(2)}, u32[]{:S(2)}) collective-permute-start(f32[16,64,128]{2,1,0:T(8,128)S(1)} %get-tuple-element.127), channel_id=1, source_target_pairs={{0,2},{2,4},{4,6},{6,8},{8,10},{10,12},{12,14},{14,16},{16,18},{18... | collective-permute-start | bytes 1572872 | tf_op jit(solution)/shard_map/ppermute | solution.py:354
  9.2 0.9 %copy-done.2 = f32[64,16,3,3,3]{0,1,4,3,2:T(8,128)S(1)} copy-done((f32[64,16,3,3,3]{0,1,4,3,2:T(8,128)S(1)}, f32[64,16,3,3,3]{0,1,4,3,2:T(8,128)}, u32[]{:S(2)}) %copy-start.2) | copy-done | bytes 110616
  10.1 2.0 %own.2 = (bf16[128,2048]{1,0:T(8,128)(2,1)S(1)}, bf16[128,2048]{1,0:T(8,128)(2,1)S(1)}, f32[64,2048]{1,0:T(8,128)S(1)}, bf16[256,384]{1,0:T(8,128)(2,1)S(1)}, bf...) custom-call(f32[4096,128]{1,0:T(8,128)S(1)} %bitcast.19, f32[432,64]{1,0:T(8,128)S(1)} %bitcast.24), custom_call_target="tpu_custom_call" | custom-call | bytes 792 | tf_op jit(solution)/shard_map/own/pallas_call | solution.py:333
  12.1 1.4 %halo.2 = (bf16[64,2048]{1,0:T(8,128)(2,1)S(1)}, bf16[64,2048]{1,0:T(8,128)(2,1)S(1)}, f32[32,2048]{1,0:T(8,128)S(1)}, f32[32,2048]{1,0:T(8,128)S(1)}, f32[64,128]{1,0:T(8,128)S(1)}) custom-call(f32[1024,128]{1,0:T(8,128)S(1)} %bitcast.23, f32[64,2048]{1,0:T(8,128)S(1)} %get-tuple-element.65.refs_1_, bf16[256,192]{1,0:T(8,128)(2,1)S(1)} %get-tuple-element.64.refs_2_), custom_call_target="tpu_custom_call" | custom-call | bytes 612 | tf_op jit(solution)/shard_map/halo/pallas_call | solution.py:333
  13.5 1.6 %collective-permute-start.2 = (f32[32,2048]{1,0:T(8,128)S(1)}, f32[32,2048]{1,0:T(8,128)S(1)}, u32[]{:S(2)}, u32[]{:S(2)}) collective-permute-start(f32[32,2048]{1,0:T(8,128)S(1)} %get-tuple-element.69), channel_id=1, source_target_pairs={{0,1},{1,0},{2,3},{3,2},{4,5},{5,4},{6,7},{7,6},{8,9},{9,8},{10,11... | collective-permute-start | bytes 786440 | tf_op jit(solution)/shard_map/ppermute | solution.py:348
  15.6 2.0 %own.3 = (bf16[128,2048]{1,0:T(8,128)(2,1)S(1)}, bf16[128,2048]{1,0:T(8,128)(2,1)S(1)}, f32[64,2048]{1,0:T(8,128)S(1)}) custom-call(f32[4096,128]{1,0:T(8,128)S(1)} %bitcast.20, bf16[256,384]{1,0:T(8,128)(2,1)S(1)} %get-tuple-element.61.refs_0_, f32[64,128]{1,0:T(8,128)S(1)} %get-tuple-element.62.refs_1_), custom_call_target="tpu_custom_call" | custom-call | bytes 576 | tf_op jit(solution)/shard_map/own/pallas_call | solution.py:333
  17.6 1.3 %halo.3 = (bf16[64,2048]{1,0:T(8,128)(2,1)S(1)}, bf16[64,2048]{1,0:T(8,128)(2,1)S(1)}, f32[32,2048]{1,0:T(8,128)S(1)}, f32[32,2048]{1,0:T(8,128)S(1)}) custom-call(f32[1024,128]{1,0:T(8,128)S(1)} %bitcast.22, f32[64,2048]{1,0:T(8,128)S(1)} %get-tuple-element.63.refs_1_, bf16[256,192]{1,0:T(8,128)(2,1)S(1)} %get-tuple-element.64.refs_2_, ...), custom_call_target="tpu_custom_call" | custom-call | bytes 612 | tf_op jit(solution)/shard_map/halo/pallas_call | solution.py:333
  19.5 2.9 %collective-permute-done.2 = f32[32,2048]{1,0:T(8,128)S(1)} collective-permute-done((f32[32,2048]{1,0:T(8,128)S(1)}, f32[32,2048]{1,0:T(8,128)S(1)}, u32[]{:S(2)}, u32[]{:S(2)}) %collective-permute-start.2) | collective-permute-done | bytes 262176 | tf_op jit(solution)/shard_map/ppermute | solution.py:348
  22.6 1.3 %collective-permute-start.5 = (f32[32,2048]{1,0:T(8,128)S(1)}, f32[32,2048]{1,0:T(8,128)S(1)}, u32[]{:S(2)}, u32[]{:S(2)}) collective-permute-start(f32[32,2048]{1,0:T(8,128)S(1)} %get-tuple-element.100.refs_0_), channel_id=1, source_target_pairs={{2,0},{4,2},{6,4},{8,6},{10,8},{12,10},{14,12},{16,14},{18,16},{20... | collective-permute-start | bytes 786440 | tf_op jit(solution)/shard_map/ppermute | solution.py:354
  23.9 1.5 %collective-permute-start.7 = (f32[32,2048]{1,0:T(8,128)S(1)}, f32[32,2048]{1,0:T(8,128)S(1)}, u32[]{:S(2)}, u32[]{:S(2)}) collective-permute-start(f32[32,2048]{1,0:T(8,128)S(1)} %get-tuple-element.100.refs_0_), channel_id=1, source_target_pairs={{0,1},{1,0},{2,3},{3,2},{4,5},{5,4},{6,7},{7,6},{8,9},{9,8},{10,11... | collective-permute-start | bytes 786440 | tf_op jit(solution)/shard_map/ppermute | solution.py:348
  25.4 1.6 %activation.2.refs_0_ = f32[2048,64]{1,0:T(8,128)} custom-call(f32[32,2048]{1,0:T(8,128)S(1)} %get-tuple-element.123.chunk), custom_call_target="tpu_custom_call" | custom-call | bytes 360 | tf_op jit(solution)/shard_map/activation/pallas_call | solution.py:333
  27.0 1.1 %collective-permute-done.3 = f32[32,2048]{1,0:T(8,128)S(1)} collective-permute-done((f32[32,2048]{1,0:T(8,128)S(1)}, f32[32,2048]{1,0:T(8,128)S(1)}, u32[]{:S(2)}, u32[]{:S(2)}) %collective-permute-start.3) | collective-permute-done | bytes 262176 | tf_op jit(solution)/shard_map/ppermute | solution.py:348
  28.2 1.3 %collective-permute-start.6 = (f32[32,2048]{1,0:T(8,128)S(1)}, f32[32,2048]{1,0:T(8,128)S(1)}, u32[]{:S(2)}, u32[]{:S(2)}) collective-permute-start(f32[32,2048]{1,0:T(8,128)S(1)} %get-tuple-element.111.refs_2_.refs_0_), channel_id=1, source_target_pairs={{2,0},{4,2},{6,4},{8,6},{10,8},{12,10},{14,12},{16,14},{18,16},{20... | collective-permute-start | bytes 786440 | tf_op jit(solution)/shard_map/ppermute | solution.py:354
  29.5 1.5 %collective-permute-start.4 = (f32[32,2048]{1,0:T(8,128)S(1)}, f32[32,2048]{1,0:T(8,128)S(1)}, u32[]{:S(2)}, u32[]{:S(2)}) collective-permute-start(f32[32,2048]{1,0:T(8,128)S(1)} %get-tuple-element.111.refs_2_.refs_0_), channel_id=1, source_target_pairs={{0,1},{1,0},{2,3},{3,2},{4,5},{5,4},{6,7},{7,6},{8,9},{9,8},{10,11... | collective-permute-start | bytes 786440 | tf_op jit(solution)/shard_map/ppermute | solution.py:348
  31.0 2.7 %collective-permute-done.7.refs_1_ = f32[32,2048]{1,0:T(8,128)S(1)} collective-permute-done((f32[32,2048]{1,0:T(8,128)S(1)}, f32[32,2048]{1,0:T(8,128)S(1)}, u32[]{:S(2)}, u32[]{:S(2)}) %collective-permute-start.7) | collective-permute-done | bytes 262176 | tf_op jit(solution)/shard_map/ppermute | solution.py:348
  33.7 1.3 %collective-permute-start.9 = (f32[32,2048]{1,0:T(8,128)S(1)}, f32[32,2048]{1,0:T(8,128)S(1)}, u32[]{:S(2)}, u32[]{:S(2)}) collective-permute-start(f32[32,2048]{1,0:T(8,128)S(1)} %collective-permute-done.7.refs_1_), channel_id=1, source_target_pairs={{2,0},{4,2},{6,4},{8,6},{10,8},{12,10},{14,12},{16,14},{18,16},{20... | collective-permute-start | bytes 786440 | tf_op jit(solution)/shard_map/ppermute | solution.py:354
  35.0 1.4 %filter.2.refs_12_ = f32[192,256]{1,0:T(8,128)S(1)} custom-call(f32[32,2048]{1,0:T(8,128)S(1)} %get-tuple-element.100.refs_0_, f32[32,2048]{1,0:T(8,128)S(1)} %collective-permute-done.7.refs_1_, bf16[128,2048]{1,0:T(8,128)(2,1)S(1)} %get-tuple-element.74.refs_2_.refs_4_, bf16[128,2048]{1,0:T(8,128)(2,1)S(1)} %get-tuple-element.75.refs_3_.refs_5_, ...), custom_call_target="tpu_custom_call" | custom-call | bytes 576 | tf_op jit(solution)/shard_map/filter/pallas_call | solution.py:333
  36.4 1.6 %activation.3 = f32[2048,64]{1,0:T(8,128)} custom-call(f32[32,2048]{1,0:T(8,128)S(1)} %get-tuple-element.80.chunk, f32[2048,64]{1,0:T(8,128)} %activation.2.refs_0_), custom_call_target="tpu_custom_call", output_to_operand_aliasing={{}: (1, {})} | custom-call | bytes 360 | tf_op jit(solution)/shard_map/activation/pallas_call | solution.py:333
  38.0 1.3 %collective-permute-done.4.refs_3_.refs_1_ = f32[32,2048]{1,0:T(8,128)S(1)} collective-permute-done((f32[32,2048]{1,0:T(8,128)S(1)}, f32[32,2048]{1,0:T(8,128)S(1)}, u32[]{:S(2)}, u32[]{:S(2)}) %collective-permute-start.4) | collective-permute-done | bytes 262176 | tf_op jit(solution)/shard_map/ppermute | solution.py:348
  39.3 1.5 %collective-permute-start.8 = (f32[32,2048]{1,0:T(8,128)S(1)}, f32[32,2048]{1,0:T(8,128)S(1)}, u32[]{:S(2)}, u32[]{:S(2)}) collective-permute-start(f32[32,2048]{1,0:T(8,128)S(1)} %collective-permute-done.4.refs_3_.refs_1_), channel_id=1, source_target_pairs={{2,0},{4,2},{6,4},{8,6},{10,8},{12,10},{14,12},{16,14},{18,16},{20... | collective-permute-start | bytes 786440 | tf_op jit(solution)/shard_map/ppermute | solution.py:354
  40.8 1.6 %filter.3 = (f32[112,128]{1,0:T(8,128)S(1)}, f32[112,128]{1,0:T(8,128)S(1)}) custom-call(f32[32,2048]{1,0:T(8,128)S(1)} %get-tuple-element.100.refs_0_, f32[32,2048]{1,0:T(8,128)S(1)} %collective-permute-done.7.refs_1_, f32[32,2048]{1,0:T(8,128)S(1)} %get-tuple-element.111.refs_2_.refs_0_, f32[32,2048]{1,0:T(8,128)S(1)} %collective-permute-done.4.refs_3_.refs_1_, ...), custom_call_target="tpu_custom_call" | custom-call | bytes 576 | tf_op jit(solution)/shard_map/filter/pallas_call | solution.py:333
  42.4 1.2 %collective-permute-start.10 = (f32[112,128]{1,0:T(8,128)S(1)}, f32[112,128]{1,0:T(8,128)S(1)}, u32[]{:S(2)}, u32[]{:S(2)}) collective-permute-start(f32[112,128]{1,0:T(8,128)S(1)} %get-tuple-element.92), channel_id=1, source_target_pairs={{0,2},{2,0},{4,6},{6,4},{8,10},{10,8},{12,14},{14,12},{16,18},{18,... | collective-permute-start | bytes 172040 | tf_op jit(solution)/shard_map/ppermute | solution.py:362
  43.6 0.9 %collective-permute-done.10 = f32[112,128]{1,0:T(8,128)S(1)} collective-permute-done((f32[112,128]{1,0:T(8,128)S(1)}, f32[112,128]{1,0:T(8,128)S(1)}, u32[]{:S(2)}, u32[]{:S(2)}) %collective-permute-start.10) | collective-permute-done | bytes 57376 | tf_op jit(solution)/shard_map/ppermute | solution.py:362
  44.5 2.1 %collective-permute-start.11 = (f32[112,128]{1,0:T(8,128)S(1)}, f32[112,128]{1,0:T(8,128)S(1)}, u32[]{:S(2)}, u32[]{:S(2)}) collective-permute-start(f32[112,128]{1,0:T(8,128)S(1)} %add.28), channel_id=1, source_target_pairs={{0,4},{2,6},{4,0},{6,2},{8,12},{10,14},{12,8},{14,10},{16,20},{18,... | collective-permute-start | bytes 172040 | tf_op jit(solution)/shard_map/ppermute | solution.py:362
  46.6 2.6 %back.3.refs_9_ = f32[32,128,128]{2,1,0:T(8,128)} custom-call(f32[32,2048]{1,0:T(8,128)S(1)} %get-tuple-element.100.refs_0_, f32[32,2048]{1,0:T(8,128)S(1)} %collective-permute-done.7.refs_1_, f32[32,2048]{1,0:T(8,128)S(1)} %collective-permute-done.5.refs_2_.refs_4_, f32[32,2048]{1,0:T(8,128)S(1)} %collective-permute-done.9.refs_3_.refs_5_, ...), custom_call_target="tpu_custom_call" | custom-call | bytes 900 | tf_op jit(solution)/shard_map/back/pallas_call | solution.py:333
  49.2 2.3 %collective-permute-start.12 = (f32[112,128]{1,0:T(8,128)S(1)}, f32[112,128]{1,0:T(8,128)S(1)}, u32[]{:S(2)}, u32[]{:S(2)}) collective-permute-start(f32[112,128]{1,0:T(8,128)S(1)} %add.29), channel_id=1, source_target_pairs={{0,8},{2,10},{4,12},{6,14},{8,0},{10,2},{12,4},{14,6},{16,24},{18,... | collective-permute-start | bytes 172040 | tf_op jit(solution)/shard_map/ppermute | solution.py:362
  51.5 2.8 %back.4.refs_5_ = f32[32,128,128]{2,1,0:T(8,128)} custom-call(f32[32,2048]{1,0:T(8,128)S(1)} %get-tuple-element.100.refs_0_, f32[32,2048]{1,0:T(8,128)S(1)} %collective-permute-done.7.refs_1_, f32[32,2048]{1,0:T(8,128)S(1)} %get-tuple-element.111.refs_2_.refs_0_, ...), custom_call_target="tpu_custom_call", output_to_operand_aliasing={{}: (9, {})} | custom-call | bytes 900 | tf_op jit(solution)/shard_map/back/pallas_call | solution.py:333
  54.4 2.7 %collective-permute-start.13 = (f32[112,128]{1,0:T(8,128)S(1)}, f32[112,128]{1,0:T(8,128)S(1)}, u32[]{:S(2)}, u32[]{:S(2)}) collective-permute-start(f32[112,128]{1,0:T(8,128)S(1)} %add.30), channel_id=1, source_target_pairs={{0,16},{2,18},{4,20},{6,22},{8,24},{10,26},{12,28},{14,30},{16,0},... | collective-permute-start | bytes 172040 | tf_op jit(solution)/shard_map/ppermute | solution.py:362
  57.0 2.6 %back.5 = f32[32,128,128]{2,1,0:T(8,128)} custom-call(f32[32,2048]{1,0:T(8,128)S(1)} %get-tuple-element.111.refs_2_.refs_0_, f32[32,2048]{1,0:T(8,128)S(1)} %collective-permute-done.4.refs_3_.refs_1_, f32[32,2048]{1,0:T(8,128)S(1)} %collective-permute-done.6.refs_6_.refs_2_, ...), custom_call_target="tpu_custom_call", output_to_operand_aliasing={{}: (5, {})} | custom-call | bytes 900 | tf_op jit(solution)/shard_map/back/pallas_call | solution.py:333
  59.8 1.2 %collective-permute-done.14 = f32[112,128]{1,0:T(8,128)S(1)} collective-permute-done((f32[112,128]{1,0:T(8,128)S(1)}, f32[112,128]{1,0:T(8,128)S(1)}, u32[]{:S(2)}, u32[]{:S(2)}) %collective-permute-start.14) | collective-permute-done | bytes 57376 | tf_op jit(solution)/shard_map/ppermute | solution.py:362
  (27 shorter events, 2.4 us)
Async XLA Ops:
  0.6 8.5 %copy-start = (f32[16,2,128,128]{3,2,1,0:T(8,128)S(1)}, f32[16,2,128,128]{3,2,1,0:T(8,128)}, u32[]{:S(2)}) copy-start(f32[16,2,128,128]{3,2,1,0:T(8,128)} %param.3) | copy-start | bytes 6291460
  2.1 12.9 %copy-start.1 = (f32[32,1,64,64]{3,2,1,0:T(8,128)S(1)}, f32[32,1,64,64]{3,2,1,0:T(8,128)}, u32[]{:S(2)}) copy-start(f32[32,1,64,64]{3,2,1,0:T(8,128)} %param.5) | copy-start | bytes 1572868
  2.1 10.0 %collective-permute-start.1 = (f32[16,64,128]{2,1,0:T(8,128)S(1)}, f32[16,64,128]{2,1,0:T(8,128)S(1)}, u32[]{:S(2)}, u32[]{:S(2)}) collective-permute-start(f32[16,64,128]{2,1,0:T(8,128)S(1)} %get-tuple-element.126), channel_id=1, source_target_pairs={{0,2},{2,4},{4,6},{6,8},{8,10},{10,12},{12,14},{14,16},{16,18},{18... | collective-permute-start | bytes 1572872 | tf_op jit(solution)/shard_map/ppermute | solution.py:354
  4.6 13.0 %collective-permute-start = (f32[16,64,128]{2,1,0:T(8,128)S(1)}, f32[16,64,128]{2,1,0:T(8,128)S(1)}, u32[]{:S(2)}, u32[]{:S(2)}) collective-permute-start(f32[16,64,128]{2,1,0:T(8,128)S(1)} %get-tuple-element.127), channel_id=1, source_target_pairs={{0,2},{2,4},{4,6},{6,8},{8,10},{10,12},{12,14},{14,16},{16,18},{18... | collective-permute-start | bytes 1572872 | tf_op jit(solution)/shard_map/ppermute | solution.py:354
  9.2 0.9 %copy-start.2 = (f32[64,16,3,3,3]{0,1,4,3,2:T(8,128)S(1)}, f32[64,16,3,3,3]{0,1,4,3,2:T(8,128)}, u32[]{:S(2)}) copy-start(f32[64,16,3,3,3]{0,1,4,3,2:T(8,128)} %param.4) | copy-start | bytes 331780
  13.5 9.0 %collective-permute-start.2 = (f32[32,2048]{1,0:T(8,128)S(1)}, f32[32,2048]{1,0:T(8,128)S(1)}, u32[]{:S(2)}, u32[]{:S(2)}) collective-permute-start(f32[32,2048]{1,0:T(8,128)S(1)} %get-tuple-element.69), channel_id=1, source_target_pairs={{0,1},{1,0},{2,3},{3,2},{4,5},{5,4},{6,7},{7,6},{8,9},{9,8},{10,11... | collective-permute-start | bytes 786440 | tf_op jit(solution)/shard_map/ppermute | solution.py:348
  18.9 9.2 %collective-permute-start.3 = (f32[32,2048]{1,0:T(8,128)S(1)}, f32[32,2048]{1,0:T(8,128)S(1)}, u32[]{:S(2)}, u32[]{:S(2)}) collective-permute-start(f32[32,2048]{1,0:T(8,128)S(1)} %get-tuple-element.71), channel_id=1, source_target_pairs={{0,1},{1,0},{2,3},{3,2},{4,5},{5,4},{6,7},{7,6},{8,9},{9,8},{10,11... | collective-permute-start | bytes 786440 | tf_op jit(solution)/shard_map/ppermute | solution.py:348
  22.6 12.4 %collective-permute-start.5 = (f32[32,2048]{1,0:T(8,128)S(1)}, f32[32,2048]{1,0:T(8,128)S(1)}, u32[]{:S(2)}, u32[]{:S(2)}) collective-permute-start(f32[32,2048]{1,0:T(8,128)S(1)} %get-tuple-element.100.refs_0_), channel_id=1, source_target_pairs={{2,0},{4,2},{6,4},{8,6},{10,8},{12,10},{14,12},{16,14},{18,16},{20... | collective-permute-start | bytes 786440 | tf_op jit(solution)/shard_map/ppermute | solution.py:354
  23.9 9.8 %collective-permute-start.7 = (f32[32,2048]{1,0:T(8,128)S(1)}, f32[32,2048]{1,0:T(8,128)S(1)}, u32[]{:S(2)}, u32[]{:S(2)}) collective-permute-start(f32[32,2048]{1,0:T(8,128)S(1)} %get-tuple-element.100.refs_0_), channel_id=1, source_target_pairs={{0,1},{1,0},{2,3},{3,2},{4,5},{5,4},{6,7},{7,6},{8,9},{9,8},{10,11... | collective-permute-start | bytes 786440 | tf_op jit(solution)/shard_map/ppermute | solution.py:348
  28.2 8.2 %collective-permute-start.6 = (f32[32,2048]{1,0:T(8,128)S(1)}, f32[32,2048]{1,0:T(8,128)S(1)}, u32[]{:S(2)}, u32[]{:S(2)}) collective-permute-start(f32[32,2048]{1,0:T(8,128)S(1)} %get-tuple-element.111.refs_2_.refs_0_), channel_id=1, source_target_pairs={{2,0},{4,2},{6,4},{8,6},{10,8},{12,10},{14,12},{16,14},{18,16},{20... | collective-permute-start | bytes 786440 | tf_op jit(solution)/shard_map/ppermute | solution.py:354
  29.5 9.8 %collective-permute-start.4 = (f32[32,2048]{1,0:T(8,128)S(1)}, f32[32,2048]{1,0:T(8,128)S(1)}, u32[]{:S(2)}, u32[]{:S(2)}) collective-permute-start(f32[32,2048]{1,0:T(8,128)S(1)} %get-tuple-element.111.refs_2_.refs_0_), channel_id=1, source_target_pairs={{0,1},{1,0},{2,3},{3,2},{4,5},{5,4},{6,7},{7,6},{8,9},{9,8},{10,11... | collective-permute-start | bytes 786440 | tf_op jit(solution)/shard_map/ppermute | solution.py:348
  33.7 10.8 %collective-permute-start.9 = (f32[32,2048]{1,0:T(8,128)S(1)}, f32[32,2048]{1,0:T(8,128)S(1)}, u32[]{:S(2)}, u32[]{:S(2)}) collective-permute-start(f32[32,2048]{1,0:T(8,128)S(1)} %collective-permute-done.7.refs_1_), channel_id=1, source_target_pairs={{2,0},{4,2},{6,4},{8,6},{10,8},{12,10},{14,12},{16,14},{18,16},{20... | collective-permute-start | bytes 786440 | tf_op jit(solution)/shard_map/ppermute | solution.py:354
  39.3 9.9 %collective-permute-start.8 = (f32[32,2048]{1,0:T(8,128)S(1)}, f32[32,2048]{1,0:T(8,128)S(1)}, u32[]{:S(2)}, u32[]{:S(2)}) collective-permute-start(f32[32,2048]{1,0:T(8,128)S(1)} %collective-permute-done.4.refs_3_.refs_1_), channel_id=1, source_target_pairs={{2,0},{4,2},{6,4},{8,6},{10,8},{12,10},{14,12},{16,14},{18,16},{20... | collective-permute-start | bytes 786440 | tf_op jit(solution)/shard_map/ppermute | solution.py:354
  42.4 2.1 %collective-permute-start.10 = (f32[112,128]{1,0:T(8,128)S(1)}, f32[112,128]{1,0:T(8,128)S(1)}, u32[]{:S(2)}, u32[]{:S(2)}) collective-permute-start(f32[112,128]{1,0:T(8,128)S(1)} %get-tuple-element.92), channel_id=1, source_target_pairs={{0,2},{2,0},{4,6},{6,4},{8,10},{10,8},{12,14},{14,12},{16,18},{18,... | collective-permute-start | bytes 172040 | tf_op jit(solution)/shard_map/ppermute | solution.py:362
  44.5 4.7 %collective-permute-start.11 = (f32[112,128]{1,0:T(8,128)S(1)}, f32[112,128]{1,0:T(8,128)S(1)}, u32[]{:S(2)}, u32[]{:S(2)}) collective-permute-start(f32[112,128]{1,0:T(8,128)S(1)} %add.28), channel_id=1, source_target_pairs={{0,4},{2,6},{4,0},{6,2},{8,12},{10,14},{12,8},{14,10},{16,20},{18,... | collective-permute-start | bytes 172040 | tf_op jit(solution)/shard_map/ppermute | solution.py:362
  49.2 5.2 %collective-permute-start.12 = (f32[112,128]{1,0:T(8,128)S(1)}, f32[112,128]{1,0:T(8,128)S(1)}, u32[]{:S(2)}, u32[]{:S(2)}) collective-permute-start(f32[112,128]{1,0:T(8,128)S(1)} %add.29), channel_id=1, source_target_pairs={{0,8},{2,10},{4,12},{6,14},{8,0},{10,2},{12,4},{14,6},{16,24},{18,... | collective-permute-start | bytes 172040 | tf_op jit(solution)/shard_map/ppermute | solution.py:362
  54.4 5.3 %collective-permute-start.13 = (f32[112,128]{1,0:T(8,128)S(1)}, f32[112,128]{1,0:T(8,128)S(1)}, u32[]{:S(2)}, u32[]{:S(2)}) collective-permute-start(f32[112,128]{1,0:T(8,128)S(1)} %add.30), channel_id=1, source_target_pairs={{0,16},{2,18},{4,20},{6,22},{8,24},{10,26},{12,28},{14,30},{16,0},... | collective-permute-start | bytes 172040 | tf_op jit(solution)/shard_map/ppermute | solution.py:362
  59.7 1.3 %collective-permute-start.14 = (f32[112,128]{1,0:T(8,128)S(1)}, f32[112,128]{1,0:T(8,128)S(1)}, u32[]{:S(2)}, u32[]{:S(2)}) collective-permute-start(f32[112,128]{1,0:T(8,128)S(1)} %add.31), channel_id=1, source_target_pairs={{0,2},{2,0},{4,6},{6,4},{8,10},{10,8},{12,14},{14,12},{16,18},{18,... | collective-permute-start | bytes 172040 | tf_op jit(solution)/shard_map/ppermute | solution.py:362

commit v7 on v6

--- a/solution.py
+++ b/solution.py
@@ -387,7 +387,11 @@
         taps = jnp.pad(taps, ((0, 0), (0, 0), (0, 0), (0, chans - real), (0, 0)))
     dims = (chans, outs, planes, height, half)
     rows = height // CHUNKS
-    halos = [from_behind(volume[:, -1, h * rows : (h + 1) * rows], "space", 1) for h in range(CHUNKS)]
+    ends, source = [volume[:, -1, :rows]], volume
+    for h in range(1, CHUNKS):
+        source, _ = lax.optimization_barrier((source, ends[-1]))
+        ends.append(source[:, -1, h * rows : (h + 1) * rows])
+    halos = [from_behind(end, "space", 1) for end in ends]
     halos = [halo.reshape(chans * rows, width) for halo in halos]
     x_own, parts, before = [], [], []
     for h in range(CHUNKS):

time: 62.1 us -> 62.5 us (level)
  local copies, waits for them, and re-layouts: 2.52 us -> 3.41 us
    squeeze x1 -> x2, local copies, waits for them, and re-layouts: 1.42 us -> 2.32 us  [the longest x1 1.23 us: on_device(): ends, source = ([volume[:, -1, :rows]], volume)]
  transfers between devices with their start and end apart: 15 -> 15, of which waited for: 6 -> 6; matrix products, arithmetic and copies ran while one was open for 0% -> 2% of each run, Pallas kernels for 35% -> 34%
where the time goes in v7:
time: 62.5 us; the launch traced here: 62.2 us
  starting transfers between devices  25.6 us (41%)
  Pallas kernels  21.3 us (34%)
  waiting for transfers between devices  9.97 us (16%)
  local copies, waits for them, and re-layouts  3.41 us (5%)
  other arithmetic  0.95 us (2%)
  between operations  0.92 us (1%)
    pallas_call x12, Pallas kernels, call(): pl.pallas_call(kernel, name=name, out_shape=[jax.ShapeDtypeStruct(s, t) f...  21.3 us
    ppermute x6, starting transfers between devices, from_behind(): lax.ppermute(value, axis, [(source, source + steps) for source in range(i...  12.4 us
    ppermute x5, starting transfers between devices, swapped(): return lax.ppermute(value, axis, [(s, s ^ bit) for s in range(count)])  8.36 us
    ppermute x4, waiting for transfers between devices, turned(): lax.ppermute(value, axis, [(s, (s + steps) % count) for s in range(count)])  7.83 us
    ppermute x4, starting transfers between devices, turned(): lax.ppermute(value, axis, [(s, (s + steps) % count) for s in range(count)])  4.84 us
    ppermute x5, waiting for transfers between devices, swapped(): return lax.ppermute(value, axis, [(s, s ^ bit) for s in range(count)])  2.12 us
  transfers between devices with their start and end apart: 15, of which 6 were waited for; matrix products, arithmetic and copies ran while one was open for 2% of the time, Pallas kernels for 34%

profile of v7, /device:TPU:0, one launch (start us, length us, event | category | flops | bytes accessed | tf_op | source)
XLA Modules:
  0.0 62.2 jit_solution(2385191491939526453)
XLA Ops:
  0.6 1.2 %slice_bitcast_fusion.1 = f32[16,64,128]{2,1,0:T(8,128)S(1)} fusion(f32[16,2,128,128]{3,2,1,0:T(8,128)} %param.3), kind=kLoop, calls=%fused_computation.1 | loop fusion | bytes 1048576 | tf_op jit(solution)/shard_map/squeeze | solution.py:390
  1.9 2.5 %collective-permute-start.1 = (f32[16,64,128]{2,1,0:T(8,128)S(1)}, f32[16,64,128]{2,1,0:T(8,128)S(1)}, u32[]{:S(2)}, u32[]{:S(2)}) collective-permute-start(f32[16,64,128]{2,1,0:T(8,128)S(1)} %slice_bitcast_fusion.1), channel_id=1, source_target_pairs={{0,2},{2,4},{4,6},{6,8},{8,10},{10,12},{12,14},{14,16},{16,18},{18... | collective-permute-start | bytes 1572872 | tf_op jit(solution)/shard_map/ppermute | solution.py:354
  4.4 1.1 %slice_bitcast_fusion = f32[16,64,128]{2,1,0:T(8,128)S(1)} fusion(f32[16,2,128,128]{3,2,1,0:T(8,128)} %param.3), kind=kLoop, calls=%fused_computation | loop fusion | bytes 1048576 | tf_op jit(solution)/shard_map/squeeze | solution.py:393
  5.5 4.5 %collective-permute-start = (f32[16,64,128]{2,1,0:T(8,128)S(1)}, f32[16,64,128]{2,1,0:T(8,128)S(1)}, u32[]{:S(2)}, u32[]{:S(2)}) collective-permute-start(f32[16,64,128]{2,1,0:T(8,128)S(1)} %slice_bitcast_fusion), channel_id=1, source_target_pairs={{0,2},{2,4},{4,6},{6,8},{8,10},{10,12},{12,14},{14,16},{16,18},{18... | collective-permute-start | bytes 1572872 | tf_op jit(solution)/shard_map/ppermute | solution.py:354
  10.1 0.9 %copy-done.2 = f32[64,16,3,3,3]{0,1,4,3,2:T(8,128)S(1)} copy-done((f32[64,16,3,3,3]{0,1,4,3,2:T(8,128)S(1)}, f32[64,16,3,3,3]{0,1,4,3,2:T(8,128)}, u32[]{:S(2)}) %copy-start.2) | copy-done | bytes 110616
  11.0 2.0 %own.2 = (bf16[128,2048]{1,0:T(8,128)(2,1)S(1)}, bf16[128,2048]{1,0:T(8,128)(2,1)S(1)}, f32[64,2048]{1,0:T(8,128)S(1)}, bf16[256,384]{1,0:T(8,128)(2,1)S(1)}, bf...) custom-call(f32[4096,128]{1,0:T(8,128)S(1)} %bitcast.19, f32[432,64]{1,0:T(8,128)S(1)} %bitcast.24), custom_call_target="tpu_custom_call" | custom-call | bytes 792 | tf_op jit(solution)/shard_map/own/pallas_call | solution.py:333
  13.0 1.4 %halo.2 = (bf16[64,2048]{1,0:T(8,128)(2,1)S(1)}, bf16[64,2048]{1,0:T(8,128)(2,1)S(1)}, f32[32,2048]{1,0:T(8,128)S(1)}, f32[32,2048]{1,0:T(8,128)S(1)}, f32[64,128]{1,0:T(8,128)S(1)}) custom-call(f32[1024,128]{1,0:T(8,128)S(1)} %bitcast.23, f32[64,2048]{1,0:T(8,128)S(1)} %get-tuple-element.67.refs_1_, bf16[256,192]{1,0:T(8,128)(2,1)S(1)} %get-tuple-element.66.refs_2_), custom_call_target="tpu_custom_call" | custom-call | bytes 612 | tf_op jit(solution)/shard_map/halo/pallas_call | solution.py:333
  14.4 1.6 %collective-permute-start.2 = (f32[32,2048]{1,0:T(8,128)S(1)}, f32[32,2048]{1,0:T(8,128)S(1)}, u32[]{:S(2)}, u32[]{:S(2)}) collective-permute-start(f32[32,2048]{1,0:T(8,128)S(1)} %get-tuple-element.71), channel_id=1, source_target_pairs={{0,1},{1,0},{2,3},{3,2},{4,5},{5,4},{6,7},{7,6},{8,9},{9,8},{10,11... | collective-permute-start | bytes 786440 | tf_op jit(solution)/shard_map/ppermute | solution.py:348
  16.5 2.0 %own.3 = (bf16[128,2048]{1,0:T(8,128)(2,1)S(1)}, bf16[128,2048]{1,0:T(8,128)(2,1)S(1)}, f32[64,2048]{1,0:T(8,128)S(1)}) custom-call(f32[4096,128]{1,0:T(8,128)S(1)} %bitcast.20, bf16[256,384]{1,0:T(8,128)(2,1)S(1)} %get-tuple-element.63.refs_0_, f32[64,128]{1,0:T(8,128)S(1)} %get-tuple-element.64.refs_1_), custom_call_target="tpu_custom_call" | custom-call | bytes 576 | tf_op jit(solution)/shard_map/own/pallas_call | solution.py:333
  18.5 1.3 %halo.3 = (bf16[64,2048]{1,0:T(8,128)(2,1)S(1)}, bf16[64,2048]{1,0:T(8,128)(2,1)S(1)}, f32[32,2048]{1,0:T(8,128)S(1)}, f32[32,2048]{1,0:T(8,128)S(1)}) custom-call(f32[1024,128]{1,0:T(8,128)S(1)} %bitcast.22, f32[64,2048]{1,0:T(8,128)S(1)} %get-tuple-element.65.refs_1_, bf16[256,192]{1,0:T(8,128)(2,1)S(1)} %get-tuple-element.66.refs_2_, ...), custom_call_target="tpu_custom_call" | custom-call | bytes 612 | tf_op jit(solution)/shard_map/halo/pallas_call | solution.py:333
  20.4 2.3 %collective-permute-done.2 = f32[32,2048]{1,0:T(8,128)S(1)} collective-permute-done((f32[32,2048]{1,0:T(8,128)S(1)}, f32[32,2048]{1,0:T(8,128)S(1)}, u32[]{:S(2)}, u32[]{:S(2)}) %collective-permute-start.2) | collective-permute-done | bytes 262176 | tf_op jit(solution)/shard_map/ppermute | solution.py:348
  22.8 1.3 %collective-permute-start.5 = (f32[32,2048]{1,0:T(8,128)S(1)}, f32[32,2048]{1,0:T(8,128)S(1)}, u32[]{:S(2)}, u32[]{:S(2)}) collective-permute-start(f32[32,2048]{1,0:T(8,128)S(1)} %get-tuple-element.102.refs_0_), channel_id=1, source_target_pairs={{2,0},{4,2},{6,4},{8,6},{10,8},{12,10},{14,12},{16,14},{18,16},{20... | collective-permute-start | bytes 786440 | tf_op jit(solution)/shard_map/ppermute | solution.py:354
  24.1 1.6 %collective-permute-start.7 = (f32[32,2048]{1,0:T(8,128)S(1)}, f32[32,2048]{1,0:T(8,128)S(1)}, u32[]{:S(2)}, u32[]{:S(2)}) collective-permute-start(f32[32,2048]{1,0:T(8,128)S(1)} %get-tuple-element.102.refs_0_), channel_id=1, source_target_pairs={{0,1},{1,0},{2,3},{3,2},{4,5},{5,4},{6,7},{7,6},{8,9},{9,8},{10,11... | collective-permute-start | bytes 786440 | tf_op jit(solution)/shard_map/ppermute | solution.py:348
  25.7 1.6 %activation.2.refs_0_ = f32[2048,64]{1,0:T(8,128)} custom-call(f32[32,2048]{1,0:T(8,128)S(1)} %get-tuple-element.125.chunk), custom_call_target="tpu_custom_call" | custom-call | bytes 360 | tf_op jit(solution)/shard_map/activation/pallas_call | solution.py:333
  27.3 1.5 %collective-permute-done.3 = f32[32,2048]{1,0:T(8,128)S(1)} collective-permute-done((f32[32,2048]{1,0:T(8,128)S(1)}, f32[32,2048]{1,0:T(8,128)S(1)}, u32[]{:S(2)}, u32[]{:S(2)}) %collective-permute-start.3) | collective-permute-done | bytes 262176 | tf_op jit(solution)/shard_map/ppermute | solution.py:348
  28.8 1.3 %collective-permute-start.6 = (f32[32,2048]{1,0:T(8,128)S(1)}, f32[32,2048]{1,0:T(8,128)S(1)}, u32[]{:S(2)}, u32[]{:S(2)}) collective-permute-start(f32[32,2048]{1,0:T(8,128)S(1)} %get-tuple-element.113.refs_2_.refs_0_), channel_id=1, source_target_pairs={{2,0},{4,2},{6,4},{8,6},{10,8},{12,10},{14,12},{16,14},{18,16},{20... | collective-permute-start | bytes 786440 | tf_op jit(solution)/shard_map/ppermute | solution.py:354
  30.1 1.1 %collective-permute-start.4 = (f32[32,2048]{1,0:T(8,128)S(1)}, f32[32,2048]{1,0:T(8,128)S(1)}, u32[]{:S(2)}, u32[]{:S(2)}) collective-permute-start(f32[32,2048]{1,0:T(8,128)S(1)} %get-tuple-element.113.refs_2_.refs_0_), channel_id=1, source_target_pairs={{0,1},{1,0},{2,3},{3,2},{4,5},{5,4},{6,7},{7,6},{8,9},{9,8},{10,11... | collective-permute-start | bytes 786440 | tf_op jit(solution)/shard_map/ppermute | solution.py:348
  31.3 2.7 %collective-permute-done.7.refs_1_ = f32[32,2048]{1,0:T(8,128)S(1)} collective-permute-done((f32[32,2048]{1,0:T(8,128)S(1)}, f32[32,2048]{1,0:T(8,128)S(1)}, u32[]{:S(2)}, u32[]{:S(2)}) %collective-permute-start.7) | collective-permute-done | bytes 262176 | tf_op jit(solution)/shard_map/ppermute | solution.py:348
  34.0 1.3 %collective-permute-start.9 = (f32[32,2048]{1,0:T(8,128)S(1)}, f32[32,2048]{1,0:T(8,128)S(1)}, u32[]{:S(2)}, u32[]{:S(2)}) collective-permute-start(f32[32,2048]{1,0:T(8,128)S(1)} %collective-permute-done.7.refs_1_), channel_id=1, source_target_pairs={{2,0},{4,2},{6,4},{8,6},{10,8},{12,10},{14,12},{16,14},{18,16},{20... | collective-permute-start | bytes 786440 | tf_op jit(solution)/shard_map/ppermute | solution.py:354
  35.3 1.4 %filter.2.refs_12_ = f32[192,256]{1,0:T(8,128)S(1)} custom-call(f32[32,2048]{1,0:T(8,128)S(1)} %get-tuple-element.102.refs_0_, f32[32,2048]{1,0:T(8,128)S(1)} %collective-permute-done.7.refs_1_, bf16[128,2048]{1,0:T(8,128)(2,1)S(1)} %get-tuple-element.76.refs_2_.refs_4_, bf16[128,2048]{1,0:T(8,128)(2,1)S(1)} %get-tuple-element.77.refs_3_.refs_5_, ...), custom_call_target="tpu_custom_call" | custom-call | bytes 576 | tf_op jit(solution)/shard_map/filter/pallas_call | solution.py:333
  36.7 1.6 %activation.3 = f32[2048,64]{1,0:T(8,128)} custom-call(f32[32,2048]{1,0:T(8,128)S(1)} %get-tuple-element.82.chunk, f32[2048,64]{1,0:T(8,128)} %activation.2.refs_0_), custom_call_target="tpu_custom_call", output_to_operand_aliasing={{}: (1, {})} | custom-call | bytes 360 | tf_op jit(solution)/shard_map/activation/pallas_call | solution.py:333
  38.3 1.3 %collective-permute-done.4.refs_3_.refs_1_ = f32[32,2048]{1,0:T(8,128)S(1)} collective-permute-done((f32[32,2048]{1,0:T(8,128)S(1)}, f32[32,2048]{1,0:T(8,128)S(1)}, u32[]{:S(2)}, u32[]{:S(2)}) %collective-permute-start.4) | collective-permute-done | bytes 262176 | tf_op jit(solution)/shard_map/ppermute | solution.py:348
  39.6 1.5 %collective-permute-start.8 = (f32[32,2048]{1,0:T(8,128)S(1)}, f32[32,2048]{1,0:T(8,128)S(1)}, u32[]{:S(2)}, u32[]{:S(2)}) collective-permute-start(f32[32,2048]{1,0:T(8,128)S(1)} %collective-permute-done.4.refs_3_.refs_1_), channel_id=1, source_target_pairs={{2,0},{4,2},{6,4},{8,6},{10,8},{12,10},{14,12},{16,14},{18,16},{20... | collective-permute-start | bytes 786440 | tf_op jit(solution)/shard_map/ppermute | solution.py:354
  41.1 1.6 %filter.3 = (f32[112,128]{1,0:T(8,128)S(1)}, f32[112,128]{1,0:T(8,128)S(1)}) custom-call(f32[32,2048]{1,0:T(8,128)S(1)} %get-tuple-element.102.refs_0_, f32[32,2048]{1,0:T(8,128)S(1)} %collective-permute-done.7.refs_1_, f32[32,2048]{1,0:T(8,128)S(1)} %get-tuple-element.113.refs_2_.refs_0_, f32[32,2048]{1,0:T(8,128)S(1)} %collective-permute-done.4.refs_3_.refs_1_, ...), custom_call_target="tpu_custom_call" | custom-call | bytes 576 | tf_op jit(solution)/shard_map/filter/pallas_call | solution.py:333
  42.7 1.2 %collective-permute-start.10 = (f32[112,128]{1,0:T(8,128)S(1)}, f32[112,128]{1,0:T(8,128)S(1)}, u32[]{:S(2)}, u32[]{:S(2)}) collective-permute-start(f32[112,128]{1,0:T(8,128)S(1)} %get-tuple-element.94), channel_id=1, source_target_pairs={{0,2},{2,0},{4,6},{6,4},{8,10},{10,8},{12,14},{14,12},{16,18},{18,... | collective-permute-start | bytes 172040 | tf_op jit(solution)/shard_map/ppermute | solution.py:362
  44.8 1.7 %collective-permute-start.11 = (f32[112,128]{1,0:T(8,128)S(1)}, f32[112,128]{1,0:T(8,128)S(1)}, u32[]{:S(2)}, u32[]{:S(2)}) collective-permute-start(f32[112,128]{1,0:T(8,128)S(1)} %add.28), channel_id=1, source_target_pairs={{0,4},{2,6},{4,0},{6,2},{8,12},{10,14},{12,8},{14,10},{16,20},{18,... | collective-permute-start | bytes 172040 | tf_op jit(solution)/shard_map/ppermute | solution.py:362
  46.4 2.6 %back.3.refs_9_ = f32[32,128,128]{2,1,0:T(8,128)} custom-call(f32[32,2048]{1,0:T(8,128)S(1)} %get-tuple-element.102.refs_0_, f32[32,2048]{1,0:T(8,128)S(1)} %collective-permute-done.7.refs_1_, f32[32,2048]{1,0:T(8,128)S(1)} %collective-permute-done.5.refs_2_.refs_4_, f32[32,2048]{1,0:T(8,128)S(1)} %collective-permute-done.9.refs_3_.refs_5_, ...), custom_call_target="tpu_custom_call" | custom-call | bytes 900 | tf_op jit(solution)/shard_map/back/pallas_call | solution.py:333
  49.0 2.3 %collective-permute-start.12 = (f32[112,128]{1,0:T(8,128)S(1)}, f32[112,128]{1,0:T(8,128)S(1)}, u32[]{:S(2)}, u32[]{:S(2)}) collective-permute-start(f32[112,128]{1,0:T(8,128)S(1)} %add.29), channel_id=1, source_target_pairs={{0,8},{2,10},{4,12},{6,14},{8,0},{10,2},{12,4},{14,6},{16,24},{18,... | collective-permute-start | bytes 172040 | tf_op jit(solution)/shard_map/ppermute | solution.py:362
  51.3 2.8 %back.4.refs_5_ = f32[32,128,128]{2,1,0:T(8,128)} custom-call(f32[32,2048]{1,0:T(8,128)S(1)} %get-tuple-element.102.refs_0_, f32[32,2048]{1,0:T(8,128)S(1)} %collective-permute-done.7.refs_1_, f32[32,2048]{1,0:T(8,128)S(1)} %get-tuple-element.113.refs_2_.refs_0_, ...), custom_call_target="tpu_custom_call", output_to_operand_aliasing={{}: (9, {})} | custom-call | bytes 900 | tf_op jit(solution)/shard_map/back/pallas_call | solution.py:333
  54.2 3.2 %collective-permute-start.13 = (f32[112,128]{1,0:T(8,128)S(1)}, f32[112,128]{1,0:T(8,128)S(1)}, u32[]{:S(2)}, u32[]{:S(2)}) collective-permute-start(f32[112,128]{1,0:T(8,128)S(1)} %add.30), channel_id=1, source_target_pairs={{0,16},{2,18},{4,20},{6,22},{8,24},{10,26},{12,28},{14,30},{16,0},... | collective-permute-start | bytes 172040 | tf_op jit(solution)/shard_map/ppermute | solution.py:362
  57.4 2.6 %back.5 = f32[32,128,128]{2,1,0:T(8,128)} custom-call(f32[32,2048]{1,0:T(8,128)S(1)} %get-tuple-element.113.refs_2_.refs_0_, f32[32,2048]{1,0:T(8,128)S(1)} %collective-permute-done.4.refs_3_.refs_1_, f32[32,2048]{1,0:T(8,128)S(1)} %collective-permute-done.6.refs_6_.refs_2_, ...), custom_call_target="tpu_custom_call", output_to_operand_aliasing={{}: (5, {})} | custom-call | bytes 900 | tf_op jit(solution)/shard_map/back/pallas_call | solution.py:333
  60.1 1.2 %collective-permute-done.14 = f32[112,128]{1,0:T(8,128)S(1)} collective-permute-done((f32[112,128]{1,0:T(8,128)S(1)}, f32[112,128]{1,0:T(8,128)S(1)}, u32[]{:S(2)}, u32[]{:S(2)}) %collective-permute-start.14) | collective-permute-done | bytes 57376 | tf_op jit(solution)/shard_map/ppermute | solution.py:362
  (28 shorter events, 3.3 us)
Async XLA Ops:
  0.6 9.4 %copy-start = (f32[16,2,128,128]{3,2,1,0:T(8,128)S(1)}, f32[16,2,128,128]{3,2,1,0:T(8,128)}, u32[]{:S(2)}) copy-start(f32[16,2,128,128]{3,2,1,0:T(8,128)} %param.3) | copy-start | bytes 6291460
  1.9 14.0 %copy-start.1 = (f32[32,1,64,64]{3,2,1,0:T(8,128)S(1)}, f32[32,1,64,64]{3,2,1,0:T(8,128)}, u32[]{:S(2)}) copy-start(f32[32,1,64,64]{3,2,1,0:T(8,128)} %param.5) | copy-start | bytes 1572868
  1.9 11.1 %collective-permute-start.1 = (f32[16,64,128]{2,1,0:T(8,128)S(1)}, f32[16,64,128]{2,1,0:T(8,128)S(1)}, u32[]{:S(2)}, u32[]{:S(2)}) collective-permute-start(f32[16,64,128]{2,1,0:T(8,128)S(1)} %slice_bitcast_fusion.1), channel_id=1, source_target_pairs={{0,2},{2,4},{4,6},{6,8},{8,10},{10,12},{12,14},{14,16},{16,18},{18... | collective-permute-start | bytes 1572872 | tf_op jit(solution)/shard_map/ppermute | solution.py:354
  5.5 13.0 %collective-permute-start = (f32[16,64,128]{2,1,0:T(8,128)S(1)}, f32[16,64,128]{2,1,0:T(8,128)S(1)}, u32[]{:S(2)}, u32[]{:S(2)}) collective-permute-start(f32[16,64,128]{2,1,0:T(8,128)S(1)} %slice_bitcast_fusion), channel_id=1, source_target_pairs={{0,2},{2,4},{4,6},{6,8},{8,10},{10,12},{12,14},{14,16},{16,18},{18... | collective-permute-start | bytes 1572872 | tf_op jit(solution)/shard_map/ppermute | solution.py:354
  10.1 0.9 %copy-start.2 = (f32[64,16,3,3,3]{0,1,4,3,2:T(8,128)S(1)}, f32[64,16,3,3,3]{0,1,4,3,2:T(8,128)}, u32[]{:S(2)}) copy-start(f32[64,16,3,3,3]{0,1,4,3,2:T(8,128)} %param.4) | copy-start | bytes 331780
  14.4 8.4 %collective-permute-start.2 = (f32[32,2048]{1,0:T(8,128)S(1)}, f32[32,2048]{1,0:T(8,128)S(1)}, u32[]{:S(2)}, u32[]{:S(2)}) collective-permute-start(f32[32,2048]{1,0:T(8,128)S(1)} %get-tuple-element.71), channel_id=1, source_target_pairs={{0,1},{1,0},{2,3},{3,2},{4,5},{5,4},{6,7},{7,6},{8,9},{9,8},{10,11... | collective-permute-start | bytes 786440 | tf_op jit(solution)/shard_map/ppermute | solution.py:348
  19.8 8.9 %collective-permute-start.3 = (f32[32,2048]{1,0:T(8,128)S(1)}, f32[32,2048]{1,0:T(8,128)S(1)}, u32[]{:S(2)}, u32[]{:S(2)}) collective-permute-start(f32[32,2048]{1,0:T(8,128)S(1)} %get-tuple-element.73), channel_id=1, source_target_pairs={{0,1},{1,0},{2,3},{3,2},{4,5},{5,4},{6,7},{7,6},{8,9},{9,8},{10,11... | collective-permute-start | bytes 786440 | tf_op jit(solution)/shard_map/ppermute | solution.py:348
  22.8 12.4 %collective-permute-start.5 = (f32[32,2048]{1,0:T(8,128)S(1)}, f32[32,2048]{1,0:T(8,128)S(1)}, u32[]{:S(2)}, u32[]{:S(2)}) collective-permute-start(f32[32,2048]{1,0:T(8,128)S(1)} %get-tuple-element.102.refs_0_), channel_id=1, source_target_pairs={{2,0},{4,2},{6,4},{8,6},{10,8},{12,10},{14,12},{16,14},{18,16},{20... | collective-permute-start | bytes 786440 | tf_op jit(solution)/shard_map/ppermute | solution.py:354
  24.1 9.8 %collective-permute-start.7 = (f32[32,2048]{1,0:T(8,128)S(1)}, f32[32,2048]{1,0:T(8,128)S(1)}, u32[]{:S(2)}, u32[]{:S(2)}) collective-permute-start(f32[32,2048]{1,0:T(8,128)S(1)} %get-tuple-element.102.refs_0_), channel_id=1, source_target_pairs={{0,1},{1,0},{2,3},{3,2},{4,5},{5,4},{6,7},{7,6},{8,9},{9,8},{10,11... | collective-permute-start | bytes 786440 | tf_op jit(solution)/shard_map/ppermute | solution.py:348
  28.8 7.8 %collective-permute-start.6 = (f32[32,2048]{1,0:T(8,128)S(1)}, f32[32,2048]{1,0:T(8,128)S(1)}, u32[]{:S(2)}, u32[]{:S(2)}) collective-permute-start(f32[32,2048]{1,0:T(8,128)S(1)} %get-tuple-element.113.refs_2_.refs_0_), channel_id=1, source_target_pairs={{2,0},{4,2},{6,4},{8,6},{10,8},{12,10},{14,12},{16,14},{18,16},{20... | collective-permute-start | bytes 786440 | tf_op jit(solution)/shard_map/ppermute | solution.py:354
  30.1 9.5 %collective-permute-start.4 = (f32[32,2048]{1,0:T(8,128)S(1)}, f32[32,2048]{1,0:T(8,128)S(1)}, u32[]{:S(2)}, u32[]{:S(2)}) collective-permute-start(f32[32,2048]{1,0:T(8,128)S(1)} %get-tuple-element.113.refs_2_.refs_0_), channel_id=1, source_target_pairs={{0,1},{1,0},{2,3},{3,2},{4,5},{5,4},{6,7},{7,6},{8,9},{9,8},{10,11... | collective-permute-start | bytes 786440 | tf_op jit(solution)/shard_map/ppermute | solution.py:348
  34.0 10.8 %collective-permute-start.9 = (f32[32,2048]{1,0:T(8,128)S(1)}, f32[32,2048]{1,0:T(8,128)S(1)}, u32[]{:S(2)}, u32[]{:S(2)}) collective-permute-start(f32[32,2048]{1,0:T(8,128)S(1)} %collective-permute-done.7.refs_1_), channel_id=1, source_target_pairs={{2,0},{4,2},{6,4},{8,6},{10,8},{12,10},{14,12},{16,14},{18,16},{20... | collective-permute-start | bytes 786440 | tf_op jit(solution)/shard_map/ppermute | solution.py:354
  39.6 9.4 %collective-permute-start.8 = (f32[32,2048]{1,0:T(8,128)S(1)}, f32[32,2048]{1,0:T(8,128)S(1)}, u32[]{:S(2)}, u32[]{:S(2)}) collective-permute-start(f32[32,2048]{1,0:T(8,128)S(1)} %collective-permute-done.4.refs_3_.refs_1_), channel_id=1, source_target_pairs={{2,0},{4,2},{6,4},{8,6},{10,8},{12,10},{14,12},{16,14},{18,16},{20... | collective-permute-start | bytes 786440 | tf_op jit(solution)/shard_map/ppermute | solution.py:354
  42.7 2.1 %collective-permute-start.10 = (f32[112,128]{1,0:T(8,128)S(1)}, f32[112,128]{1,0:T(8,128)S(1)}, u32[]{:S(2)}, u32[]{:S(2)}) collective-permute-start(f32[112,128]{1,0:T(8,128)S(1)} %get-tuple-element.94), channel_id=1, source_target_pairs={{0,2},{2,0},{4,6},{6,4},{8,10},{10,8},{12,14},{14,12},{16,18},{18,... | collective-permute-start | bytes 172040 | tf_op jit(solution)/shard_map/ppermute | solution.py:362
  44.8 4.3 %collective-permute-start.11 = (f32[112,128]{1,0:T(8,128)S(1)}, f32[112,128]{1,0:T(8,128)S(1)}, u32[]{:S(2)}, u32[]{:S(2)}) collective-permute-start(f32[112,128]{1,0:T(8,128)S(1)} %add.28), channel_id=1, source_target_pairs={{0,4},{2,6},{4,0},{6,2},{8,12},{10,14},{12,8},{14,10},{16,20},{18,... | collective-permute-start | bytes 172040 | tf_op jit(solution)/shard_map/ppermute | solution.py:362
  49.0 5.1 %collective-permute-start.12 = (f32[112,128]{1,0:T(8,128)S(1)}, f32[112,128]{1,0:T(8,128)S(1)}, u32[]{:S(2)}, u32[]{:S(2)}) collective-permute-start(f32[112,128]{1,0:T(8,128)S(1)} %add.29), channel_id=1, source_target_pairs={{0,8},{2,10},{4,12},{6,14},{8,0},{10,2},{12,4},{14,6},{16,24},{18,... | collective-permute-start | bytes 172040 | tf_op jit(solution)/shard_map/ppermute | solution.py:362
  54.2 5.8 %collective-permute-start.13 = (f32[112,128]{1,0:T(8,128)S(1)}, f32[112,128]{1,0:T(8,128)S(1)}, u32[]{:S(2)}, u32[]{:S(2)}) collective-permute-start(f32[112,128]{1,0:T(8,128)S(1)} %add.30), channel_id=1, source_target_pairs={{0,16},{2,18},{4,20},{6,22},{8,24},{10,26},{12,28},{14,30},{16,0},... | collective-permute-start | bytes 172040 | tf_op jit(solution)/shard_map/ppermute | solution.py:362
  60.0 1.3 %collective-permute-start.14 = (f32[112,128]{1,0:T(8,128)S(1)}, f32[112,128]{1,0:T(8,128)S(1)}, u32[]{:S(2)}, u32[]{:S(2)}) collective-permute-start(f32[112,128]{1,0:T(8,128)S(1)} %add.31), channel_id=1, source_target_pairs={{0,2},{2,0},{4,6},{6,4},{8,10},{10,8},{12,14},{14,12},{16,18},{18,... | collective-permute-start | bytes 172040 | tf_op jit(solution)/shard_map/ppermute | solution.py:362
